TPU v7x, 32 devices: a whole 2x2x4 slice. The times are simulated.
32 devices in a mesh: rep: 8 (over z, core), shard: 4 (over y, x).
Axes of the slice: x: 2, y: 2, z: 4, core: 2. Of those that a mesh axis runs over, the one named last changes fastest.
Arguments:
- tokens: float32 [64, 1024, 768], P(('rep', 'shard')), may hold values from -6 to 6
- segments: int32 [64, 1024], P(('rep', 'shard')), may hold values from 0 to 3, never falling along the last dimension, each value on 1 to 800 neighbouring positions
- time_steps: int32 [64], P(('rep', 'shard')), may hold values from 0 to 1999
- time_table: bfloat16 [2000, 768], P('shard'), may hold values from -4 to 4
- ln1_gain: bfloat16 [768], P('shard'), may hold values from 0.5 to 1.5
- ln1_bias: bfloat16 [768], P('shard'), may hold values from -1 to 1
- q_weight: bfloat16 [768, 768], P('shard'), may hold values from -0.21875 to 0.21875
- q_bias: bfloat16 [768], P('shard'), may hold values from -1 to 1
- k_weight: bfloat16 [768, 768], P('shard'), may hold values from -0.21875 to 0.21875
- v_weight: bfloat16 [768, 768], P('shard'), may hold values from -0.21875 to 0.21875
- v_bias: bfloat16 [768], P('shard'), may hold values from -1 to 1
- o_weight: bfloat16 [768, 768], P('shard'), may hold values from -0.875 to 0.875
- o_bias: bfloat16 [768], P('shard'), may hold values from -1 to 1
- ln2_gain: bfloat16 [768], P('shard'), may hold values from 0.5 to 1.5
- ln2_bias: bfloat16 [768], P('shard'), may hold values from -1 to 1
- up_weight: bfloat16 [768, 3072], P('shard'), may hold values from -0.21875 to 0.21875
- up_bias: bfloat16 [3072], P('shard'), may hold values from -1 to 1
- down_weight: bfloat16 [3072, 768], P('shard'), may hold values from -0.109375 to 0.109375
- down_bias: bfloat16 [768], P('shard'), may hold values from -1 to 1
- cotangent: float32 [64, 1024, 768], P(('rep', 'shard')), may hold values from -6 to 6
Outputs:
- result: float32 [64, 1024, 768], P(('rep', 'shard'))
- grad_tokens: float32 [64, 1024, 768], P(('rep', 'shard'))
- grad_time_table: float32 [2000, 768], P('shard')
- grad_ln1_gain: float32 [768], P('shard')
- grad_ln1_bias: float32 [768], P('shard')
- grad_q_weight: float32 [768, 768], P('shard')
- grad_q_bias: float32 [768], P('shard')
- grad_k_weight: float32 [768, 768], P('shard')
- grad_v_weight: float32 [768, 768], P('shard')
- grad_v_bias: float32 [768], P('shard')
- grad_o_weight: float32 [768, 768], P('shard')
- grad_o_bias: float32 [768], P('shard')
- grad_ln2_gain: float32 [768], P('shard')
- grad_ln2_bias: float32 [768], P('shard')
- grad_up_weight: float32 [768, 3072], P('shard')
- grad_up_bias: float32 [3072], P('shard')
- grad_down_weight: float32 [3072, 768], P('shard')
- grad_down_bias: float32 [768], P('shard')
Inputs may be any that keep to these rules, and one draw needn't show every extreme that they name: `segments`: within a sequence segment numbers never fall; each document holds 1 to 800 tokens and one holds exactly 800.
All inputs are finite; a program needn't handle non-finite values.
Results may differ from a plain program's by a relative error of at most 0.022.
Values may be sent and summed in bfloat16 or wider, within the bound.
No kernel may reach another device: no remote copies, remote signals or barrier semaphores. Data moves between devices by JAX's collectives and lax.ppermute only.
A program may use at most 320 MiB of HBM per device.

v0:
```python
import functools
import math

import jax
import jax.numpy as jnp
from jax import lax
from jax.experimental import pallas as pl
from jax.experimental.pallas import tpu as pltpu
from jax.sharding import PartitionSpec as P

NEG=-1e30
EPS=1e-5
L=1024
D=768
FF=3072
HC=D//2
BF=jnp.bfloat16
F32=jnp.float32
LOG2E=math.log2(math.e)
LN2=math.log(2.0)
QS=0.125*LOG2E
VR=14
VP=16
NV=12
ANY=pl.BlockSpec(memory_space=pl.ANY)
S_=jax.ShapeDtypeStruct


def nt(a,b):
    return lax.dot_general(a,b,(((1,),(1,)),((),())),preferred_element_type=F32)


def nn(a,b):
    return lax.dot_general(a,b,(((1,),(0,)),((),())),preferred_element_type=F32)


def tn(a,b):
    return lax.dot_general(a,b,(((0,),(0,)),((),())),preferred_element_type=F32)


def full(*s):
    return pl.BlockSpec(s,lambda i,*_:(0,)*len(s),pipeline_mode=pl.Buffered(1))


def norm(x):
    mean=jnp.mean(x,axis=1,keepdims=True)
    off=x-mean
    var=jnp.mean(off*off,axis=1,keepdims=True)
    r=lax.rsqrt(var+EPS)
    return off*r,r


def sum8(x):
    return jnp.sum(x.reshape(x.shape[0]//8,8,x.shape[1]),axis=0)


def cost(flops,nbytes,trans=0):
    return pl.CostEstimate(flops=int(flops)//10,bytes_accessed=int(nbytes)//10,transcendentals=int(trans)//10)


def seg_features(seg):
    lane=jnp.arange(128)%64
    hit=seg[:,None]==lane[None,:]
    first=(lane<4)[None]
    fq=jnp.where(first&hit,1.0,0.0).astype(BF)
    fk=jnp.where(first,jnp.where(hit,0.0,NEG),jnp.where((lane<7)[None],1.0,0.0)).astype(BF)
    return fq,fk


def qkv_kernel(idx_ref,*refs,ns,wr):
    tok_ref,row_ref,vec_ref=refs[:3]
    own=refs[3:6]
    mine=refs[6:6+ns-1]
    other=refs[6+ns-1:6+2*(ns-1)]
    hi=6+2*(ns-1)
    q_ref,k_ref,v_ref,nt_ref,w_ref,sem=refs[hi:hi+6]
    def copies(w):
        c=idx_ref[0]
        cps=[]
        def put(src,sh,cols):
            rows=pl.ds(pl.multiple_of(sh*wr,16),wr)
            dst=w_ref.at[w,rows] if cols is None else w_ref.at[w,rows,pl.ds(pl.multiple_of(cols*HC,128),HC)]
            cps.append(pltpu.make_async_copy(src,dst,sem.at[w,len(cps)]))
        put(own[w],idx_ref[1],None)
        for j in range(1,ns):
            put(mine[j-1].at[pl.ds(w*wr,wr)],idx_ref[1+j],c)
            put(other[j-1].at[pl.ds(w*wr,wr)],idx_ref[1+j],1-c)
        return cps
    first=pl.program_id(0)==0
    @pl.when(first)
    def _():
        for w in range(3):
            for cp in copies(w):
                cp.start()
    def arrived(w):
        @pl.when(first)
        def _():
            for cp in copies(w):
                cp.wait()
    xhat,_=norm(tok_ref[...]+row_ref[0])
    n1=(xhat*vec_ref[0:1,:]+vec_ref[1:2,:]).astype(BF)
    arrived(0)
    q_ref[...]=((nn(n1,w_ref[0])+vec_ref[2:3,:])*QS).astype(BF)
    arrived(1)
    k_ref[...]=nn(n1,w_ref[1]).astype(BF)
    arrived(2)
    v_ref[...]=(nn(n1,w_ref[2])+vec_ref[3:4,:]).astype(BF)
    nt_ref[...]=n1.T


def qkv(idx,tok,row,vec,own,mine,other,tb=512):
    T=tok.shape[0]
    per=L//tb
    ns=len(mine)+1
    wr=own[0].shape[0]
    blk=pl.BlockSpec((tb,D),lambda i,*_:(i,0))
    return pl.pallas_call(
        functools.partial(qkv_kernel,ns=ns,wr=wr),
        grid_spec=pltpu.PrefetchScalarGridSpec(
            num_scalar_prefetch=1,grid=(T//tb,),
            in_specs=[blk,pl.BlockSpec((1,1,D),lambda i,*_:(i//per,0,0)),full(VR,D)]+[ANY]*(3+2*(ns-1)),
            out_specs=[blk]*3+[pl.BlockSpec((D,tb),lambda i,*_:(0,i)),full(3,D,D)],
            scratch_shapes=[pltpu.SemaphoreType.DMA((3,1+2*(ns-1)))]),
        out_shape=[S_((T,D),BF)]*3+[S_((D,T),BF),S_((3,D,D),BF)],
        compiler_params=pltpu.CompilerParams(dimension_semantics=("arbitrary",)),
        cost_estimate=cost(6*T*D*D,T*D*10+9*D*D),
        name="qkv")(idx,tok,row,vec,*own,*mine,*other)


def pack_a_kernel(idx_ref,q_ref,k_ref,v_ref,out_ref):
    wr=q_ref.shape[0]
    for ch in (0,1):
        @pl.when(idx_ref[0]==ch)
        def _():
            for w,ref in enumerate((q_ref,k_ref,v_ref)):
                out_ref[w*wr:(w+1)*wr,:]=ref[:,ch*HC:(ch+1)*HC]


def pack_b_kernel(idx_ref,o_ref,u_ref,d_ref,out_ref):
    wr=o_ref.shape[0]
    for ch in (0,1):
        @pl.when(idx_ref[0]==ch)
        def _():
            out_ref[0:wr,:]=o_ref[:,ch*HC:(ch+1)*HC]
            for b in range(4):
                out_ref[wr+b*wr:2*wr+b*wr,:]=u_ref[:,(ch*4+b)*HC:(ch*4+b+1)*HC]
            out_ref[5*wr:,:]=d_ref[:,ch*HC:(ch+1)*HC]


def pack(kernel,idx,ws,name):
    rows=sum(x.shape[0]*x.shape[1]//D for x in ws)
    vm=pl.BlockSpec(memory_space=pltpu.VMEM)
    return pl.pallas_call(kernel,in_specs=[pl.BlockSpec(memory_space=pltpu.SMEM)]+[vm]*3,out_specs=vm,
        out_shape=S_((rows,HC),BF),cost_estimate=cost(0,4*rows*D),name=name)(idx,*ws)


MAIN=800
ROWS=816
LANES=896
REST=768


def windows(s):
    s16=(s//16)*16
    return pl.multiple_of(jnp.minimum(s16,L-ROWS),16),pl.multiple_of(jnp.minimum(s16,L-LANES),16)


def fwd_kernel(s_ref,q_ref,k_ref,v_ref,fq_ref,fk_ref,*refs,f0,ns):
    o_ref,fx_ref=refs[-2:]
    s0=s_ref[s_ref[ns+f0+pl.program_id(0)]]
    wr,wl=windows(s0)
    lane=lax.broadcasted_iota(jnp.int32,(1,128),1)
    lo=lane<64
    l6=lane&63
    rest_row=lax.broadcasted_iota(jnp.int32,(256,1),0)
    ahead=rest_row<s0
    qb=ROWS//3
    rest=lambda ref: jnp.where(ahead,ref[0:256,:],ref[REST:L,:])
    main=lambda ref: ref[pl.ds(wl,LANES),:]
    one=jnp.where(l6==0,1.0,0.0).astype(BF)
    kv=[]
    for take in (rest,main):
        k=take(k_ref)
        v=take(v_ref)
        fk=take(fk_ref)
        kv.append([(jnp.where(own,k,fk),jnp.where(own,v,one)) for own in (lo,~lo)])
    qf=[(rest(q_ref),rest(fq_ref))]
    for b in range(3):
        rows=pl.ds(pl.multiple_of(wr+b*qb,16),qb)
        qf.append((q_ref[rows,:],fq_ref[rows,:]))
    units=[(b,h) for b in range(4) for h in (0,1)]
    def score(b,h):
        return nt(jnp.where(lo if h==0 else ~lo,*qf[b]),kv[min(b,1)][h][0])
    pend=[score(*u) for u in units[:3]]
    accs=[]
    ls=[]
    for i,(b,h) in enumerate(units):
        s=pend.pop(0)
        if i+3<len(units):
            pend.append(score(*units[i+3]))
        m=jnp.max(s,axis=1,keepdims=True)
        p=jnp.exp2(s-m).astype(BF)
        acc=nn(p,kv[min(b,1)][h][1])
        l=acc[:,64:65] if h==0 else acc[:,0:1]
        accs.append(acc*(1.0/l))
        ls.append(-(m+jnp.log2(l)))
        if h==1:
            o=jnp.where(lo,accs[0],accs[1]).astype(BF)
            nl=jnp.where(lo,ls[1],ls[0])
            hi=nl.astype(BF).astype(F32)
            r1=nl-hi
            mid=r1.astype(BF).astype(F32)
            r2=r1-mid
            fx=jnp.where(l6==4,hi,jnp.where(l6==5,mid,jnp.where(l6==6,r2,qf[b][1].astype(F32)))).astype(BF)
            if b==0:
                o_ref[0:256,:]=o
                fx_ref[0:256,:]=fx
                o_ref[REST:L,:]=o
                fx_ref[REST:L,:]=fx
            else:
                at=wr+(b-1)*qb
                rows=pl.ds(pl.multiple_of(at,16),qb)
                pos=lax.broadcasted_iota(jnp.int32,(qb,1),0)+(at-s0)
                inside=(pos>=0)&(pos<MAIN)
                o_ref[rows,:]=jnp.where(inside,o,o_ref[rows,:])
                fx_ref[rows,:]=jnp.where(inside,fx,fx_ref[rows,:])
            accs=[]
            ls=[]


def attn_fwd(starts,q,k,v,fq,fk,prev,f0,n):
    T=q.shape[0]
    ns=T//L
    nu=ns*(D//128)
    blk=pl.BlockSpec((L,128),lambda i,s:(s[ns+f0+i],s[ns+nu+f0+i]))
    fb=pl.BlockSpec((L,128),lambda i,s:(s[ns+f0+i],0))
    prev=list(prev)
    return pl.pallas_call(
        functools.partial(fwd_kernel,f0=f0,ns=ns),
        grid_spec=pltpu.PrefetchScalarGridSpec(
            num_scalar_prefetch=1,grid=(n,),
            in_specs=[blk,blk,blk,fb,fb]+[ANY]*len(prev),out_specs=[blk,blk]),
        out_shape=[S_((T,D),BF)]*2,
        input_output_aliases={6+i:i for i in range(len(prev))},
        compiler_params=pltpu.CompilerParams(dimension_semantics=("arbitrary",)),
        cost_estimate=cost(n*2*4*L*L*256,n*L*128*14,n*2*L*L),
        name="attn_fwd")(starts,q,k,v,fq,fk,*prev)


def bwd_kernel(s_ref,q_ref,k_ref,v_ref,fx_ref,fk_ref,o_ref,do_ref,*refs,f0,ns):
    out_ref=refs[-1]
    s0=s_ref[s_ref[ns+f0+pl.program_id(0)]]
    wr,wl=windows(s0)
    lane=lax.broadcasted_iota(jnp.int32,(1,128),1)
    lo=lane<64
    l6=lane&63
    zero=jnp.zeros((),BF)
    ones2=jnp.where(l6<2,1.0,0.0).astype(BF)
    rest_row=lax.broadcasted_iota(jnp.int32,(256,1),0)
    ahead=rest_row<s0
    rest=lambda ref: jnp.where(ahead,ref[0:256,:],ref[REST:L,:])
    def block(take_k,nk,takes):
        k=take_k(k_ref)
        v=take_k(v_ref)
        fk=take_k(fk_ref)
        kx=[]
        vx=[]
        km=[]
        for own in (lo,~lo):
            kx.append(jnp.where(own,k,fk))
            vx.append(jnp.where(own,v,ones2))
            km.append(jnp.where(own,k,zero))
        dv=jnp.zeros((nk,128),F32)
        dk=jnp.zeros((nk,128),F32)
        dqs=[]
        for take in takes:
            q=take(q_ref)
            fx=take(fx_ref)
            do=take(do_ref)
            prod=do.astype(F32)*take(o_ref).astype(F32)
            d0=-jnp.sum(jnp.where(lo,prod,0.0),axis=1,keepdims=True)
            d1=-jnp.sum(jnp.where(lo,0.0,prod),axis=1,keepdims=True)
            nd=jnp.where(lo,d1,d0)
            hi=nd.astype(BF).astype(F32)
            fd=jnp.where(l6==0,hi,jnp.where(l6==1,nd-hi,0.0)).astype(BF)
            dq=jnp.zeros(q.shape,F32)
            for h,own in enumerate((lo,~lo)):
                p=jnp.exp2(nt(kx[h],jnp.where(own,q,fx)))
                dpt=nt(vx[h],jnp.where(own,do,fd))
                pb=p.astype(BF)
                ds=(p*dpt).astype(BF)
                dv=dv+nn(pb,jnp.where(own,do,zero))
                dk=dk+nn(ds,jnp.where(own,q,zero))
                dq=dq+tn(ds,km[h])
            dqs.append((dq*0.125).astype(BF))
        return dqs,(dk*LN2).astype(BF),dv.astype(BF)
    dqs,dk,dv=block(rest,256,[rest])
    for w,x in enumerate((dqs[0],dk,dv)):
        out_ref[w,0:256,:]=x
        out_ref[w,REST:L,:]=x
    at=lambda start,n: pl.ds(pl.multiple_of(start,16),n)
    cuts=[(0,256),(256,256),(512,256),(768,128)]
    dqs,dk,dv=block(lambda ref: ref[at(wr,ROWS),:],ROWS,[lambda ref,c=c: ref[at(wl+c[0],c[1]),:] for c in cuts])
    def put(w,start,x):
        n=x.shape[0]
        pos=lax.broadcasted_iota(jnp.int32,(n,1),0)+(start-s0)
        out_ref[w,at(start,n),:]=jnp.where((pos>=0)&(pos<MAIN),x,out_ref[w,at(start,n),:])
    for c,x in zip(cuts,dqs):
        put(0,wl+c[0],x)
    put(1,wr,dk)
    put(2,wr,dv)


def attn_bwd(starts,q,k,v,fx,fk,o,do,prev,f0,n):
    T=q.shape[0]
    ns=T//L
    nu=ns*(D//128)
    blk=pl.BlockSpec((L,128),lambda i,s:(s[ns+f0+i],s[ns+nu+f0+i]))
    fb=pl.BlockSpec((L,128),lambda i,s:(s[ns+f0+i],0))
    prev=list(prev)
    return pl.pallas_call(
        functools.partial(bwd_kernel,f0=f0,ns=ns),
        grid_spec=pltpu.PrefetchScalarGridSpec(
            num_scalar_prefetch=1,grid=(n,),
            in_specs=[blk,blk,blk,blk,fb,blk,blk]+[ANY]*len(prev),
            out_specs=pl.BlockSpec((3,L,128),lambda i,s:(0,s[ns+f0+i],s[ns+nu+f0+i]))),
        out_shape=S_((3,T,D),BF),
        input_output_aliases={8+i:i for i in range(len(prev))},
        compiler_params=pltpu.CompilerParams(dimension_semantics=("arbitrary",)),
        cost_estimate=cost(n*2*10*L*L*256,n*L*128*20,n*2*L*L),
        name="attn_bwd")(starts,q,k,v,fx,fk,o,do,*prev)


def mid_kernel(idx_ref,*refs,tb,fc,ns,wr,fr):
    tok_ref,row_ref,att_ref,cot_ref,vec_ref=refs[:5]
    own=refs[5:8]
    mine=refs[8:8+ns-1]
    other=refs[8+ns-1:8+2*(ns-1)]
    b0=8+2*(ns-1)
    res_ref,gm_ref,ga_ref,keep_ref,send_ref,sv_ref,sub_ref,ow,up,dn,aup,adn,aow,sem=refs[b0:]
    i=pl.program_id(0)
    n=pl.num_programs(0)
    c=idx_ref[0]
    def copies():
        cps=[]
        def put(src,dst):
            cps.append(pltpu.make_async_copy(src,dst,sem.at[len(cps)]))
        r16=lambda sh,m: pl.ds(pl.multiple_of(sh*m,16),m)
        sh=idx_ref[1+ns]
        put(own[0],ow.at[r16(sh,wr)])
        put(own[1],up.at[r16(sh,wr)])
        put(own[2],dn.at[r16(sh,fr)])
        for j in range(1,ns):
            for src,sh,cc in ((mine[j-1],idx_ref[1+ns+j],c),(other[j-1],idx_ref[1+2*ns+j],1-c)):
                cd=pl.ds(pl.multiple_of(cc*HC,128),HC)
                put(src.at[pl.ds(0,wr)],ow.at[r16(sh,wr),cd])
                for b in range(4):
                    put(src.at[pl.ds(wr+b*wr,wr)],up.at[r16(sh,wr),pl.ds(pl.multiple_of(cc*4*HC+b*HC,128),HC)])
                put(src.at[pl.ds(5*wr,fr)],dn.at[r16(sh,fr),cd])
        return cps
    @pl.when(i==0)
    def _():
        cps=copies()
        for cp in cps:
            cp.start()
        aup[...]=jnp.zeros_like(aup)
        adn[...]=jnp.zeros_like(adn)
        aow[...]=jnp.zeros_like(aow)
        sv_ref[...]=jnp.zeros_like(sv_ref)
        sub_ref[...]=jnp.zeros_like(sub_ref)
        for cp in cps:
            cp.wait()
    ob=vec_ref[4:5,:]
    g2=vec_ref[5:6,:]
    b2=vec_ref[6:7,:]
    db=vec_ref[7:8,:]
    att=att_ref[...]
    mixed=tok_ref[...]+row_ref[0]+nn(att,ow[...])+ob
    xhat,r=norm(mixed)
    n2=(xhat*g2+b2).astype(BF)
    n2t=n2.T
    cot=cot_ref[...]
    g=cot.astype(BF)
    res=mixed+db
    gn2=jnp.zeros((tb,D),F32)
    for j in range(FF//fc):
        cs=slice(j*fc,(j+1)*fc)
        pre=nn(n2,up[:,cs])+vec_ref[8+j:9+j,:]
        gact=nt(g,dn[cs,:])
        phi=0.5+0.5*lax.erf(pre*(2**-0.5))
        pdf=jnp.exp2(pre*pre*(-0.5*LOG2E))*(1.0/math.sqrt(2*math.pi))
        act=(pre*phi).astype(BF)
        gp=gact*(phi+pre*pdf)
        gpre=gp.astype(BF)
        sub_ref[:,cs]+=sum8(gp)
        res=res+nn(act,dn[cs,:])
        gn2=gn2+nt(gpre,up[:,cs])
        adn[cs,:]+=tn(act,g)
        aup[:,cs]+=nn(n2t,gpre)
    res_ref[...]=res
    e=gn2*g2
    c1=jnp.mean(e,axis=1,keepdims=True)
    c2=jnp.mean(e*xhat,axis=1,keepdims=True)
    gm=cot+r*(e-c1-xhat*c2)
    gml=gm.astype(BF)
    gm_ref[...]=gml
    ga_ref[...]=nt(gml,ow[...]).astype(BF)
    aow[...]+=tn(att,gml)
    sv_ref[0:8,:]+=sum8(gm)
    sv_ref[8:16,:]+=sum8(gn2*xhat)
    sv_ref[16:24,:]+=sum8(gn2)
    sv_ref[24:32,:]+=sum8(cot)
    @pl.when(i==n-1)
    def _():
        for ref,base,odd in ((keep_ref,1+ns,0),(send_ref,1+2*ns,1)):
            for ch in (0,1):
                @pl.when(c==(ch+odd)%2)
                def _():
                    def body(j,carry):
                        sh=idx_ref[base+j]
                        rw=pl.ds(pl.multiple_of(sh*wr,8),wr)
                        ref[j,0:wr,:]=aow[rw,ch*HC:(ch+1)*HC].astype(BF)
                        for b in range(4):
                            lo=(ch*4+b)*HC
                            ref[j,wr+b*wr:2*wr+b*wr,:]=aup[rw,lo:lo+HC].astype(BF)
                        ref[j,5*wr:5*wr+fr,:]=adn[pl.ds(pl.multiple_of(sh*fr,8),fr),ch*HC:(ch+1)*HC].astype(BF)
                        return carry
                    lax.fori_loop(0,ns,body,0)


def mid(idx,tok,row,att,cot,vec,own,mine,other,tb=256,fc=D):
    T=tok.shape[0]
    per=L//tb
    ns=len(mine)+1
    wr=own[0].shape[0]
    fr=own[2].shape[0]
    rb=5*wr+fr
    blk=pl.BlockSpec((tb,D),lambda i,*_:(i,0))
    return pl.pallas_call(
        functools.partial(mid_kernel,tb=tb,fc=fc,ns=ns,wr=wr,fr=fr),
        grid_spec=pltpu.PrefetchScalarGridSpec(
            num_scalar_prefetch=1,grid=(T//tb,),
            in_specs=[blk,pl.BlockSpec((1,1,D),lambda i,*_:(i//per,0,0)),blk,blk,full(VR,D)]+[ANY]*(3+2*(ns-1)),
            out_specs=[blk,blk,blk,full(ns,rb,HC),full(ns,rb,HC),full(32,D),full(8,FF)],
            scratch_shapes=[pltpu.VMEM((D,D),BF),pltpu.VMEM((D,FF),BF),pltpu.VMEM((FF,D),BF),
                pltpu.VMEM((D,FF),F32),pltpu.VMEM((FF,D),F32),pltpu.VMEM((D,D),F32),
                pltpu.SemaphoreType.DMA((3+12*(ns-1),))]),
        out_shape=[S_((T,D),F32),S_((T,D),BF),S_((T,D),BF),S_((ns,rb,HC),BF),S_((ns,rb,HC),BF),S_((32,D),F32),S_((8,FF),F32)],
        compiler_params=pltpu.CompilerParams(dimension_semantics=("arbitrary",),vmem_limit_bytes=67043328),
        cost_estimate=cost(6*T*D*(D+2*FF),T*D*20+30*D*FF,2*T*FF),
        name="mid")(idx,tok,row,att,cot,vec,*own,*mine,*other)


def dw_kernel(idx_ref,nt_ref,d_ref,keep_ref,send_ref,sv_ref,acc,*,ns,wr):
    i=pl.program_id(0)
    c=idx_ref[0]
    @pl.when(i==0)
    def _():
        acc[...]=jnp.zeros_like(acc)
        sv_ref[...]=jnp.zeros_like(sv_ref)
    for w in range(3):
        acc[w]+=nn(nt_ref[...],d_ref[w])
    sv_ref[0:8,:]+=sum8(d_ref[0].astype(F32))
    sv_ref[8:16,:]+=sum8(d_ref[2].astype(F32))
    @pl.when(i==pl.num_programs(0)-1)
    def _():
        for ref,base,odd in ((keep_ref,1+ns,0),(send_ref,1+2*ns,1)):
            for ch in (0,1):
                @pl.when(c==(ch+odd)%2)
                def _():
                    def body(j,carry):
                        rw=pl.ds(pl.multiple_of(idx_ref[base+j]*wr,8),wr)
                        for w in range(3):
                            ref[j,w*wr:(w+1)*wr,:]=acc[w,rw,ch*HC:(ch+1)*HC].astype(BF)
                        return carry
                    lax.fori_loop(0,ns,body,0)


def dw(idx,n1t,d,ns,tb=512):
    T=n1t.shape[1]
    wr=D//ns
    return pl.pallas_call(
        functools.partial(dw_kernel,ns=ns,wr=wr),
        grid_spec=pltpu.PrefetchScalarGridSpec(
            num_scalar_prefetch=1,grid=(T//tb,),
            in_specs=[pl.BlockSpec((D,tb),lambda i,*_:(0,i)),pl.BlockSpec((3,tb,D),lambda i,*_:(0,i,0))],
            out_specs=[full(ns,3*wr,HC),full(ns,3*wr,HC),full(16,D)],
            scratch_shapes=[pltpu.VMEM((3,D,D),F32)]),
        out_shape=[S_((ns,3*wr,HC),BF)]*2+[S_((16,D),F32)],
        compiler_params=pltpu.CompilerParams(dimension_semantics=("arbitrary",)),
        cost_estimate=cost(6*T*D*D,T*D*8+12*D*D),
        name="dw")(idx,n1t,d)


def dx_kernel(tok_ref,row_ref,d_ref,gm_ref,w_ref,vec_ref,gt_ref,sv_ref,ts_ref,*,per):
    i=pl.program_id(0)
    @pl.when(i==0)
    def _():
        sv_ref[...]=jnp.zeros_like(sv_ref)
    @pl.when(i%per==0)
    def _():
        ts_ref[...]=jnp.zeros_like(ts_ref)
    gn=nt(d_ref[0],w_ref[0])+nt(d_ref[1],w_ref[1])+nt(d_ref[2],w_ref[2])
    xhat,r=norm(tok_ref[...]+row_ref[0])
    e=gn*vec_ref[0:1,:]
    c1=jnp.mean(e,axis=1,keepdims=True)
    c2=jnp.mean(e*xhat,axis=1,keepdims=True)
    gt=gm_ref[...].astype(F32)+r*(e-c1-xhat*c2)
    gt_ref[...]=gt
    sv_ref[0:8,:]+=sum8(gn*xhat)
    sv_ref[8:16,:]+=sum8(gn)
    ts_ref[0]+=sum8(gt)


def dx(tok,row,d,gm,w,vec,tb=512):
    T=tok.shape[0]
    per=L//tb
    blk=pl.BlockSpec((tb,D),lambda i:(i,0))
    return pl.pallas_call(
        functools.partial(dx_kernel,per=per),grid=(T//tb,),
        in_specs=[blk,pl.BlockSpec((1,1,D),lambda i:(i//per,0,0)),pl.BlockSpec((3,tb,D),lambda i:(0,i,0)),blk,full(3,D,D),full(VR,D)],
        out_specs=[blk,full(16,D),pl.BlockSpec((1,8,D),lambda i:(i//per,0,0))],
        out_shape=[S_((T,D),F32),S_((16,D),F32),S_((T//L,8,D),F32)],
        compiler_params=pltpu.CompilerParams(dimension_semantics=("arbitrary",)),
        cost_estimate=cost(6*T*D*D,T*D*16+6*D*D),
        name="dx")(tok,row,d,gm,w,vec)


def rows8(x):
    return jnp.sum(x,axis=0,keepdims=True)


def sums_kernel(id_ref,sv1_ref,svq_ref,sv2_ref,sub_ref,ts_ref,out_ref):
    src=[sv1_ref[0:8],sv1_ref[8:16],svq_ref[0:8],svq_ref[8:16]]+[sv2_ref[8*i:8*i+8] for i in range(4)]
    src+=[sub_ref[:,i*D:(i+1)*D] for i in range(FF//D)]
    rows=[rows8(x) for x in src]+[id_ref[0:1],id_ref[1:2]]+[rows8(ts_ref[i]) for i in range(ts_ref.shape[0])]
    out_ref[...]=jnp.concatenate(rows,axis=0).astype(BF)


def sums(ids,sv1,svq,sv2,sub,ts):
    vm=pl.BlockSpec(memory_space=pltpu.VMEM)
    return pl.pallas_call(sums_kernel,in_specs=[vm]*6,out_specs=vm,
        out_shape=S_((VR+ts.shape[0],D),BF),cost_estimate=cost(0,10**6),name="sums")(ids,sv1,svq,sv2,sub,ts)


def group_kernel(idx_ref,*refs,ns,nseq):
    out_ref,acc=refs[ns:]
    tot=refs[0][0:VR].astype(F32)
    for j in range(1,ns):
        tot=tot+refs[j][0:VR].astype(F32)
    for j in range(ns):
        acc[idx_ref[1+j]]=refs[j][VR:VR+nseq].astype(F32)
    out_ref[...]=jnp.concatenate([tot]+[acc[j] for j in range(ns)],axis=0).astype(BF)


def group(idx,pays,nseq):
    ns=len(pays)
    vm=pl.BlockSpec(memory_space=pltpu.VMEM)
    return pl.pallas_call(functools.partial(group_kernel,ns=ns,nseq=nseq),
        in_specs=[pl.BlockSpec(memory_space=pltpu.SMEM)]+[vm]*ns,out_specs=vm,
        out_shape=S_((VR+ns*nseq,D),BF),scratch_shapes=[pltpu.VMEM((ns,nseq,D),F32)],
        cost_estimate=cost(0,10**6),name="group")(idx,*pays)


def table_kernel(me_ref,*refs,nr,rows,own):
    sum_ref,tab_ref,acc,allr=refs[nr:]
    r0=me_ref[0]
    for j in range(nr):
        acc[r0^j]=refs[j][...].astype(F32)
    tot=acc[0,0:VR]
    for r in range(1,nr):
        tot=tot+acc[r,0:VR]
    sum_ref[...]=tot
    for r in range(nr):
        allr[r*rows:(r+1)*rows,:]=acc[r,VR:VR+rows]
    n=nr*rows
    ids=tot[NV:NV+1,0:n]*32.0+tot[NV+1:NV+2,0:n]
    line=lax.broadcasted_iota(jnp.int32,(own,n),0)+me_ref[1]*own
    hit=jnp.where(line==ids.astype(jnp.int32),1.0,0.0).astype(BF)
    tab_ref[...]=nn(hit,allr[...].astype(BF))


def table(me,pays,own):
    nr=len(pays)
    rows=pays[0].shape[0]-VR
    vm=pl.BlockSpec(memory_space=pltpu.VMEM)
    return pl.pallas_call(functools.partial(table_kernel,nr=nr,rows=rows,own=own),
        in_specs=[pl.BlockSpec(memory_space=pltpu.SMEM)]+[vm]*nr,out_specs=[vm,vm],
        out_shape=[S_((VR,D),F32),S_((own,D),F32)],
        scratch_shapes=[pltpu.VMEM((nr,VR+rows,D),F32),pltpu.VMEM((nr*rows,D),F32)],
        cost_estimate=cost(0,4*10**6),name="table")(me,*pays)


def unpack_kernel(idx_ref,a_ref,b_ref,*outs,parts):
    for ch in (0,1):
        @pl.when(idx_ref[0]==ch)
        def _():
            for h,ref in enumerate((a_ref,b_ref) if ch==0 else (b_ref,a_ref)):
                r0=0
                for out,(nr,nb) in zip(outs,parts):
                    for b in range(nb):
                        out[:,(h*nb+b)*HC:(h*nb+b+1)*HC]=ref[r0:r0+nr,:].astype(F32)
                        r0+=nr


def unpack(idx,a,b,parts):
    vm=pl.BlockSpec(memory_space=pltpu.VMEM)
    return pl.pallas_call(functools.partial(unpack_kernel,parts=parts),
        in_specs=[pl.BlockSpec(memory_space=pltpu.SMEM),vm,vm],out_specs=[vm]*len(parts),
        out_shape=[S_((nr,2*nb*HC),F32) for nr,nb in parts],
        cost_estimate=cost(0,12*a.shape[0]*HC),name="unpack")(idx,a,b)


def small_kernel(me_ref,ts_ref,*refs,w,fr,nseq):
    vecs=refs[:9]
    out_ref,id_ref=refs[9:]
    def spread(rows,width,at):
        n=rows[0].shape[1]
        y=jnp.concatenate(rows+[jnp.zeros((8-len(rows),n),F32)]*(len(rows)<8),axis=0)
        y=jnp.concatenate([y,jnp.zeros((8,width-n),F32)],axis=1)
        return pltpu.roll(y,at,1)
    row=lambda ref: ref[...].astype(F32).reshape(1,ref.shape[0])
    v=spread([row(r) for r in vecs[:8]],D,me_ref[1]*w)
    u=spread([row(vecs[8])],FF,me_ref[1]*fr)
    lane=lax.broadcasted_iota(jnp.int32,(1,D),1)
    def steps(at,high):
        y=jnp.zeros((1,D),jnp.int32)
        for i in range(nseq):
            t=ts_ref[i]
            y=jnp.where(lane==at*nseq+i,t//32 if high else t%32,y)
        return y.astype(F32)
    id_ref[...]=jnp.concatenate([steps(me_ref[2],True),steps(me_ref[2],False)],axis=0)
    out_ref[...]=jnp.concatenate([v]+[u[0:1,i*D:(i+1)*D] for i in range(FF//D)]+[steps(me_ref[1],True),steps(me_ref[1],False)],axis=0).astype(BF)


def small_rows(me,time_steps,vecs):
    vm=pl.BlockSpec(memory_space=pltpu.VMEM)
    sm=pl.BlockSpec(memory_space=pltpu.SMEM)
    return pl.pallas_call(functools.partial(small_kernel,w=vecs[0].shape[0],fr=vecs[8].shape[0],nseq=time_steps.shape[0]),
        in_specs=[sm,sm]+[vm]*9,out_specs=[vm,vm],
        out_shape=[S_((VR,D),BF),S_((2,D),F32)],cost_estimate=cost(0,10**6),name="small")(me,time_steps,*vecs)


class Ring:
    def __init__(self,rep,shard):
        self.R,self.S=rep,shard
        self.nb=shard.bit_length()-1
        self.Z=rep//2
        r=lax.axis_index("rep")
        self.s=lax.axis_index("shard")
        self.c=r%2
        self.z=r//2

    def move(self,x,to):
        pairs=[]
        for r in range(self.R):
            for s in range(self.S):
                r2,s2=to(r,s)
                pairs.append((r*self.S+s,r2*self.S+s2))
        return lax.ppermute(x,("rep","shard"),pairs)

    def order(self,c,t):
        return (t+c*(self.nb//2))%self.nb

    def mask(self,c,j):
        m=0
        for t in range(self.nb):
            if j>>t&1:
                m|=1<<self.order(c,t)
        return m

    def step(self,x,t):
        return self.move(x,lambda r,s:(r,s^(1<<self.order(r%2,t))))

    def direct(self,x,j):
        return self.move(x,lambda r,s:(r,s^j))

    def core(self,x):
        return self.move(x,lambda r,s:(r^1,s))

    def plane(self,x,j):
        return self.move(x,lambda r,s:(r^(2*j),s))

    def index(self):
        m=[[self.mask(c,j) for j in range(self.S)] for c in (0,1)]
        base=list(range(self.S))
        t=jnp.where(self.c==0,jnp.array([0]+base+m[0]+m[1],jnp.int32),jnp.array([0]+base+m[1]+m[0],jnp.int32))
        head=jnp.arange(1+3*self.S)==0
        return jnp.where(head,self.c,t^self.s).astype(jnp.int32)


def tie(*xs):
    return lax.optimization_barrier(xs)


def add(*terms):
    y=terms[0].astype(F32)
    for x in terms[1:]:
        y=y+x.astype(F32)
    return y.astype(BF)


def upper(terms,n):
    return add(*[x[n:] for x in terms]),[x[:n] for x in terms]


def plane_rows(g,x):
    x=x.reshape(g.Z,-1,HC)
    return [lax.dynamic_index_in_dim(x,g.z^j,0,keepdims=False) for j in range(1,g.Z)]


def plane_send(g,rows):
    return [g.plane(x,j) for j,x in enumerate(rows,1)]


def plane_sum(g,x,parts):
    mine=lax.dynamic_index_in_dim(x.reshape(g.Z,-1,HC),g.z,0,keepdims=False).astype(F32)
    for p in parts:
        mine=mine+p.astype(F32)
    return mine.astype(BF)


def plane_join(g,mine,parts):
    out=jnp.zeros((g.Z,)+mine.shape,BF)
    for j,p in enumerate([mine]+parts):
        out=lax.dynamic_update_index_in_dim(out,p,g.z^j,0)
    return out.reshape(-1,HC)


def local(tokens,segments,time_steps,time_table,ln1_gain,ln1_bias,q_weight,q_bias,k_weight,v_weight,v_bias,o_weight,o_bias,ln2_gain,ln2_bias,up_weight,up_bias,down_weight,down_bias,cotangent):
    nseq=tokens.shape[0]
    T=nseq*L
    g=Ring(lax.axis_size("rep"),lax.axis_size("shard"))
    S=g.S
    w=ln1_gain.shape[0]
    fr=down_weight.shape[0]
    own=time_table.shape[0]
    idx=g.index()
    r=g.z*2+g.c
    me=jnp.stack([r,g.s,r*S+g.s]).astype(jnp.int32)
    small,ids=small_rows(me,time_steps,(ln1_gain,ln1_bias,q_bias,v_bias,o_bias,ln2_gain,ln2_bias,down_bias,up_bias))
    small,segments,o_weight_,q_weight_=tie(small,segments,o_weight,q_weight)
    pack_a=pack(pack_a_kernel,idx,(q_weight_,k_weight,v_weight),"pack_a")
    mine_a=[g.direct(pack_a,j) for j in range(1,S)]
    segments,pack_a=tie(segments,pack_a)
    vec=small.astype(F32)
    for j in reversed(range(1,S)):
        vec=vec+g.direct(small,j).astype(F32)
    steps=vec[NV,:S*nseq]*32.0+vec[NV+1,:S*nseq]
    hit=steps.astype(jnp.int32)[:,None]==jnp.arange(own)[None,:]+g.s*own
    rows=jnp.dot(hit.astype(BF),time_table,preferred_element_type=F32).astype(BF).reshape(S,nseq,D)
    pick=lambda j: lax.dynamic_index_in_dim(rows,g.s^j,0,keepdims=False)
    picks=[pick(j) for j in range(S)]
    picks[0],*mine_a=tie(picks[0],*mine_a)
    row=picks[0].astype(F32)
    for j in range(1,S):
        row=row+g.direct(picks[j],j).astype(F32)
    row=row.reshape(nseq,1,D)
    pack_b=pack(pack_b_kernel,idx,(o_weight_,up_weight,down_weight),"pack_b")
    tok=tokens.reshape(T,D)
    cot=cotangent.reshape(T,D)
    fq,fk=seg_features(segments.reshape(T))
    counts=jnp.sum(segments[:,:,None]==jnp.arange(4),axis=1)
    before=jnp.cumsum(counts==MAIN,axis=1)==0
    np_=D//128
    starts=jnp.concatenate([jnp.sum(jnp.where(before,counts,0),axis=1).astype(jnp.int32),
        jnp.array([i//np_ for i in range(nseq*np_)]+[i%np_ for i in range(nseq*np_)],jnp.int32)])
    fq,fk,pack_b,row,*mine_a=tie(fq,fk,pack_b,row,*mine_a)
    other_a=[g.core(x) for x in mine_a]
    mine_b=[pack_b]
    first=[g.step(pack_b,t) for t in range(g.nb)]
    q,k,v,n1t,wqkv=qkv(idx,tok,row,vec,(q_weight,k_weight,v_weight),mine_a,other_a)
    fwd=attn_fwd(starts,q,k,v,fq,fk,(),0,3*nseq//2)
    o1,fx1,*first=tie(*fwd,*first)
    for t in range(g.nb):
        mine_b=mine_b+[first[t]]+[g.step(x,t) for x in mine_b[1:]]
    direct=[1<<t for t in range(g.nb)]
    other_b=[None]+[g.core(x) if j in direct else None for j,x in enumerate(mine_b[1:],1)]
    fwd=attn_fwd(starts,q,k,v,fq,fk,(o1,fx1),3*nseq//2,3*nseq)
    late=[j for j in range(1,S) if j not in direct]
    o1,fx1,*got=tie(*fwd,*[mine_b[j] for j in late])
    for j,x in zip(late,got):
        mine_b[j]=x
        other_b[j]=g.core(x)
    att,fx=attn_fwd(starts,q,k,v,fq,fk,(o1,fx1),9*nseq//2,6*nseq-9*nseq//2)
    res,gm,ga,keep_b,send_b,sv2,sub=mid(idx,tok,row,att,cot,vec,(o_weight,up_weight,down_weight),mine_b[1:],other_b[1:])
    cuts=[0,nseq,nseq+5*nseq//2,5*nseq,6*nseq]
    call=lambda prev,i: attn_bwd(starts,q,k,v,fx,fk,att,ga,prev,cuts[i],cuts[i+1]-cuts[i])
    got=g.core(send_b)
    d=call((),0)
    d,got=tie(d,got)
    n=S
    x=[keep_b]
    for t in reversed(range(g.nb)):
        n//=2
        up,x=upper(x+[got],n)
        d,up=tie(d,up)
        got=g.step(up,t)
        i=g.nb-t
        if i<=2:
            d=call((d,),i)
            d,got=tie(d,got)
    xb=add(*[y[0] for y in x],got[0])
    d,xb,*rows_b=tie(d,xb,*plane_rows(g,xb))
    parts=plane_send(g,rows_b)
    d=call((d,),3)
    keep_a,send_a,svq=dw(idx,n1t,d,S)
    keep_a,send_a,*parts=tie(keep_a,send_a,*parts)
    got=g.core(send_a)
    mine=plane_sum(g,xb,parts)
    back=[g.plane(mine,j) for j in range(1,g.Z)]
    gm,mine_,got=tie(gm,mine,got)
    up,x=upper([keep_a,got],S//2)
    gm,up=tie(gm,up)
    got=g.step(up,g.nb-1)
    gt,sv1,ts=dx(tok,row,d,gm,wqkv,vec)
    ts,got=tie(ts,got)
    n=S//2
    for t in reversed(range(g.nb-1)):
        n//=2
        up,x=upper(x+[got],n)
        ts,up=tie(ts,up)
        got=g.step(up,t)
    pay=sums(ids,sv1,svq,sv2,sub,ts)
    pays=[pay]+[g.direct(pay,j) for j in range(1,S)]
    pays[-1],got=tie(pays[-1],got)
    xa=add(*[y[0] for y in x],got[0])
    rows_a=plane_rows(g,xa)
    *pays,rows_a[0]=tie(*pays,rows_a[0])
    parts_a=plane_send(g,rows_a)
    pay=group(idx,pays,nseq)
    out_b=plane_join(g,mine_,back)
    out_b,pay,*parts_a=tie(out_b,pay,*parts_a)
    other_b=g.core(out_b)
    mine=plane_sum(g,xa,parts_a)
    pay,mine=tie(pay,mine)
    back_a=[g.plane(mine,j) for j in range(1,g.Z)]
    pays=[pay]+[g.move(pay,lambda r,s,j=j:(r^j,s)) for j in range(1,g.R)]
    go,gup,gdn=unpack(idx,out_b,other_b,((w,1),(w,4),(fr,1)))
    gup,*both=tie(gup,*back_a,*pays)
    back_a,pays=both[:g.Z-1],both[g.Z-1:]
    out_a=plane_join(g,mine,back_a)
    other_a=g.core(out_a)
    vsum,gtab=table(me,pays,own)
    vsum,other_a=tie(vsum,other_a)
    gq,gk,gv=unpack(idx,out_a,other_a,((w,1),)*3)
    sums8=lax.dynamic_slice_in_dim(vsum[:8],g.s*w,w,1)
    subs=lax.dynamic_slice_in_dim(vsum[8:NV].reshape(FF),g.s*up_bias.shape[0],up_bias.shape[0],0)
    return (res.reshape(tokens.shape),gt.reshape(tokens.shape),gtab,sums8[0],sums8[1],gq,sums8[2],gk,gv,sums8[3],go,sums8[4],sums8[5],sums8[6],gup,subs,gdn,sums8[7])


def solution(mesh):
    b=("rep","shard")
    s=P("shard")
    m=P("shard",None)
    t=P(b,None,None)
    return jax.shard_map(local,mesh=mesh,
        in_specs=(t,P(b,None),P(b),m,s,s,m,s,m,m,s,m,s,s,s,m,s,m,s,t),
        out_specs=(t,t,m,s,s,m,s,m,m,s,m,s,s,s,m,s,m,s),check_vma=False)
```

profile of v0, /device:TPU:0, one launch (start us, length us, event | category | flops | bytes accessed | tf_op | source)
XLA Modules:
  0.0 387.1 jit_solution(17839026900530220423)
XLA Ops:
  1.3 1.5 small.1
  2.8 1.2 compare_select_fusion.3.idx_ref
  4.0 2.0 pack_a.1
  5.9 2.9 collective-permute-start.3
  8.9 1.5 collective-permute-start.4
  10.4 2.0 collective-permute-start.1
  12.4 1.5 collective-permute-start.2
  14.6 1.1 fusion.1.fk_ref
  15.7 5.6 %collective-permute-done = bf16[14,768]{1,0:T(8,128)(2,1)S(1)} collective-permute-done((bf16[14,768]{1,0:T(8,128)(2,1)}, bf16[14,768]{1,0:T(8,128)(2,1)S(1)}, u32[]{:S(2)}, u32[]{:S(2)}) %collective-permute-start) | collective-permute-done | bytes 21536 | tf_op jit(solution)/shard_map/ppermute | solution.py:660
  21.4 1.4 collective-permute-start.5
  23.6 1.4 convolution_convert_fusion
  25.4 1.8 collective-permute-start.7
  27.2 1.4 collective-permute-start.8
  28.6 1.1 select_convert_fusion.fq_ref
  29.7 2.9 pack_b.1
  34.3 1.5 collective-permute-start.12
  38.4 1.5 collective-permute-done.11.refs_11_
  39.9 18.8 %qkv.1 = (bf16[2048,768]{1,0:T(8,128)(2,1)}, bf16[2048,768]{1,0:T(8,128)(2,1)}, bf16[2048,768]{1,0:T(8,128)(2,1)}, bf16[768,2048]{1,0:T(8,128)(2,1)}, bf16[3,768,768]{2,1,0:T(8,128)(2,1)}) custom-call(s32[13]{0:T(128)} %compare_select_fusion.3.idx_ref, f32[2048,768]{1,0:T(8,128)} %bitcast.70, f32[2,1,768]{2,1,0:T(1,128)} %reshape.146.refs_1_.row_ref, ...), custom_call_target="tpu_custom_call" | custom-call | flops 724775744 | bytes 2103705 | tf_op jit(solution)/shard_map/qkv/pallas_call | solution.py:117
  58.7 11.3 %attn_fwd.3 = (bf16[2048,768]{1,0:T(8,128)(2,1)}, bf16[2048,768]{1,0:T(8,128)(2,1)}) custom-call(s32[26]{0:T(128)} %pad_add_fusion.1.s_ref, bf16[2048,768]{1,0:T(8,128)(2,1)} %get-tuple-element.146.q_ref, bf16[2048,768]{1,0:T(8,128)(2,1)} %get-tuple-element.147.k_ref, bf16[2048,768]{1,0:T(8,128)(2,1)} %get-tuple-element.148.v_ref, ...), custom_call_target="tpu_custom_call" | custom-call | flops 644245120 | bytes 550502 | tf_op jit(solution)/shard_map/attn_fwd/pallas_call | solution.py:238
  70.0 1.6 collective-permute-start.14
  72.1 19.9 %attn_fwd.4 = (bf16[2048,768]{1,0:T(8,128)(2,1)}, bf16[2048,768]{1,0:T(8,128)(2,1)}) custom-call(s32[26]{0:T(128)} %pad_add_fusion.1.s_ref, bf16[2048,768]{1,0:T(8,128)(2,1)} %get-tuple-element.146.q_ref, bf16[2048,768]{1,0:T(8,128)(2,1)} %get-tuple-element.147.k_ref, ...), custom_call_target="tpu_custom_call", output_to_operand_aliasing={{0}: (6, {}), {1}: (7, {})} | custom-call | flops 1288490240 | bytes 1101004 | tf_op jit(solution)/shard_map/attn_fwd/pallas_call | solution.py:238
  92.1 11.3 %attn_fwd.5 = (bf16[2048,768]{1,0:T(8,128)(2,1)}, bf16[2048,768]{1,0:T(8,128)(2,1)}) custom-call(s32[26]{0:T(128)} %pad_add_fusion.1.s_ref, bf16[2048,768]{1,0:T(8,128)(2,1)} %get-tuple-element.146.q_ref, bf16[2048,768]{1,0:T(8,128)(2,1)} %get-tuple-element.147.k_ref, ...), custom_call_target="tpu_custom_call", output_to_operand_aliasing={{0}: (6, {}), {1}: (7, {})} | custom-call | flops 644245120 | bytes 550502 | tf_op jit(solution)/shard_map/attn_fwd/pallas_call | solution.py:238
  103.4 89.0 %mid.1 = (f32[2048,768]{1,0:T(8,128)}, bf16[2048,768]{1,0:T(8,128)(2,1)}, bf16[2048,768]{1,0:T(8,128)(2,1)}, bf16[4,1728,384]{2,1,0:T(8,128)(2,1)}, bf16[4,1728,...) custom-call(s32[13]{0:T(128)} %compare_select_fusion.3.idx_ref, f32[2048,768]{1,0:T(8,128)} %bitcast.71, ...), custom_call_target="tpu_custom_call" | custom-call | flops 6522981376 | bytes 10223616 | tf_op jit(solution)/shard_map/mid/pallas_call | solution.py:439
  192.9 14.0 %attn_bwd.4.refs_0_ = bf16[3,2048,768]{2,1,0:T(8,128)(2,1)} custom-call(s32[26]{0:T(128)} %pad_add_fusion.1.s_ref, bf16[2048,768]{1,0:T(8,128)(2,1)} %get-tuple-element.146.q_ref, bf16[2048,768]{1,0:T(8,128)(2,1)} %get-tuple-element.147.k_ref, bf16[2048,768]{1,0:T(8,128)(2,1)} %get-tuple-element.148.v_ref, bf16[2048,768]{1,0:T(8,128)(2,1)} %get-tuple-element.165.fx_ref, ...), custom_call_target="tpu_custom_call" | custom-call | flops 1073741824 | bytes 524288 | tf_op jit(solution)/shard_map/attn_bwd/pallas_call | solution.py:321
  206.9 4.7 %add_convert_fusion = bf16[2,1728,384]{2,1,0:T(8,128)(2,1)} fusion(bf16[4,1728,384]{2,1,0:T(8,128)(2,1)} %collective-permute-done.18, bf16[4,1728,384]{2,1,0:T(8,128)(2,1)} %get-tuple-element.169), kind=kLoop, calls=%fused_computation | loop fusion | flops 5308416 | bytes 7962624 | tf_op jit(solution)/shard_map/convert_element_type | solution.py:700
  212.2 29.9 %attn_bwd.5.refs_0_ = bf16[3,2048,768]{2,1,0:T(8,128)(2,1)} custom-call(s32[26]{0:T(128)} %pad_add_fusion.1.s_ref, bf16[2048,768]{1,0:T(8,128)(2,1)} %get-tuple-element.146.q_ref, bf16[2048,768]{1,0:T(8,128)(2,1)} %get-tuple-element.147.k_ref, bf16[2048,768]{1,0:T(8,128)(2,1)} %get-tuple-element.148.v_ref, ...), custom_call_target="tpu_custom_call", output_to_operand_aliasing={{}: (8, {})} | custom-call | flops 2684354560 | bytes 1310720 | tf_op jit(solution)/shard_map/attn_bwd/pallas_call | solution.py:321
  242.1 1.7 collective-permute-done.19
  243.8 4.2 %add_convert_fusion.2 = bf16[1,1728,384]{2,1,0:T(8,128)(2,1)} fusion(bf16[2,1728,384]{2,1,0:T(8,128)(2,1)S(1)} %collective-permute-done.19, bf16[4,1728,384]{2,1,0:T(8,128)(2,1)} %collective-permute-done.18, bf16[4,1728,384]{2,1,0:T(8,128)(2,1)} %get-tuple-element.169), kind=kLoop, calls=%fused_computation.2 | loop fusion | flops 3981312 | bytes 5308416 | tf_op jit(solution)/shard_map/convert_element_type | solution.py:700
  248.6 19.3 %attn_bwd.6.refs_0_ = bf16[3,2048,768]{2,1,0:T(8,128)(2,1)} custom-call(s32[26]{0:T(128)} %pad_add_fusion.1.s_ref, bf16[2048,768]{1,0:T(8,128)(2,1)} %get-tuple-element.146.q_ref, bf16[2048,768]{1,0:T(8,128)(2,1)} %get-tuple-element.147.k_ref, bf16[2048,768]{1,0:T(8,128)(2,1)} %get-tuple-element.148.v_ref, ...), custom_call_target="tpu_custom_call", output_to_operand_aliasing={{}: (8, {})} | custom-call | flops 1610612736 | bytes 786432 | tf_op jit(solution)/shard_map/attn_bwd/pallas_call | solution.py:321
  268.0 3.2 add_convert_fusion.1
  271.3 1.9 collective-permute-start.21
  273.1 2.4 collective-permute-start.22
  275.7 13.8 %attn_bwd.7.d_ref = bf16[3,2048,768]{2,1,0:T(8,128)(2,1)} custom-call(s32[26]{0:T(128)} %pad_add_fusion.1.s_ref, bf16[2048,768]{1,0:T(8,128)(2,1)} %get-tuple-element.146.q_ref, bf16[2048,768]{1,0:T(8,128)(2,1)} %get-tuple-element.147.k_ref, bf16[2048,768]{1,0:T(8,128)(2,1)} %get-tuple-element.148.v_ref, ...), custom_call_target="tpu_custom_call", output_to_operand_aliasing={{}: (8, {})} | custom-call | flops 1073741824 | bytes 524288 | tf_op jit(solution)/shard_map/attn_bwd/pallas_call | solution.py:321
  289.5 14.4 %dw.1 = (bf16[4,576,384]{2,1,0:T(8,128)(2,1)}, bf16[4,576,384]{2,1,0:T(8,128)(2,1)}, f32[16,768]{1,0:T(8,128)}) custom-call(s32[13]{0:T(128)} %compare_select_fusion.3.idx_ref, bf16[768,2048]{1,0:T(8,128)(2,1)} %get-tuple-element.182.nt_ref, bf16[3,2048,768]{2,1,0:T(8,128)(2,1)} %attn_bwd.7.d_ref), custom_call_target="tpu_custom_call" | custom-call | flops 724775744 | bytes 1966080 | tf_op jit(solution)/shard_map/dw/pallas_call | solution.py:482
  304.7 2.0 fusion.4
  306.7 1.9 collective-permute-done.24
  308.6 2.9 add_convert_fusion.3
  313.4 3.5 collective-permute-start.26
  317.0 1.0 bitcast_dynamic-update-slice_fusion.3
  318.1 15.8 %dx.1 = (f32[2048,768]{1,0:T(8,128)}, f32[16,768]{1,0:T(8,128)}, f32[2,8,768]{2,1,0:T(8,128)}) custom-call(f32[2048,768]{1,0:T(8,128)} %bitcast.72, f32[2,1,768]{2,1,0:T(1,128)} %reshape.146.refs_1_.row_ref, bf16[3,2048,768]{2,1,0:T(8,128)(2,1)} %attn_bwd.7.d_ref, bf16[2048,768]{1,0:T(8,128)(2,1)} %get-tuple-element.195.gm_ref, ...), custom_call_target="tpu_custom_call" | custom-call | flops 724775744 | bytes 2870476 | tf_op jit(solution)/shard_map/dx/pallas_call | solution.py:519
  333.9 1.3 add_convert_fusion.5
  335.2 1.4 collective-permute-start.32
  336.6 1.0 bitcast_dynamic-update-slice_fusion.2
  337.6 1.7 sums.1.refs_0_
  339.3 1.2 collective-permute-start.31
  340.5 1.0 bitcast_dynamic-update-slice_fusion.1
  341.5 1.5 collective-permute-start.29
  345.4 1.5 add_convert_fusion.4
  347.6 3.8 collective-permute-start.34
  351.5 1.0 bitcast_dynamic-update-slice_fusion
  352.6 1.6 group.1.refs_0_
  354.1 2.4 collective-permute-done.34
  356.5 1.5 collective-permute-done.35
  359.3 1.4 collective-permute-start.41
  360.7 2.4 collective-permute-start.43
  363.7 1.5 collective-permute-start.37
  365.2 1.2 collective-permute-start.38
  366.4 1.9 collective-permute-start.39
  368.6 2.2 collective-permute-start.45
  370.9 1.2 collective-permute-start.46
  373.1 4.5 %unpack.2 = (f32[192,768]{1,0:T(8,128)}, f32[192,3072]{1,0:T(8,128)}, f32[768,768]{1,0:T(8,128)}) custom-call(s32[13]{0:T(128)} %compare_select_fusion.3.idx_ref, bf16[1728,384]{1,0:T(8,128)(2,1)} %bitcast.77, bf16[1728,384]{1,0:T(8,128)(2,1)} %copy-done.5), custom_call_target="tpu_custom_call" | custom-call | bytes 796262 | tf_op jit(solution)/shard_map/unpack/pallas_call | solution.py:608
  377.6 1.0 collective-permute-done.38
  378.8 2.5 table.1
  382.8 2.5 unpack.3
  (145 shorter events, 21.5 us)
Async XLA Ops:
  5.9 21.2 %collective-permute-start.3 = (bf16[576,384]{1,0:T(8,128)(2,1)}, bf16[576,384]{1,0:T(8,128)(2,1)S(1)}, u32[]{:S(2)}, u32[]{:S(2)}) collective-permute-start(bf16[576,384]{1,0:T(8,128)(2,1)} %pack_a.1), channel_id=1, source_target_pairs={{0,1},{1,0},{2,3},{3,2},{4,5},{5,4},{6,7},{7,6},{8,9},{9,8},{10,11... | collective-permute-start | bytes 1327112 | tf_op jit(solution)/shard_map/ppermute | solution.py:660
  8.9 23.8 %collective-permute-start.4 = (bf16[576,384]{1,0:T(8,128)(2,1)}, bf16[576,384]{1,0:T(8,128)(2,1)S(1)}, u32[]{:S(2)}, u32[]{:S(2)}) collective-permute-start(bf16[576,384]{1,0:T(8,128)(2,1)} %pack_a.1), channel_id=1, source_target_pairs={{0,2},{1,3},{2,0},{3,1},{4,6},{5,7},{6,4},{7,5},{8,10},{9,11},{10,... | collective-permute-start | bytes 1327112 | tf_op jit(solution)/shard_map/ppermute | solution.py:660
  10.4 11.0 %collective-permute-start = (bf16[14,768]{1,0:T(8,128)(2,1)}, bf16[14,768]{1,0:T(8,128)(2,1)S(1)}, u32[]{:S(2)}, u32[]{:S(2)}) collective-permute-start(bf16[14,768]{1,0:T(8,128)(2,1)} %get-tuple-element.137), channel_id=1, source_target_pairs={{0,3},{1,2},{2,1},{3,0},{4,7},{5,6},{6,5},{7,4},{8,11},{9,10},{10,... | collective-permute-start | bytes 64520 | tf_op jit(solution)/shard_map/ppermute | solution.py:660
  10.4 12.4 %collective-permute-start.1 = (bf16[14,768]{1,0:T(8,128)(2,1)}, bf16[14,768]{1,0:T(8,128)(2,1)S(1)}, u32[]{:S(2)}, u32[]{:S(2)}) collective-permute-start(bf16[14,768]{1,0:T(8,128)(2,1)} %get-tuple-element.137), channel_id=1, source_target_pairs={{0,2},{1,3},{2,0},{3,1},{4,6},{5,7},{6,4},{7,5},{8,10},{9,11},{10,... | collective-permute-start | bytes 64520 | tf_op jit(solution)/shard_map/ppermute | solution.py:660
  12.4 10.4 %collective-permute-start.2 = (bf16[14,768]{1,0:T(8,128)(2,1)}, bf16[14,768]{1,0:T(8,128)(2,1)S(1)}, u32[]{:S(2)}, u32[]{:S(2)}) collective-permute-start(bf16[14,768]{1,0:T(8,128)(2,1)} %get-tuple-element.137), channel_id=1, source_target_pairs={{0,1},{1,0},{2,3},{3,2},{4,5},{5,4},{6,7},{7,6},{8,9},{9,8},{10,11... | collective-permute-start | bytes 64520 | tf_op jit(solution)/shard_map/ppermute | solution.py:660
  21.4 11.6 %collective-permute-start.5 = (bf16[576,384]{1,0:T(8,128)(2,1)}, bf16[576,384]{1,0:T(8,128)(2,1)S(1)}, u32[]{:S(2)}, u32[]{:S(2)}) collective-permute-start(bf16[576,384]{1,0:T(8,128)(2,1)} %pack_a.1), channel_id=1, source_target_pairs={{0,3},{1,2},{2,1},{3,0},{4,7},{5,6},{6,5},{7,4},{8,11},{9,10},{10,... | collective-permute-start | bytes 1327112 | tf_op jit(solution)/shard_map/ppermute | solution.py:660
  23.6 9.1 %copy-start.8 = (f32[14,768]{1,0:T(8,128)}, f32[14,768]{1,0:T(8,128)S(1)}, u32[]{:S(2)}) copy-start(f32[14,768]{1,0:T(8,128)S(1)} %convert_add_fusion.2.refs_2_.refs_4_.vec_ref) | copy-start | bytes 129028
  23.6 12.7 %copy-start.19 = (s32[2,1024]{1,0:T(2,128)S(1)}, s32[2,1024]{1,0:T(2,128)}, u32[]{:S(2)}) copy-start(s32[2,1024]{1,0:T(2,128)} %param.24) | copy-start | bytes 24580
  23.6 13.8 %copy-start.23 = (s32[24]{0:T(128)S(1)}, s32[24]{0:T(128)}, u32[]{:S(2)}) copy-start(s32[24]{0:T(128)} %constant.141.clone) | copy-start | bytes 292
  25.0 7.9 %collective-permute-start.6 = (bf16[2,768]{1,0:T(2,128)(2,1)S(1)}, bf16[2,768]{1,0:T(2,128)(2,1)S(1)}, u32[]{:S(2)}, u32[]{:S(2)}) collective-permute-start(bf16[2,768]{1,0:T(2,128)(2,1)S(1)} %get-tuple-element.263), channel_id=1, source_target_pairs={{0,1},{1,0},{2,3},{3,2},{4,5},{5,4},{6,7},{7,6},{8,9},{9,8},{10,11... | collective-permute-start | bytes 9224 | tf_op jit(solution)/shard_map/ppermute | solution.py:660
  25.4 7.6 %collective-permute-start.7 = (bf16[2,768]{1,0:T(2,128)(2,1)S(1)}, bf16[2,768]{1,0:T(2,128)(2,1)S(1)}, u32[]{:S(2)}, u32[]{:S(2)}) collective-permute-start(bf16[2,768]{1,0:T(2,128)(2,1)S(1)} %get-tuple-element.262), channel_id=1, source_target_pairs={{0,2},{1,3},{2,0},{3,1},{4,6},{5,7},{6,4},{7,5},{8,10},{9,11},{10,... | collective-permute-start | bytes 9224 | tf_op jit(solution)/shard_map/ppermute | solution.py:660
  27.2 12.8 %copy-start.10 = (bf16[576,384]{1,0:T(8,128)(2,1)}, bf16[576,384]{1,0:T(8,128)(2,1)S(1)}, u32[]{:S(2)}) copy-start(bf16[576,384]{1,0:T(8,128)(2,1)S(1)} %collective-permute-done.3.refs_6_) | copy-start | bytes 1327108
  27.2 5.8 %collective-permute-start.8 = (bf16[2,768]{1,0:T(2,128)(2,1)S(1)}, bf16[2,768]{1,0:T(2,128)(2,1)S(1)}, u32[]{:S(2)}, u32[]{:S(2)}) collective-permute-start(bf16[2,768]{1,0:T(2,128)(2,1)S(1)} %get-tuple-element.261), channel_id=1, source_target_pairs={{0,3},{1,2},{2,1},{3,0},{4,7},{5,6},{6,5},{7,4},{8,11},{9,10},{10,... | collective-permute-start | bytes 9224 | tf_op jit(solution)/shard_map/ppermute | solution.py:660
  32.7 7.3 %copy-start.11 = (bf16[576,384]{1,0:T(8,128)(2,1)}, bf16[576,384]{1,0:T(8,128)(2,1)S(1)}, u32[]{:S(2)}) copy-start(bf16[576,384]{1,0:T(8,128)(2,1)S(1)} %collective-permute-done.4.refs_7_) | copy-start | bytes 1327108
  34.3 35.7 %collective-permute-start.12 = (bf16[1728,384]{1,0:T(8,128)(2,1)}, bf16[1728,384]{1,0:T(8,128)(2,1)S(1)}, u32[]{:S(2)}, u32[]{:S(2)}) collective-permute-start(bf16[1728,384]{1,0:T(8,128)(2,1)} %pack_b.1), channel_id=1, source_target_pairs={{0,1},{1,0},{2,3},{3,2},{4,6},{5,7},{6,4},{7,5},{8,9},{9,8},{10,11... | collective-permute-start | bytes 3981320 | tf_op jit(solution)/shard_map/ppermute | solution.py:660
  35.8 34.2 %collective-permute-start.13 = (bf16[1728,384]{1,0:T(8,128)(2,1)}, bf16[1728,384]{1,0:T(8,128)(2,1)S(1)}, u32[]{:S(2)}, u32[]{:S(2)}) collective-permute-start(bf16[1728,384]{1,0:T(8,128)(2,1)} %pack_b.1), channel_id=1, source_target_pairs={{0,2},{1,3},{2,0},{3,1},{4,5},{5,4},{6,7},{7,6},{8,10},{9,11},{10,... | collective-permute-start | bytes 3981320 | tf_op jit(solution)/shard_map/ppermute | solution.py:660
  36.5 2.0 collective-permute-start.10
  36.5 3.4 collective-permute-start.11
  37.0 2.9 collective-permute-start.9
  70.0 22.0 %copy-start.6 = (bf16[1728,384]{1,0:T(8,128)(2,1)}, bf16[1728,384]{1,0:T(8,128)(2,1)S(1)}, u32[]{:S(2)}) copy-start(bf16[1728,384]{1,0:T(8,128)(2,1)S(1)} %collective-permute-done.12.refs_8_) | copy-start | bytes 3981316
  70.0 22.0 %copy-start.7 = (bf16[1728,384]{1,0:T(8,128)(2,1)}, bf16[1728,384]{1,0:T(8,128)(2,1)S(1)}, u32[]{:S(2)}) copy-start(bf16[1728,384]{1,0:T(8,128)(2,1)S(1)} %collective-permute-done.13.refs_9_) | copy-start | bytes 3981316
  70.0 22.0 %collective-permute-start.14 = (bf16[1728,384]{1,0:T(8,128)(2,1)S(1)}, bf16[1728,384]{1,0:T(8,128)(2,1)}, u32[]{:S(2)}, u32[]{:S(2)}) collective-permute-start(bf16[1728,384]{1,0:T(8,128)(2,1)S(1)} %collective-permute-done.12.refs_8_), channel_id=1, source_target_pairs={{0,2},{1,3},{2,0},{3,1},{4,5},{5,4},{6,7},{7,6},{8,10},{9,11},{10,... | collective-permute-start | bytes 3981320 | tf_op jit(solution)/shard_map/ppermute | solution.py:660
  71.5 31.8 %collective-permute-start.15 = (bf16[1728,384]{1,0:T(8,128)(2,1)S(1)}, bf16[1728,384]{1,0:T(8,128)(2,1)}, u32[]{:S(2)}, u32[]{:S(2)}) collective-permute-start(bf16[1728,384]{1,0:T(8,128)(2,1)S(1)} %collective-permute-done.12.refs_8_), channel_id=1, source_target_pairs={{0,4},{1,5},{2,6},{3,7},{4,0},{5,1},{6,2},{7,3},{8,12},{9,13},{10,... | collective-permute-start | bytes 3981320 | tf_op jit(solution)/shard_map/ppermute | solution.py:660
  71.6 31.8 %collective-permute-start.16 = (bf16[1728,384]{1,0:T(8,128)(2,1)S(1)}, bf16[1728,384]{1,0:T(8,128)(2,1)}, u32[]{:S(2)}, u32[]{:S(2)}) collective-permute-start(bf16[1728,384]{1,0:T(8,128)(2,1)S(1)} %collective-permute-done.13.refs_9_), channel_id=1, source_target_pairs={{0,4},{1,5},{2,6},{3,7},{4,0},{5,1},{6,2},{7,3},{8,12},{9,13},{10,... | collective-permute-start | bytes 3981320 | tf_op jit(solution)/shard_map/ppermute | solution.py:660
  91.9 11.4 %collective-permute-start.17 = (bf16[1728,384]{1,0:T(8,128)(2,1)}, bf16[1728,384]{1,0:T(8,128)(2,1)}, u32[]{:S(2)}, u32[]{:S(2)}) collective-permute-start(bf16[1728,384]{1,0:T(8,128)(2,1)} %collective-permute-done.14.refs_10_), channel_id=1, source_target_pairs={{0,4},{1,5},{2,6},{3,7},{4,0},{5,1},{6,2},{7,3},{8,12},{9,13},{10,... | collective-permute-start | bytes 3981320 | tf_op jit(solution)/shard_map/ppermute | solution.py:660
  192.4 14.5 %collective-permute-start.18 = (bf16[4,1728,384]{2,1,0:T(8,128)(2,1)}, bf16[4,1728,384]{2,1,0:T(8,128)(2,1)}, u32[]{:S(2)}, u32[]{:S(2)}) collective-permute-start(bf16[4,1728,384]{2,1,0:T(8,128)(2,1)} %get-tuple-element.167), channel_id=1, source_target_pairs={{0,4},{1,5},{2,6},{3,7},{4,0},{5,1},{6,2},{7,3},{8,12},{9,13},{10,... | collective-permute-start | bytes 15925256 | tf_op jit(solution)/shard_map/ppermute | solution.py:660
  211.6 32.2 %collective-permute-start.19 = (bf16[2,1728,384]{2,1,0:T(8,128)(2,1)}, bf16[2,1728,384]{2,1,0:T(8,128)(2,1)S(1)}, u32[]{:S(2)}, u32[]{:S(2)}) collective-permute-start(bf16[2,1728,384]{2,1,0:T(8,128)(2,1)} %add_convert_fusion), channel_id=1, source_target_pairs={{0,2},{1,3},{2,0},{3,1},{4,5},{5,4},{6,7},{7,6},{8,10},{9,11},{10,... | collective-permute-start | bytes 7962632 | tf_op jit(solution)/shard_map/ppermute | solution.py:660
  243.8 4.8 %copy-start.1 = (bf16[2,1728,384]{2,1,0:T(8,128)(2,1)}, bf16[2,1728,384]{2,1,0:T(8,128)(2,1)S(1)}, u32[]{:S(2)}) copy-start(bf16[2,1728,384]{2,1,0:T(8,128)(2,1)S(1)} %collective-permute-done.19) | copy-start | bytes 7962628
  248.1 19.9 %collective-permute-start.20 = (bf16[1,1728,384]{2,1,0:T(8,128)(2,1)}, bf16[1,1728,384]{2,1,0:T(8,128)(2,1)}, u32[]{:S(2)}, u32[]{:S(2)}) collective-permute-start(bf16[1,1728,384]{2,1,0:T(8,128)(2,1)} %add_convert_fusion.2), channel_id=1, source_target_pairs={{0,1},{1,0},{2,3},{3,2},{4,6},{5,7},{6,4},{7,5},{8,9},{9,8},{10,11... | collective-permute-start | bytes 3981320 | tf_op jit(solution)/shard_map/ppermute | solution.py:660
  271.3 32.6 %collective-permute-start.21 = (bf16[432,384]{1,0:T(8,128)(2,1)S(1)}, bf16[432,384]{1,0:T(8,128)(2,1)S(1)}, u32[]{:S(2)}, u32[]{:S(2)}) collective-permute-start(bf16[432,384]{1,0:T(8,128)(2,1)S(1)} %get-tuple-element.185), channel_id=1, source_target_pairs={{0,8},{1,9},{2,10},{3,11},{4,12},{5,13},{6,14},{7,15},{8,0},{9,1},... | collective-permute-start | bytes 995336 | tf_op jit(solution)/shard_map/ppermute | solution.py:660
  273.1 30.7 %collective-permute-start.22 = (bf16[432,384]{1,0:T(8,128)(2,1)S(1)}, bf16[432,384]{1,0:T(8,128)(2,1)S(1)}, u32[]{:S(2)}, u32[]{:S(2)}) collective-permute-start(bf16[432,384]{1,0:T(8,128)(2,1)S(1)} %get-tuple-element.186), channel_id=1, source_target_pairs={{0,16},{1,17},{2,18},{3,19},{4,20},{5,21},{6,22},{7,23},{8,24},{9,... | collective-permute-start | bytes 995336 | tf_op jit(solution)/shard_map/ppermute | solution.py:660
  275.6 28.3 %collective-permute-start.23 = (bf16[432,384]{1,0:T(8,128)(2,1)S(1)}, bf16[432,384]{1,0:T(8,128)(2,1)S(1)}, u32[]{:S(2)}, u32[]{:S(2)}) collective-permute-start(bf16[432,384]{1,0:T(8,128)(2,1)S(1)} %get-tuple-element.187), channel_id=1, source_target_pairs={{0,24},{1,25},{2,26},{3,27},{4,28},{5,29},{6,30},{7,31},{8,16},{9,... | collective-permute-start | bytes 995336 | tf_op jit(solution)/shard_map/ppermute | solution.py:660
  304.7 3.9 %collective-permute-start.24 = (bf16[4,576,384]{2,1,0:T(8,128)(2,1)}, bf16[4,576,384]{2,1,0:T(8,128)(2,1)S(1)}, u32[]{:S(2)}, u32[]{:S(2)}) collective-permute-start(bf16[4,576,384]{2,1,0:T(8,128)(2,1)} %get-tuple-element.191), channel_id=1, source_target_pairs={{0,4},{1,5},{2,6},{3,7},{4,0},{5,1},{6,2},{7,3},{8,12},{9,13},{10,... | collective-permute-start | bytes 5308424 | tf_op jit(solution)/shard_map/ppermute | solution.py:660
  308.6 9.5 %copy-start.4 = (bf16[4,576,384]{2,1,0:T(8,128)(2,1)}, bf16[4,576,384]{2,1,0:T(8,128)(2,1)S(1)}, u32[]{:S(2)}) copy-start(bf16[4,576,384]{2,1,0:T(8,128)(2,1)S(1)} %collective-permute-done.24) | copy-start | bytes 5308420
  311.6 22.3 %collective-permute-start.28 = (bf16[2,576,384]{2,1,0:T(8,128)(2,1)}, bf16[2,576,384]{2,1,0:T(8,128)(2,1)}, u32[]{:S(2)}, u32[]{:S(2)}) collective-permute-start(bf16[2,576,384]{2,1,0:T(8,128)(2,1)} %add_convert_fusion.3), channel_id=1, source_target_pairs={{0,2},{1,3},{2,0},{3,1},{4,5},{5,4},{6,7},{7,6},{8,10},{9,11},{10,... | collective-permute-start | bytes 2654216 | tf_op jit(solution)/shard_map/ppermute | solution.py:660
  312.5 24.1 %collective-permute-start.25 = (bf16[432,384]{1,0:T(8,128)(2,1)}, bf16[432,384]{1,0:T(8,128)(2,1)}, u32[]{:S(2)}, u32[]{:S(2)}) collective-permute-start(bf16[432,384]{1,0:T(8,128)(2,1)} %fusion.4), channel_id=1, source_target_pairs={{0,8},{1,9},{2,10},{3,11},{4,12},{5,13},{6,14},{7,15},{8,0},{9,1},... | collective-permute-start | bytes 995336 | tf_op jit(solution)/shard_map/ppermute | solution.py:660
  313.4 27.1 %collective-permute-start.26 = (bf16[432,384]{1,0:T(8,128)(2,1)}, bf16[432,384]{1,0:T(8,128)(2,1)}, u32[]{:S(2)}, u32[]{:S(2)}) collective-permute-start(bf16[432,384]{1,0:T(8,128)(2,1)} %fusion.4), channel_id=1, source_target_pairs={{0,16},{1,17},{2,18},{3,19},{4,20},{5,21},{6,22},{7,23},{8,24},{9,... | collective-permute-start | bytes 995336 | tf_op jit(solution)/shard_map/ppermute | solution.py:660
  316.9 34.6 %collective-permute-start.27 = (bf16[432,384]{1,0:T(8,128)(2,1)}, bf16[432,384]{1,0:T(8,128)(2,1)}, u32[]{:S(2)}, u32[]{:S(2)}) collective-permute-start(bf16[432,384]{1,0:T(8,128)(2,1)} %fusion.4), channel_id=1, source_target_pairs={{0,24},{1,25},{2,26},{3,27},{4,28},{5,29},{6,30},{7,31},{8,16},{9,... | collective-permute-start | bytes 995336 | tf_op jit(solution)/shard_map/ppermute | solution.py:660
  318.1 15.8 %copy-start.3 = (bf16[4,576,384]{2,1,0:T(8,128)(2,1)S(1)}, bf16[4,576,384]{2,1,0:T(8,128)(2,1)}, u32[]{:S(2)}) copy-start(bf16[4,576,384]{2,1,0:T(8,128)(2,1)} %get-tuple-element.193) | copy-start | bytes 5308420
  335.2 10.2 %collective-permute-start.32 = (bf16[1,576,384]{2,1,0:T(8,128)(2,1)S(1)}, bf16[1,576,384]{2,1,0:T(8,128)(2,1)}, u32[]{:S(2)}, u32[]{:S(2)}) collective-permute-start(bf16[1,576,384]{2,1,0:T(8,128)(2,1)S(1)} %add_convert_fusion.5), channel_id=1, source_target_pairs={{0,1},{1,0},{2,3},{3,2},{4,6},{5,7},{6,4},{7,5},{8,9},{9,8},{10,11... | collective-permute-start | bytes 1327112 | tf_op jit(solution)/shard_map/ppermute | solution.py:660
  339.3 5.5 %collective-permute-start.31 = (bf16[16,768]{1,0:T(8,128)(2,1)}, bf16[16,768]{1,0:T(8,128)(2,1)S(1)}, u32[]{:S(2)}, u32[]{:S(2)}) collective-permute-start(bf16[16,768]{1,0:T(8,128)(2,1)} %sums.1.refs_0_), channel_id=1, source_target_pairs={{0,3},{1,2},{2,1},{3,0},{4,7},{5,6},{6,5},{7,4},{8,11},{9,10},{10,... | collective-permute-start | bytes 73736 | tf_op jit(solution)/shard_map/ppermute | solution.py:660
  341.5 5.5 %collective-permute-start.29 = (bf16[16,768]{1,0:T(8,128)(2,1)}, bf16[16,768]{1,0:T(8,128)(2,1)S(1)}, u32[]{:S(2)}, u32[]{:S(2)}) collective-permute-start(bf16[16,768]{1,0:T(8,128)(2,1)} %sums.1.refs_0_), channel_id=1, source_target_pairs={{0,1},{1,0},{2,3},{3,2},{4,5},{5,4},{6,7},{7,6},{8,9},{9,8},{10,11... | collective-permute-start | bytes 73736 | tf_op jit(solution)/shard_map/ppermute | solution.py:660
  343.0 4.0 %collective-permute-start.30 = (bf16[16,768]{1,0:T(8,128)(2,1)}, bf16[16,768]{1,0:T(8,128)(2,1)S(1)}, u32[]{:S(2)}, u32[]{:S(2)}) collective-permute-start(bf16[16,768]{1,0:T(8,128)(2,1)} %sums.1.refs_0_), channel_id=1, source_target_pairs={{0,2},{1,3},{2,0},{3,1},{4,6},{5,7},{6,4},{7,5},{8,10},{9,11},{10,... | collective-permute-start | bytes 73736 | tf_op jit(solution)/shard_map/ppermute | solution.py:660
  347.0 4.5 %copy-start.21 = (bf16[16,768]{1,0:T(8,128)(2,1)}, bf16[16,768]{1,0:T(8,128)(2,1)S(1)}, u32[]{:S(2)}) copy-start(bf16[16,768]{1,0:T(8,128)(2,1)S(1)} %collective-permute-done.29.refs_1_) | copy-start | bytes 73732
  347.1 4.4 %copy-start.22 = (bf16[16,768]{1,0:T(8,128)(2,1)}, bf16[16,768]{1,0:T(8,128)(2,1)S(1)}, u32[]{:S(2)}) copy-start(bf16[16,768]{1,0:T(8,128)(2,1)S(1)} %collective-permute-done.30.refs_2_) | copy-start | bytes 73732
  347.1 7.1 %collective-permute-start.33 = (bf16[144,384]{1,0:T(8,128)(2,1)S(1)}, bf16[144,384]{1,0:T(8,128)(2,1)S(1)}, u32[]{:S(2)}, u32[]{:S(2)}) collective-permute-start(bf16[144,384]{1,0:T(8,128)(2,1)S(1)} %get-tuple-element.216), channel_id=1, source_target_pairs={{0,8},{1,9},{2,10},{3,11},{4,12},{5,13},{6,14},{7,15},{8,0},{9,1},... | collective-permute-start | bytes 331784 | tf_op jit(solution)/shard_map/ppermute | solution.py:660
  347.6 8.9 %collective-permute-start.34 = (bf16[144,384]{1,0:T(8,128)(2,1)S(1)}, bf16[144,384]{1,0:T(8,128)(2,1)S(1)}, u32[]{:S(2)}, u32[]{:S(2)}) collective-permute-start(bf16[144,384]{1,0:T(8,128)(2,1)S(1)} %get-tuple-element.250), channel_id=1, source_target_pairs={{0,16},{1,17},{2,18},{3,19},{4,20},{5,21},{6,22},{7,23},{8,24},{9,... | collective-permute-start | bytes 331784 | tf_op jit(solution)/shard_map/ppermute | solution.py:660
  351.4 6.7 %collective-permute-start.35 = (bf16[144,384]{1,0:T(8,128)(2,1)S(1)}, bf16[144,384]{1,0:T(8,128)(2,1)S(1)}, u32[]{:S(2)}, u32[]{:S(2)}) collective-permute-start(bf16[144,384]{1,0:T(8,128)(2,1)S(1)} %get-tuple-element.249), channel_id=1, source_target_pairs={{0,24},{1,25},{2,26},{3,27},{4,28},{5,29},{6,30},{7,31},{8,16},{9,... | collective-permute-start | bytes 331784 | tf_op jit(solution)/shard_map/ppermute | solution.py:660
  352.5 20.5 %copy-start = (bf16[4,432,384]{2,1,0:T(8,128)(2,1)}, bf16[4,432,384]{2,1,0:T(8,128)(2,1)S(1)}, u32[]{:S(2)}) copy-start(bf16[4,432,384]{2,1,0:T(8,128)(2,1)S(1)} %bitcast_dynamic-update-slice_fusion) | copy-start | bytes 3981316
  358.1 12.8 %collective-permute-start.36 = (bf16[1728,384]{1,0:T(8,128)(2,1)S(1)}, bf16[1728,384]{1,0:T(8,128)(2,1)S(1)}, u32[]{:S(2)}, u32[]{:S(2)}) collective-permute-start(bf16[1728,384]{1,0:T(8,128)(2,1)S(1)} %bitcast.76), channel_id=1, source_target_pairs={{0,4},{1,5},{2,6},{3,7},{4,0},{5,1},{6,2},{7,3},{8,12},{9,13},{10,... | collective-permute-start | bytes 3981320 | tf_op jit(solution)/shard_map/ppermute | solution.py:660
  358.8 4.3 %collective-permute-start.40 = (bf16[22,768]{1,0:T(8,128)(2,1)}, bf16[22,768]{1,0:T(8,128)(2,1)S(1)}, u32[]{:S(2)}, u32[]{:S(2)}) collective-permute-start(bf16[22,768]{1,0:T(8,128)(2,1)} %group.1.refs_0_), channel_id=1, source_target_pairs={{0,4},{1,5},{2,6},{3,7},{4,0},{5,1},{6,2},{7,3},{8,12},{9,13},{10,... | collective-permute-start | bytes 101384 | tf_op jit(solution)/shard_map/ppermute | solution.py:660
  359.3 4.4 %collective-permute-start.41 = (bf16[22,768]{1,0:T(8,128)(2,1)}, bf16[22,768]{1,0:T(8,128)(2,1)S(1)}, u32[]{:S(2)}, u32[]{:S(2)}) collective-permute-start(bf16[22,768]{1,0:T(8,128)(2,1)} %group.1.refs_0_), channel_id=1, source_target_pairs={{0,8},{1,9},{2,10},{3,11},{4,12},{5,13},{6,14},{7,15},{8,0},{9,1},... | collective-permute-start | bytes 101384 | tf_op jit(solution)/shard_map/ppermute | solution.py:660
  360.7 4.5 %collective-permute-start.42 = (bf16[22,768]{1,0:T(8,128)(2,1)}, bf16[22,768]{1,0:T(8,128)(2,1)S(1)}, u32[]{:S(2)}, u32[]{:S(2)}) collective-permute-start(bf16[22,768]{1,0:T(8,128)(2,1)} %group.1.refs_0_), channel_id=1, source_target_pairs={{0,12},{1,13},{2,14},{3,15},{4,8},{5,9},{6,10},{7,11},{8,4},{9,5},... | collective-permute-start | bytes 101384 | tf_op jit(solution)/shard_map/ppermute | solution.py:660
  360.7 5.7 %collective-permute-start.43 = (bf16[22,768]{1,0:T(8,128)(2,1)}, bf16[22,768]{1,0:T(8,128)(2,1)}, u32[]{:S(2)}, u32[]{:S(2)}) collective-permute-start(bf16[22,768]{1,0:T(8,128)(2,1)} %group.1.refs_0_), channel_id=1, source_target_pairs={{0,16},{1,17},{2,18},{3,19},{4,20},{5,21},{6,22},{7,23},{8,24},{9,... | collective-permute-start | bytes 101384 | tf_op jit(solution)/shard_map/ppermute | solution.py:660
  363.1 15.7 %copy-start.15 = (bf16[22,768]{1,0:T(8,128)(2,1)}, bf16[22,768]{1,0:T(8,128)(2,1)S(1)}, u32[]{:S(2)}) copy-start(bf16[22,768]{1,0:T(8,128)(2,1)S(1)} %collective-permute-done.40.refs_1_) | copy-start | bytes 101380
  363.1 5.6 %collective-permute-start.44 = (bf16[22,768]{1,0:T(8,128)(2,1)}, bf16[22,768]{1,0:T(8,128)(2,1)S(1)}, u32[]{:S(2)}, u32[]{:S(2)}) collective-permute-start(bf16[22,768]{1,0:T(8,128)(2,1)} %group.1.refs_0_), channel_id=1, source_target_pairs={{0,20},{1,21},{2,22},{3,23},{4,16},{5,17},{6,18},{7,19},{8,28},{9,... | collective-permute-start | bytes 101384 | tf_op jit(solution)/shard_map/ppermute | solution.py:660
  363.7 15.1 %copy-start.16 = (bf16[22,768]{1,0:T(8,128)(2,1)}, bf16[22,768]{1,0:T(8,128)(2,1)S(1)}, u32[]{:S(2)}) copy-start(bf16[22,768]{1,0:T(8,128)(2,1)S(1)} %collective-permute-done.41.refs_2_) | copy-start | bytes 101380
  363.7 13.9 %collective-permute-start.37 = (bf16[144,384]{1,0:T(8,128)(2,1)}, bf16[144,384]{1,0:T(8,128)(2,1)S(1)}, u32[]{:S(2)}, u32[]{:S(2)}) collective-permute-start(bf16[144,384]{1,0:T(8,128)(2,1)} %fusion.7), channel_id=1, source_target_pairs={{0,8},{1,9},{2,10},{3,11},{4,12},{5,13},{6,14},{7,15},{8,0},{9,1},... | collective-permute-start | bytes 331784 | tf_op jit(solution)/shard_map/ppermute | solution.py:660
  365.2 13.6 %copy-start.17 = (bf16[22,768]{1,0:T(8,128)(2,1)}, bf16[22,768]{1,0:T(8,128)(2,1)S(1)}, u32[]{:S(2)}) copy-start(bf16[22,768]{1,0:T(8,128)(2,1)S(1)} %collective-permute-done.42.refs_3_) | copy-start | bytes 101380
  365.2 13.4 %collective-permute-start.38 = (bf16[144,384]{1,0:T(8,128)(2,1)}, bf16[144,384]{1,0:T(8,128)(2,1)S(1)}, u32[]{:S(2)}, u32[]{:S(2)}) collective-permute-start(bf16[144,384]{1,0:T(8,128)(2,1)} %fusion.7), channel_id=1, source_target_pairs={{0,16},{1,17},{2,18},{3,19},{4,20},{5,21},{6,22},{7,23},{8,24},{9,... | collective-permute-start | bytes 331784 | tf_op jit(solution)/shard_map/ppermute | solution.py:660
  366.4 12.1 %collective-permute-start.39 = (bf16[144,384]{1,0:T(8,128)(2,1)}, bf16[144,384]{1,0:T(8,128)(2,1)S(1)}, u32[]{:S(2)}, u32[]{:S(2)}) collective-permute-start(bf16[144,384]{1,0:T(8,128)(2,1)} %fusion.7), channel_id=1, source_target_pairs={{0,24},{1,25},{2,26},{3,27},{4,28},{5,29},{6,30},{7,31},{8,16},{9,... | collective-permute-start | bytes 331784 | tf_op jit(solution)/shard_map/ppermute | solution.py:660
  368.6 8.9 %collective-permute-start.45 = (bf16[22,768]{1,0:T(8,128)(2,1)}, bf16[22,768]{1,0:T(8,128)(2,1)}, u32[]{:S(2)}, u32[]{:S(2)}) collective-permute-start(bf16[22,768]{1,0:T(8,128)(2,1)} %group.1.refs_0_), channel_id=1, source_target_pairs={{0,24},{1,25},{2,26},{3,27},{4,28},{5,29},{6,30},{7,31},{8,16},{9,... | collective-permute-start | bytes 101384 | tf_op jit(solution)/shard_map/ppermute | solution.py:660
  370.9 6.7 %collective-permute-start.46 = (bf16[22,768]{1,0:T(8,128)(2,1)}, bf16[22,768]{1,0:T(8,128)(2,1)}, u32[]{:S(2)}, u32[]{:S(2)}) collective-permute-start(bf16[22,768]{1,0:T(8,128)(2,1)} %group.1.refs_0_), channel_id=1, source_target_pairs={{0,28},{1,29},{2,30},{3,31},{4,24},{5,25},{6,26},{7,27},{8,20},{9,... | collective-permute-start | bytes 101384 | tf_op jit(solution)/shard_map/ppermute | solution.py:660
  378.7 2.6 collective-permute-start.47
  (8 other events, 13.0 us)
where the time goes:
time: 392 us; the launch traced here: 387 us
  Pallas kernels  276 us (70%)
  starting transfers between devices  51.7 us (13%)
  other arithmetic  26.4 us (7%)
  waiting for transfers between devices  17.8 us (5%)
  local copies, waits for them, and re-layouts  11.8 us (3%)
    pallas_call x1, Pallas kernels, mid(): pl.pallas_call(functools.partial(mid_kernel, tb=tb, fc=fc, ns=ns, wr=wr,...  89 us
    pallas_call x4, Pallas kernels, attn_bwd(): pl.pallas_call(functools.partial(bwd_kernel, f0=f0, ns=ns), grid_spec=plt...  77 us
    ppermute x48, starting transfers between devices, move(): return lax.ppermute(x, ('rep', 'shard'), pairs)  51.7 us
    pallas_call x3, Pallas kernels, attn_fwd(): pl.pallas_call(functools.partial(fwd_kernel, f0=f0, ns=ns), grid_spec=plt...  42.4 us
    pallas_call x1, Pallas kernels, qkv(): pl.pallas_call(functools.partial(qkv_kernel, ns=ns, wr=wr), grid_spec=plt...  18.8 us
    ppermute x48, waiting for transfers between devices, move(): return lax.ppermute(x, ('rep', 'shard'), pairs)  17.8 us
    pallas_call x1, Pallas kernels, dx(): pl.pallas_call(functools.partial(dx_kernel, per=per), grid=(T // tb,), in...  15.8 us
    pallas_call x1, Pallas kernels, dw(): pl.pallas_call(functools.partial(dw_kernel, ns=ns, wr=wr), grid_spec=pltp...  14.4 us
  transfers between devices with their start and end apart: 48, of which 12 were waited for; matrix products, arithmetic and copies ran while one was open for 4% of the time, Pallas kernels for 47%

commit v1 on v0

--- a/solution.py
+++ b/solution.py
@@ -562,33 +562,39 @@
         cost_estimate=cost(0,10**6),name="group")(idx,*pays)
 
 
-def table_kernel(me_ref,*refs,nr,rows,own):
-    sum_ref,tab_ref,acc,allr=refs[nr:]
-    r0=me_ref[0]
+def table_kernel(idx_ref,*refs,nr,rows,own,me,w,fr):
+    sum_refs=refs[nr:nr+8]
+    sub_ref,tab_ref,acc,allr=refs[nr+8:]
+    r0=idx_ref[me]
+    s0=idx_ref[me+1]
     for j in range(nr):
         acc[r0^j]=refs[j][...].astype(F32)
     tot=acc[0,0:VR]
     for r in range(1,nr):
         tot=tot+acc[r,0:VR]
-    sum_ref[...]=tot
+    mine=pltpu.roll(tot[0:8],D-s0*w,1)
+    for i,ref in enumerate(sum_refs):
+        ref[...]=mine[i:i+1,0:w].reshape(w)
+    wide=jnp.concatenate([tot[8+i:9+i] for i in range(FF//D)],axis=1)
+    sub_ref[...]=pltpu.roll(jnp.broadcast_to(wide,(8,FF)),FF-s0*fr,1)[0:1,0:fr].reshape(fr)
     for r in range(nr):
         allr[r*rows:(r+1)*rows,:]=acc[r,VR:VR+rows]
     n=nr*rows
     ids=tot[NV:NV+1,0:n]*32.0+tot[NV+1:NV+2,0:n]
-    line=lax.broadcasted_iota(jnp.int32,(own,n),0)+me_ref[1]*own
+    line=lax.broadcasted_iota(jnp.int32,(own,n),0)+s0*own
     hit=jnp.where(line==ids.astype(jnp.int32),1.0,0.0).astype(BF)
     tab_ref[...]=nn(hit,allr[...].astype(BF))
 
 
-def table(me,pays,own):
+def table(idx,pays,own,w,fr):
     nr=len(pays)
     rows=pays[0].shape[0]-VR
     vm=pl.BlockSpec(memory_space=pltpu.VMEM)
-    return pl.pallas_call(functools.partial(table_kernel,nr=nr,rows=rows,own=own),
-        in_specs=[pl.BlockSpec(memory_space=pltpu.SMEM)]+[vm]*nr,out_specs=[vm,vm],
-        out_shape=[S_((VR,D),F32),S_((own,D),F32)],
+    return pl.pallas_call(functools.partial(table_kernel,nr=nr,rows=rows,own=own,me=idx.shape[0]-3,w=w,fr=fr),
+        in_specs=[pl.BlockSpec(memory_space=pltpu.SMEM)]+[vm]*nr,out_specs=[vm]*10,
+        out_shape=[S_((w,),F32)]*8+[S_((fr,),F32),S_((own,D),F32)],
         scratch_shapes=[pltpu.VMEM((nr,VR+rows,D),F32),pltpu.VMEM((nr*rows,D),F32)],
-        cost_estimate=cost(0,4*10**6),name="table")(me,*pays)
+        cost_estimate=cost(0,4*10**6),name="table")(idx,*pays)
 
 
 def unpack_kernel(idx_ref,a_ref,b_ref,*outs,parts):
@@ -611,7 +617,8 @@
         cost_estimate=cost(0,12*a.shape[0]*HC),name="unpack")(idx,a,b)
 
 
-def small_kernel(me_ref,ts_ref,*refs,w,fr,nseq):
+def small_kernel(idx_ref,ts_ref,*refs,w,fr,nseq,me):
+    me_ref=[idx_ref[me+i] for i in range(3)]
     vecs=refs[:9]
     out_ref,id_ref=refs[9:]
     def spread(rows,width,at):
@@ -633,12 +640,12 @@
     out_ref[...]=jnp.concatenate([v]+[u[0:1,i*D:(i+1)*D] for i in range(FF//D)]+[steps(me_ref[1],True),steps(me_ref[1],False)],axis=0).astype(BF)
 
 
-def small_rows(me,time_steps,vecs):
+def small_rows(idx,time_steps,vecs):
     vm=pl.BlockSpec(memory_space=pltpu.VMEM)
     sm=pl.BlockSpec(memory_space=pltpu.SMEM)
-    return pl.pallas_call(functools.partial(small_kernel,w=vecs[0].shape[0],fr=vecs[8].shape[0],nseq=time_steps.shape[0]),
+    return pl.pallas_call(functools.partial(small_kernel,w=vecs[0].shape[0],fr=vecs[8].shape[0],nseq=time_steps.shape[0],me=idx.shape[0]-3),
         in_specs=[sm,sm]+[vm]*9,out_specs=[vm,vm],
-        out_shape=[S_((VR,D),BF),S_((2,D),F32)],cost_estimate=cost(0,10**6),name="small")(me,time_steps,*vecs)
+        out_shape=[S_((VR,D),BF),S_((2,D),F32)],cost_estimate=cost(0,10**6),name="small")(idx,time_steps,*vecs)
 
 
 class Ring:
@@ -684,9 +691,13 @@
     def index(self):
         m=[[self.mask(c,j) for j in range(self.S)] for c in (0,1)]
         base=list(range(self.S))
-        t=jnp.where(self.c==0,jnp.array([0]+base+m[0]+m[1],jnp.int32),jnp.array([0]+base+m[1]+m[0],jnp.int32))
-        head=jnp.arange(1+3*self.S)==0
-        return jnp.where(head,self.c,t^self.s).astype(jnp.int32)
+        n=1+3*self.S
+        t=jnp.where(self.c==0,jnp.array([0]+base+m[0]+m[1]+[0]*3,jnp.int32),jnp.array([0]+base+m[1]+m[0]+[0]*3,jnp.int32))
+        at=jnp.arange(n+3)
+        r=self.z*2+self.c
+        t=jnp.where(at==0,self.c,t^self.s)
+        t=jnp.where(at==n,r,jnp.where(at==n+1,self.s,jnp.where(at==n+2,r*self.S+self.s,t)))
+        return t.astype(jnp.int32)
 
 
 def tie(*xs):
@@ -736,9 +747,7 @@
     fr=down_weight.shape[0]
     own=time_table.shape[0]
     idx=g.index()
-    r=g.z*2+g.c
-    me=jnp.stack([r,g.s,r*S+g.s]).astype(jnp.int32)
-    small,ids=small_rows(me,time_steps,(ln1_gain,ln1_bias,q_bias,v_bias,o_bias,ln2_gain,ln2_bias,down_bias,up_bias))
+    small,ids=small_rows(idx,time_steps,(ln1_gain,ln1_bias,q_bias,v_bias,o_bias,ln2_gain,ln2_bias,down_bias,up_bias))
     small,segments,o_weight_,q_weight_=tie(small,segments,o_weight,q_weight)
     pack_a=pack(pack_a_kernel,idx,(q_weight_,k_weight,v_weight),"pack_a")
     mine_a=[g.direct(pack_a,j) for j in range(1,S)]
@@ -841,11 +850,9 @@
     back_a,pays=both[:g.Z-1],both[g.Z-1:]
     out_a=plane_join(g,mine,back_a)
     other_a=g.core(out_a)
-    vsum,gtab=table(me,pays,own)
-    vsum,other_a=tie(vsum,other_a)
+    *sums8,subs,gtab=table(idx,pays,own,w,up_bias.shape[0])
+    gtab,other_a=tie(gtab,other_a)
     gq,gk,gv=unpack(idx,out_a,other_a,((w,1),)*3)
-    sums8=lax.dynamic_slice_in_dim(vsum[:8],g.s*w,w,1)
-    subs=lax.dynamic_slice_in_dim(vsum[8:NV].reshape(FF),g.s*up_bias.shape[0],up_bias.shape[0],0)
     return (res.reshape(tokens.shape),gt.reshape(tokens.shape),gtab,sums8[0],sums8[1],gq,sums8[2],gk,gv,sums8[3],go,sums8[4],sums8[5],sums8[6],gup,subs,gdn,sums8[7])
 
 

time: 392 us -> 389 us (level)
  transfers between devices with their start and end apart: 48 -> 48, of which waited for: 12 -> 14; matrix products, arithmetic and copies ran while one was open for 4% -> 4% of each run, Pallas kernels for 47% -> 47%
where the time goes in v1:
time: 389 us; the launch traced here: 384 us
  Pallas kernels  276 us (71%)
  starting transfers between devices  50.3 us (13%)
  other arithmetic  25.9 us (7%)
  waiting for transfers between devices  19 us (5%)
  local copies, waits for them, and re-layouts  9.76 us (3%)
    pallas_call x1, Pallas kernels, mid(): pl.pallas_call(functools.partial(mid_kernel, tb=tb, fc=fc, ns=ns, wr=wr,...  89 us
    pallas_call x4, Pallas kernels, attn_bwd(): pl.pallas_call(functools.partial(bwd_kernel, f0=f0, ns=ns), grid_spec=plt...  76.9 us
    ppermute x48, starting transfers between devices, move(): return lax.ppermute(x, ('rep', 'shard'), pairs)  50.3 us
    pallas_call x3, Pallas kernels, attn_fwd(): pl.pallas_call(functools.partial(fwd_kernel, f0=f0, ns=ns), grid_spec=plt...  42.4 us
    ppermute x48, waiting for transfers between devices, move(): return lax.ppermute(x, ('rep', 'shard'), pairs)  19 us
    pallas_call x1, Pallas kernels, qkv(): pl.pallas_call(functools.partial(qkv_kernel, ns=ns, wr=wr), grid_spec=plt...  18.7 us
    pallas_call x1, Pallas kernels, dx(): pl.pallas_call(functools.partial(dx_kernel, per=per), grid=(T // tb,), in...  15.8 us
    pallas_call x1, Pallas kernels, dw(): pl.pallas_call(functools.partial(dw_kernel, ns=ns, wr=wr), grid_spec=pltp...  14.4 us
  transfers between devices with their start and end apart: 48, of which 14 were waited for; matrix products, arithmetic and copies ran while one was open for 4% of the time, Pallas kernels for 47%

profile of v1, /device:TPU:0, one launch (start us, length us, event | category | flops | bytes accessed | tf_op | source)
XLA Modules:
  0.0 384.2 jit_solution(13878933040786106851)
XLA Ops:
  0.7 1.3 compare_select_fusion.6.idx_ref
  1.9 1.5 small.1
  3.5 2.0 pack_a.1
  5.4 2.9 collective-permute-start.3
  8.4 1.5 collective-permute-start.4
  9.9 2.0 collective-permute-start.1
  11.9 1.5 collective-permute-start.2
  14.1 1.1 fusion.1.fk_ref
  15.2 5.6 %collective-permute-done = bf16[14,768]{1,0:T(8,128)(2,1)S(1)} collective-permute-done((bf16[14,768]{1,0:T(8,128)(2,1)}, bf16[14,768]{1,0:T(8,128)(2,1)S(1)}, u32[]{:S(2)}, u32[]{:S(2)}) %collective-permute-start) | collective-permute-done | bytes 21536 | tf_op jit(solution)/shard_map/ppermute | solution.py:667
  20.9 1.4 collective-permute-start.5
  23.1 1.4 convolution_convert_fusion
  24.9 1.8 collective-permute-start.7
  26.7 1.4 collective-permute-start.8
  28.1 1.1 select_convert_fusion.fq_ref
  29.2 2.9 pack_b.1
  33.8 1.5 collective-permute-start.12
  38.0 1.5 collective-permute-done.11.refs_11_
  39.4 18.7 %qkv.1 = (bf16[2048,768]{1,0:T(8,128)(2,1)}, bf16[2048,768]{1,0:T(8,128)(2,1)}, bf16[2048,768]{1,0:T(8,128)(2,1)}, bf16[768,2048]{1,0:T(8,128)(2,1)}, bf16[3,768,768]{2,1,0:T(8,128)(2,1)}) custom-call(s32[16]{0:T(128)} %compare_select_fusion.6.idx_ref, f32[2048,768]{1,0:T(8,128)} %bitcast.59, f32[2,1,768]{2,1,0:T(1,128)} %reshape.143.refs_1_.row_ref, ...), custom_call_target="tpu_custom_call" | custom-call | flops 724775744 | bytes 2103705 | tf_op jit(solution)/shard_map/qkv/pallas_call | solution.py:117
  58.2 11.3 %attn_fwd.3 = (bf16[2048,768]{1,0:T(8,128)(2,1)}, bf16[2048,768]{1,0:T(8,128)(2,1)}) custom-call(s32[26]{0:T(128)} %pad_add_fusion.s_ref, bf16[2048,768]{1,0:T(8,128)(2,1)} %get-tuple-element.154.q_ref, bf16[2048,768]{1,0:T(8,128)(2,1)} %get-tuple-element.155.k_ref, bf16[2048,768]{1,0:T(8,128)(2,1)} %get-tuple-element.156.v_ref, ...), custom_call_target="tpu_custom_call" | custom-call | flops 644245120 | bytes 550502 | tf_op jit(solution)/shard_map/attn_fwd/pallas_call | solution.py:238
  69.5 1.6 collective-permute-start.14
  71.6 19.8 %attn_fwd.4 = (bf16[2048,768]{1,0:T(8,128)(2,1)}, bf16[2048,768]{1,0:T(8,128)(2,1)}) custom-call(s32[26]{0:T(128)} %pad_add_fusion.s_ref, bf16[2048,768]{1,0:T(8,128)(2,1)} %get-tuple-element.154.q_ref, bf16[2048,768]{1,0:T(8,128)(2,1)} %get-tuple-element.155.k_ref, ...), custom_call_target="tpu_custom_call", output_to_operand_aliasing={{0}: (6, {}), {1}: (7, {})} | custom-call | flops 1288490240 | bytes 1101004 | tf_op jit(solution)/shard_map/attn_fwd/pallas_call | solution.py:238
  91.5 11.3 %attn_fwd.5 = (bf16[2048,768]{1,0:T(8,128)(2,1)}, bf16[2048,768]{1,0:T(8,128)(2,1)}) custom-call(s32[26]{0:T(128)} %pad_add_fusion.s_ref, bf16[2048,768]{1,0:T(8,128)(2,1)} %get-tuple-element.154.q_ref, bf16[2048,768]{1,0:T(8,128)(2,1)} %get-tuple-element.155.k_ref, ...), custom_call_target="tpu_custom_call", output_to_operand_aliasing={{0}: (6, {}), {1}: (7, {})} | custom-call | flops 644245120 | bytes 550502 | tf_op jit(solution)/shard_map/attn_fwd/pallas_call | solution.py:238
  102.8 89.0 %mid.1 = (f32[2048,768]{1,0:T(8,128)}, bf16[2048,768]{1,0:T(8,128)(2,1)}, bf16[2048,768]{1,0:T(8,128)(2,1)}, bf16[4,1728,384]{2,1,0:T(8,128)(2,1)}, bf16[4,1728,...) custom-call(s32[16]{0:T(128)} %compare_select_fusion.6.idx_ref, f32[2048,768]{1,0:T(8,128)} %bitcast.60, ...), custom_call_target="tpu_custom_call" | custom-call | flops 6522981376 | bytes 10223616 | tf_op jit(solution)/shard_map/mid/pallas_call | solution.py:439
  192.4 13.9 %attn_bwd.4.refs_0_ = bf16[3,2048,768]{2,1,0:T(8,128)(2,1)} custom-call(s32[26]{0:T(128)} %pad_add_fusion.s_ref, bf16[2048,768]{1,0:T(8,128)(2,1)} %get-tuple-element.154.q_ref, bf16[2048,768]{1,0:T(8,128)(2,1)} %get-tuple-element.155.k_ref, bf16[2048,768]{1,0:T(8,128)(2,1)} %get-tuple-element.156.v_ref, bf16[2048,768]{1,0:T(8,128)(2,1)} %get-tuple-element.173.fx_ref, ...), custom_call_target="tpu_custom_call" | custom-call | flops 1073741824 | bytes 524288 | tf_op jit(solution)/shard_map/attn_bwd/pallas_call | solution.py:321
  206.3 4.7 %add_convert_fusion = bf16[2,1728,384]{2,1,0:T(8,128)(2,1)} fusion(bf16[4,1728,384]{2,1,0:T(8,128)(2,1)} %collective-permute-done.18, bf16[4,1728,384]{2,1,0:T(8,128)(2,1)} %get-tuple-element.177), kind=kLoop, calls=%fused_computation | loop fusion | flops 5308416 | bytes 7962624 | tf_op jit(solution)/shard_map/convert_element_type | solution.py:711
  211.6 30.0 %attn_bwd.5.refs_0_ = bf16[3,2048,768]{2,1,0:T(8,128)(2,1)} custom-call(s32[26]{0:T(128)} %pad_add_fusion.s_ref, bf16[2048,768]{1,0:T(8,128)(2,1)} %get-tuple-element.154.q_ref, bf16[2048,768]{1,0:T(8,128)(2,1)} %get-tuple-element.155.k_ref, bf16[2048,768]{1,0:T(8,128)(2,1)} %get-tuple-element.156.v_ref, ...), custom_call_target="tpu_custom_call", output_to_operand_aliasing={{}: (8, {})} | custom-call | flops 2684354560 | bytes 1310720 | tf_op jit(solution)/shard_map/attn_bwd/pallas_call | solution.py:321
  241.5 1.7 collective-permute-done.19
  243.2 4.2 %add_convert_fusion.2 = bf16[1,1728,384]{2,1,0:T(8,128)(2,1)} fusion(bf16[2,1728,384]{2,1,0:T(8,128)(2,1)S(1)} %collective-permute-done.19, bf16[4,1728,384]{2,1,0:T(8,128)(2,1)} %collective-permute-done.18, bf16[4,1728,384]{2,1,0:T(8,128)(2,1)} %get-tuple-element.177), kind=kLoop, calls=%fused_computation.2 | loop fusion | flops 3981312 | bytes 5308416 | tf_op jit(solution)/shard_map/convert_element_type | solution.py:711
  248.1 19.3 %attn_bwd.6.refs_0_ = bf16[3,2048,768]{2,1,0:T(8,128)(2,1)} custom-call(s32[26]{0:T(128)} %pad_add_fusion.s_ref, bf16[2048,768]{1,0:T(8,128)(2,1)} %get-tuple-element.154.q_ref, bf16[2048,768]{1,0:T(8,128)(2,1)} %get-tuple-element.155.k_ref, bf16[2048,768]{1,0:T(8,128)(2,1)} %get-tuple-element.156.v_ref, ...), custom_call_target="tpu_custom_call", output_to_operand_aliasing={{}: (8, {})} | custom-call | flops 1610612736 | bytes 786432 | tf_op jit(solution)/shard_map/attn_bwd/pallas_call | solution.py:321
  267.4 3.2 add_convert_fusion.1
  270.7 1.9 collective-permute-start.21
  272.6 2.8 collective-permute-start.22
  275.3 13.7 %attn_bwd.7.d_ref = bf16[3,2048,768]{2,1,0:T(8,128)(2,1)} custom-call(s32[26]{0:T(128)} %pad_add_fusion.s_ref, bf16[2048,768]{1,0:T(8,128)(2,1)} %get-tuple-element.154.q_ref, bf16[2048,768]{1,0:T(8,128)(2,1)} %get-tuple-element.155.k_ref, bf16[2048,768]{1,0:T(8,128)(2,1)} %get-tuple-element.156.v_ref, ...), custom_call_target="tpu_custom_call", output_to_operand_aliasing={{}: (8, {})} | custom-call | flops 1073741824 | bytes 524288 | tf_op jit(solution)/shard_map/attn_bwd/pallas_call | solution.py:321
  289.0 14.4 %dw.1 = (bf16[4,576,384]{2,1,0:T(8,128)(2,1)}, bf16[4,576,384]{2,1,0:T(8,128)(2,1)}, f32[16,768]{1,0:T(8,128)}) custom-call(s32[16]{0:T(128)} %compare_select_fusion.6.idx_ref, bf16[768,2048]{1,0:T(8,128)(2,1)} %get-tuple-element.190.nt_ref, bf16[3,2048,768]{2,1,0:T(8,128)(2,1)} %attn_bwd.7.d_ref), custom_call_target="tpu_custom_call" | custom-call | flops 724775744 | bytes 1966080 | tf_op jit(solution)/shard_map/dw/pallas_call | solution.py:482
  304.3 2.0 fusion.4
  306.2 1.9 collective-permute-done.24
  308.2 2.9 add_convert_fusion.3
  311.1 1.4 collective-permute-start.28
  313.1 3.8 collective-permute-start.26
  317.0 1.0 bitcast_dynamic-update-slice_fusion.3
  318.1 15.8 %dx.1 = (f32[2048,768]{1,0:T(8,128)}, f32[16,768]{1,0:T(8,128)}, f32[2,8,768]{2,1,0:T(8,128)}) custom-call(f32[2048,768]{1,0:T(8,128)} %bitcast.61, f32[2,1,768]{2,1,0:T(1,128)} %reshape.143.refs_1_.row_ref, bf16[3,2048,768]{2,1,0:T(8,128)(2,1)} %attn_bwd.7.d_ref, bf16[2048,768]{1,0:T(8,128)(2,1)} %get-tuple-element.203.gm_ref, ...), custom_call_target="tpu_custom_call" | custom-call | flops 724775744 | bytes 2870476 | tf_op jit(solution)/shard_map/dx/pallas_call | solution.py:519
  333.9 1.3 add_convert_fusion.5
  335.9 1.0 bitcast_dynamic-update-slice_fusion.2
  336.9 1.7 sums.1.refs_0_
  338.6 1.4 collective-permute-start.31
  340.2 1.0 bitcast_dynamic-update-slice_fusion.1
  341.2 1.4 collective-permute-start.29
  343.2 1.2 collective-permute-done.31.refs_3_
  345.0 1.5 add_convert_fusion.4
  347.3 3.8 collective-permute-start.34
  351.1 1.0 bitcast_dynamic-update-slice_fusion
  352.2 1.6 group.1.refs_0_
  353.7 2.1 collective-permute-done.34
  355.8 1.9 collective-permute-done.35
  360.3 2.0 collective-permute-start.43
  362.3 1.1 collective-permute-start.44
  363.4 1.0 collective-permute-start.37
  364.4 1.3 collective-permute-start.38
  366.5 1.2 collective-permute-start.39
  368.0 2.4 collective-permute-start.45
  372.2 4.5 %unpack.2 = (f32[192,768]{1,0:T(8,128)}, f32[192,3072]{1,0:T(8,128)}, f32[768,768]{1,0:T(8,128)}) custom-call(s32[16]{0:T(128)} %compare_select_fusion.6.idx_ref, bf16[1728,384]{1,0:T(8,128)(2,1)} %bitcast.66, bf16[1728,384]{1,0:T(8,128)(2,1)} %copy-done.5), custom_call_target="tpu_custom_call" | custom-call | bytes 796262 | tf_op jit(solution)/shard_map/unpack/pallas_call | solution.py:614
  376.7 1.1 collective-permute-done.38
  378.0 2.5 table.1
  381.3 2.5 unpack.3
  (139 shorter events, 19.4 us)
Async XLA Ops:
  5.4 21.2 %collective-permute-start.3 = (bf16[576,384]{1,0:T(8,128)(2,1)}, bf16[576,384]{1,0:T(8,128)(2,1)S(1)}, u32[]{:S(2)}, u32[]{:S(2)}) collective-permute-start(bf16[576,384]{1,0:T(8,128)(2,1)} %pack_a.1), channel_id=1, source_target_pairs={{0,1},{1,0},{2,3},{3,2},{4,5},{5,4},{6,7},{7,6},{8,9},{9,8},{10,11... | collective-permute-start | bytes 1327112 | tf_op jit(solution)/shard_map/ppermute | solution.py:667
  8.4 23.8 %collective-permute-start.4 = (bf16[576,384]{1,0:T(8,128)(2,1)}, bf16[576,384]{1,0:T(8,128)(2,1)S(1)}, u32[]{:S(2)}, u32[]{:S(2)}) collective-permute-start(bf16[576,384]{1,0:T(8,128)(2,1)} %pack_a.1), channel_id=1, source_target_pairs={{0,2},{1,3},{2,0},{3,1},{4,6},{5,7},{6,4},{7,5},{8,10},{9,11},{10,... | collective-permute-start | bytes 1327112 | tf_op jit(solution)/shard_map/ppermute | solution.py:667
  9.9 11.0 %collective-permute-start = (bf16[14,768]{1,0:T(8,128)(2,1)}, bf16[14,768]{1,0:T(8,128)(2,1)S(1)}, u32[]{:S(2)}, u32[]{:S(2)}) collective-permute-start(bf16[14,768]{1,0:T(8,128)(2,1)} %get-tuple-element.145), channel_id=1, source_target_pairs={{0,3},{1,2},{2,1},{3,0},{4,7},{5,6},{6,5},{7,4},{8,11},{9,10},{10,... | collective-permute-start | bytes 64520 | tf_op jit(solution)/shard_map/ppermute | solution.py:667
  9.9 12.4 %collective-permute-start.1 = (bf16[14,768]{1,0:T(8,128)(2,1)}, bf16[14,768]{1,0:T(8,128)(2,1)S(1)}, u32[]{:S(2)}, u32[]{:S(2)}) collective-permute-start(bf16[14,768]{1,0:T(8,128)(2,1)} %get-tuple-element.145), channel_id=1, source_target_pairs={{0,2},{1,3},{2,0},{3,1},{4,6},{5,7},{6,4},{7,5},{8,10},{9,11},{10,... | collective-permute-start | bytes 64520 | tf_op jit(solution)/shard_map/ppermute | solution.py:667
  11.9 10.4 %collective-permute-start.2 = (bf16[14,768]{1,0:T(8,128)(2,1)}, bf16[14,768]{1,0:T(8,128)(2,1)S(1)}, u32[]{:S(2)}, u32[]{:S(2)}) collective-permute-start(bf16[14,768]{1,0:T(8,128)(2,1)} %get-tuple-element.145), channel_id=1, source_target_pairs={{0,1},{1,0},{2,3},{3,2},{4,5},{5,4},{6,7},{7,6},{8,9},{9,8},{10,11... | collective-permute-start | bytes 64520 | tf_op jit(solution)/shard_map/ppermute | solution.py:667
  20.9 11.6 %collective-permute-start.5 = (bf16[576,384]{1,0:T(8,128)(2,1)}, bf16[576,384]{1,0:T(8,128)(2,1)S(1)}, u32[]{:S(2)}, u32[]{:S(2)}) collective-permute-start(bf16[576,384]{1,0:T(8,128)(2,1)} %pack_a.1), channel_id=1, source_target_pairs={{0,3},{1,2},{2,1},{3,0},{4,7},{5,6},{6,5},{7,4},{8,11},{9,10},{10,... | collective-permute-start | bytes 1327112 | tf_op jit(solution)/shard_map/ppermute | solution.py:667
  23.1 9.1 %copy-start.8 = (f32[14,768]{1,0:T(8,128)}, f32[14,768]{1,0:T(8,128)S(1)}, u32[]{:S(2)}) copy-start(f32[14,768]{1,0:T(8,128)S(1)} %convert_add_fusion.2.refs_2_.refs_4_.vec_ref) | copy-start | bytes 129028
  23.1 12.7 %copy-start.19 = (s32[2,1024]{1,0:T(2,128)S(1)}, s32[2,1024]{1,0:T(2,128)}, u32[]{:S(2)}) copy-start(s32[2,1024]{1,0:T(2,128)} %param.24) | copy-start | bytes 24580
  23.1 13.8 %copy-start.23 = (s32[24]{0:T(128)S(1)}, s32[24]{0:T(128)}, u32[]{:S(2)}) copy-start(s32[24]{0:T(128)} %constant.141.clone) | copy-start | bytes 292
  24.5 7.9 %collective-permute-start.6 = (bf16[2,768]{1,0:T(2,128)(2,1)S(1)}, bf16[2,768]{1,0:T(2,128)(2,1)S(1)}, u32[]{:S(2)}, u32[]{:S(2)}) collective-permute-start(bf16[2,768]{1,0:T(2,128)(2,1)S(1)} %get-tuple-element.271), channel_id=1, source_target_pairs={{0,1},{1,0},{2,3},{3,2},{4,5},{5,4},{6,7},{7,6},{8,9},{9,8},{10,11... | collective-permute-start | bytes 9224 | tf_op jit(solution)/shard_map/ppermute | solution.py:667
  24.9 7.6 %collective-permute-start.7 = (bf16[2,768]{1,0:T(2,128)(2,1)S(1)}, bf16[2,768]{1,0:T(2,128)(2,1)S(1)}, u32[]{:S(2)}, u32[]{:S(2)}) collective-permute-start(bf16[2,768]{1,0:T(2,128)(2,1)S(1)} %get-tuple-element.270), channel_id=1, source_target_pairs={{0,2},{1,3},{2,0},{3,1},{4,6},{5,7},{6,4},{7,5},{8,10},{9,11},{10,... | collective-permute-start | bytes 9224 | tf_op jit(solution)/shard_map/ppermute | solution.py:667
  26.7 12.8 %copy-start.10 = (bf16[576,384]{1,0:T(8,128)(2,1)}, bf16[576,384]{1,0:T(8,128)(2,1)S(1)}, u32[]{:S(2)}) copy-start(bf16[576,384]{1,0:T(8,128)(2,1)S(1)} %collective-permute-done.3.refs_6_) | copy-start | bytes 1327108
  26.7 5.8 %collective-permute-start.8 = (bf16[2,768]{1,0:T(2,128)(2,1)S(1)}, bf16[2,768]{1,0:T(2,128)(2,1)S(1)}, u32[]{:S(2)}, u32[]{:S(2)}) collective-permute-start(bf16[2,768]{1,0:T(2,128)(2,1)S(1)} %get-tuple-element.269), channel_id=1, source_target_pairs={{0,3},{1,2},{2,1},{3,0},{4,7},{5,6},{6,5},{7,4},{8,11},{9,10},{10,... | collective-permute-start | bytes 9224 | tf_op jit(solution)/shard_map/ppermute | solution.py:667
  32.2 7.3 %copy-start.11 = (bf16[576,384]{1,0:T(8,128)(2,1)}, bf16[576,384]{1,0:T(8,128)(2,1)S(1)}, u32[]{:S(2)}) copy-start(bf16[576,384]{1,0:T(8,128)(2,1)S(1)} %collective-permute-done.4.refs_7_) | copy-start | bytes 1327108
  33.8 35.7 %collective-permute-start.12 = (bf16[1728,384]{1,0:T(8,128)(2,1)}, bf16[1728,384]{1,0:T(8,128)(2,1)S(1)}, u32[]{:S(2)}, u32[]{:S(2)}) collective-permute-start(bf16[1728,384]{1,0:T(8,128)(2,1)} %pack_b.1), channel_id=1, source_target_pairs={{0,1},{1,0},{2,3},{3,2},{4,6},{5,7},{6,4},{7,5},{8,9},{9,8},{10,11... | collective-permute-start | bytes 3981320 | tf_op jit(solution)/shard_map/ppermute | solution.py:667
  35.3 34.2 %collective-permute-start.13 = (bf16[1728,384]{1,0:T(8,128)(2,1)}, bf16[1728,384]{1,0:T(8,128)(2,1)S(1)}, u32[]{:S(2)}, u32[]{:S(2)}) collective-permute-start(bf16[1728,384]{1,0:T(8,128)(2,1)} %pack_b.1), channel_id=1, source_target_pairs={{0,2},{1,3},{2,0},{3,1},{4,5},{5,4},{6,7},{7,6},{8,10},{9,11},{10,... | collective-permute-start | bytes 3981320 | tf_op jit(solution)/shard_map/ppermute | solution.py:667
  36.0 2.0 collective-permute-start.10
  36.0 3.4 collective-permute-start.11
  36.5 2.9 collective-permute-start.9
  69.5 21.9 %copy-start.6 = (bf16[1728,384]{1,0:T(8,128)(2,1)}, bf16[1728,384]{1,0:T(8,128)(2,1)S(1)}, u32[]{:S(2)}) copy-start(bf16[1728,384]{1,0:T(8,128)(2,1)S(1)} %collective-permute-done.12.refs_8_) | copy-start | bytes 3981316
  69.5 21.9 %copy-start.7 = (bf16[1728,384]{1,0:T(8,128)(2,1)}, bf16[1728,384]{1,0:T(8,128)(2,1)S(1)}, u32[]{:S(2)}) copy-start(bf16[1728,384]{1,0:T(8,128)(2,1)S(1)} %collective-permute-done.13.refs_9_) | copy-start | bytes 3981316
  69.5 21.9 %collective-permute-start.14 = (bf16[1728,384]{1,0:T(8,128)(2,1)S(1)}, bf16[1728,384]{1,0:T(8,128)(2,1)}, u32[]{:S(2)}, u32[]{:S(2)}) collective-permute-start(bf16[1728,384]{1,0:T(8,128)(2,1)S(1)} %collective-permute-done.12.refs_8_), channel_id=1, source_target_pairs={{0,2},{1,3},{2,0},{3,1},{4,5},{5,4},{6,7},{7,6},{8,10},{9,11},{10,... | collective-permute-start | bytes 3981320 | tf_op jit(solution)/shard_map/ppermute | solution.py:667
  71.1 31.7 %collective-permute-start.15 = (bf16[1728,384]{1,0:T(8,128)(2,1)S(1)}, bf16[1728,384]{1,0:T(8,128)(2,1)}, u32[]{:S(2)}, u32[]{:S(2)}) collective-permute-start(bf16[1728,384]{1,0:T(8,128)(2,1)S(1)} %collective-permute-done.12.refs_8_), channel_id=1, source_target_pairs={{0,4},{1,5},{2,6},{3,7},{4,0},{5,1},{6,2},{7,3},{8,12},{9,13},{10,... | collective-permute-start | bytes 3981320 | tf_op jit(solution)/shard_map/ppermute | solution.py:667
  71.1 31.7 %collective-permute-start.16 = (bf16[1728,384]{1,0:T(8,128)(2,1)S(1)}, bf16[1728,384]{1,0:T(8,128)(2,1)}, u32[]{:S(2)}, u32[]{:S(2)}) collective-permute-start(bf16[1728,384]{1,0:T(8,128)(2,1)S(1)} %collective-permute-done.13.refs_9_), channel_id=1, source_target_pairs={{0,4},{1,5},{2,6},{3,7},{4,0},{5,1},{6,2},{7,3},{8,12},{9,13},{10,... | collective-permute-start | bytes 3981320 | tf_op jit(solution)/shard_map/ppermute | solution.py:667
  91.4 11.4 %collective-permute-start.17 = (bf16[1728,384]{1,0:T(8,128)(2,1)}, bf16[1728,384]{1,0:T(8,128)(2,1)}, u32[]{:S(2)}, u32[]{:S(2)}) collective-permute-start(bf16[1728,384]{1,0:T(8,128)(2,1)} %collective-permute-done.14.refs_10_), channel_id=1, source_target_pairs={{0,4},{1,5},{2,6},{3,7},{4,0},{5,1},{6,2},{7,3},{8,12},{9,13},{10,... | collective-permute-start | bytes 3981320 | tf_op jit(solution)/shard_map/ppermute | solution.py:667
  191.8 14.5 %collective-permute-start.18 = (bf16[4,1728,384]{2,1,0:T(8,128)(2,1)}, bf16[4,1728,384]{2,1,0:T(8,128)(2,1)}, u32[]{:S(2)}, u32[]{:S(2)}) collective-permute-start(bf16[4,1728,384]{2,1,0:T(8,128)(2,1)} %get-tuple-element.175), channel_id=1, source_target_pairs={{0,4},{1,5},{2,6},{3,7},{4,0},{5,1},{6,2},{7,3},{8,12},{9,13},{10,... | collective-permute-start | bytes 15925256 | tf_op jit(solution)/shard_map/ppermute | solution.py:667
  211.0 32.2 %collective-permute-start.19 = (bf16[2,1728,384]{2,1,0:T(8,128)(2,1)}, bf16[2,1728,384]{2,1,0:T(8,128)(2,1)S(1)}, u32[]{:S(2)}, u32[]{:S(2)}) collective-permute-start(bf16[2,1728,384]{2,1,0:T(8,128)(2,1)} %add_convert_fusion), channel_id=1, source_target_pairs={{0,2},{1,3},{2,0},{3,1},{4,5},{5,4},{6,7},{7,6},{8,10},{9,11},{10,... | collective-permute-start | bytes 7962632 | tf_op jit(solution)/shard_map/ppermute | solution.py:667
  243.2 4.9 %copy-start.1 = (bf16[2,1728,384]{2,1,0:T(8,128)(2,1)}, bf16[2,1728,384]{2,1,0:T(8,128)(2,1)S(1)}, u32[]{:S(2)}) copy-start(bf16[2,1728,384]{2,1,0:T(8,128)(2,1)S(1)} %collective-permute-done.19) | copy-start | bytes 7962628
  247.5 19.9 %collective-permute-start.20 = (bf16[1,1728,384]{2,1,0:T(8,128)(2,1)}, bf16[1,1728,384]{2,1,0:T(8,128)(2,1)}, u32[]{:S(2)}, u32[]{:S(2)}) collective-permute-start(bf16[1,1728,384]{2,1,0:T(8,128)(2,1)} %add_convert_fusion.2), channel_id=1, source_target_pairs={{0,1},{1,0},{2,3},{3,2},{4,6},{5,7},{6,4},{7,5},{8,9},{9,8},{10,11... | collective-permute-start | bytes 3981320 | tf_op jit(solution)/shard_map/ppermute | solution.py:667
  270.7 32.7 %collective-permute-start.21 = (bf16[432,384]{1,0:T(8,128)(2,1)S(1)}, bf16[432,384]{1,0:T(8,128)(2,1)S(1)}, u32[]{:S(2)}, u32[]{:S(2)}) collective-permute-start(bf16[432,384]{1,0:T(8,128)(2,1)S(1)} %get-tuple-element.193), channel_id=1, source_target_pairs={{0,8},{1,9},{2,10},{3,11},{4,12},{5,13},{6,14},{7,15},{8,0},{9,1},... | collective-permute-start | bytes 995336 | tf_op jit(solution)/shard_map/ppermute | solution.py:667
  272.6 30.9 %collective-permute-start.22 = (bf16[432,384]{1,0:T(8,128)(2,1)S(1)}, bf16[432,384]{1,0:T(8,128)(2,1)S(1)}, u32[]{:S(2)}, u32[]{:S(2)}) collective-permute-start(bf16[432,384]{1,0:T(8,128)(2,1)S(1)} %get-tuple-element.194), channel_id=1, source_target_pairs={{0,16},{1,17},{2,18},{3,19},{4,20},{5,21},{6,22},{7,23},{8,24},{9,... | collective-permute-start | bytes 995336 | tf_op jit(solution)/shard_map/ppermute | solution.py:667
  275.3 28.1 %collective-permute-start.23 = (bf16[432,384]{1,0:T(8,128)(2,1)S(1)}, bf16[432,384]{1,0:T(8,128)(2,1)S(1)}, u32[]{:S(2)}, u32[]{:S(2)}) collective-permute-start(bf16[432,384]{1,0:T(8,128)(2,1)S(1)} %get-tuple-element.195), channel_id=1, source_target_pairs={{0,24},{1,25},{2,26},{3,27},{4,28},{5,29},{6,30},{7,31},{8,16},{9,... | collective-permute-start | bytes 995336 | tf_op jit(solution)/shard_map/ppermute | solution.py:667
  304.3 3.9 %collective-permute-start.24 = (bf16[4,576,384]{2,1,0:T(8,128)(2,1)}, bf16[4,576,384]{2,1,0:T(8,128)(2,1)S(1)}, u32[]{:S(2)}, u32[]{:S(2)}) collective-permute-start(bf16[4,576,384]{2,1,0:T(8,128)(2,1)} %get-tuple-element.199), channel_id=1, source_target_pairs={{0,4},{1,5},{2,6},{3,7},{4,0},{5,1},{6,2},{7,3},{8,12},{9,13},{10,... | collective-permute-start | bytes 5308424 | tf_op jit(solution)/shard_map/ppermute | solution.py:667
  308.2 9.9 %copy-start.4 = (bf16[4,576,384]{2,1,0:T(8,128)(2,1)}, bf16[4,576,384]{2,1,0:T(8,128)(2,1)S(1)}, u32[]{:S(2)}) copy-start(bf16[4,576,384]{2,1,0:T(8,128)(2,1)S(1)} %collective-permute-done.24) | copy-start | bytes 5308420
  311.1 22.8 %collective-permute-start.28 = (bf16[2,576,384]{2,1,0:T(8,128)(2,1)}, bf16[2,576,384]{2,1,0:T(8,128)(2,1)}, u32[]{:S(2)}, u32[]{:S(2)}) collective-permute-start(bf16[2,576,384]{2,1,0:T(8,128)(2,1)} %add_convert_fusion.3), channel_id=1, source_target_pairs={{0,2},{1,3},{2,0},{3,1},{4,5},{5,4},{6,7},{7,6},{8,10},{9,11},{10,... | collective-permute-start | bytes 2654216 | tf_op jit(solution)/shard_map/ppermute | solution.py:667
  312.4 23.5 %collective-permute-start.25 = (bf16[432,384]{1,0:T(8,128)(2,1)}, bf16[432,384]{1,0:T(8,128)(2,1)}, u32[]{:S(2)}, u32[]{:S(2)}) collective-permute-start(bf16[432,384]{1,0:T(8,128)(2,1)} %fusion.4), channel_id=1, source_target_pairs={{0,8},{1,9},{2,10},{3,11},{4,12},{5,13},{6,14},{7,15},{8,0},{9,1},... | collective-permute-start | bytes 995336 | tf_op jit(solution)/shard_map/ppermute | solution.py:667
  313.1 27.0 %collective-permute-start.26 = (bf16[432,384]{1,0:T(8,128)(2,1)}, bf16[432,384]{1,0:T(8,128)(2,1)}, u32[]{:S(2)}, u32[]{:S(2)}) collective-permute-start(bf16[432,384]{1,0:T(8,128)(2,1)} %fusion.4), channel_id=1, source_target_pairs={{0,16},{1,17},{2,18},{3,19},{4,20},{5,21},{6,22},{7,23},{8,24},{9,... | collective-permute-start | bytes 995336 | tf_op jit(solution)/shard_map/ppermute | solution.py:667
  316.9 34.2 %collective-permute-start.27 = (bf16[432,384]{1,0:T(8,128)(2,1)}, bf16[432,384]{1,0:T(8,128)(2,1)}, u32[]{:S(2)}, u32[]{:S(2)}) collective-permute-start(bf16[432,384]{1,0:T(8,128)(2,1)} %fusion.4), channel_id=1, source_target_pairs={{0,24},{1,25},{2,26},{3,27},{4,28},{5,29},{6,30},{7,31},{8,16},{9,... | collective-permute-start | bytes 995336 | tf_op jit(solution)/shard_map/ppermute | solution.py:667
  318.1 15.8 %copy-start.3 = (bf16[4,576,384]{2,1,0:T(8,128)(2,1)S(1)}, bf16[4,576,384]{2,1,0:T(8,128)(2,1)}, u32[]{:S(2)}) copy-start(bf16[4,576,384]{2,1,0:T(8,128)(2,1)} %get-tuple-element.201) | copy-start | bytes 5308420
  335.2 9.9 %collective-permute-start.32 = (bf16[1,576,384]{2,1,0:T(8,128)(2,1)S(1)}, bf16[1,576,384]{2,1,0:T(8,128)(2,1)}, u32[]{:S(2)}, u32[]{:S(2)}) collective-permute-start(bf16[1,576,384]{2,1,0:T(8,128)(2,1)S(1)} %add_convert_fusion.5), channel_id=1, source_target_pairs={{0,1},{1,0},{2,3},{3,2},{4,6},{5,7},{6,4},{7,5},{8,9},{9,8},{10,11... | collective-permute-start | bytes 1327112 | tf_op jit(solution)/shard_map/ppermute | solution.py:667
  338.6 5.8 %collective-permute-start.31 = (bf16[16,768]{1,0:T(8,128)(2,1)}, bf16[16,768]{1,0:T(8,128)(2,1)S(1)}, u32[]{:S(2)}, u32[]{:S(2)}) collective-permute-start(bf16[16,768]{1,0:T(8,128)(2,1)} %sums.1.refs_0_), channel_id=1, source_target_pairs={{0,3},{1,2},{2,1},{3,0},{4,7},{5,6},{6,5},{7,4},{8,11},{9,10},{10,... | collective-permute-start | bytes 73736 | tf_op jit(solution)/shard_map/ppermute | solution.py:667
  341.2 5.4 %collective-permute-start.29 = (bf16[16,768]{1,0:T(8,128)(2,1)}, bf16[16,768]{1,0:T(8,128)(2,1)S(1)}, u32[]{:S(2)}, u32[]{:S(2)}) collective-permute-start(bf16[16,768]{1,0:T(8,128)(2,1)} %sums.1.refs_0_), channel_id=1, source_target_pairs={{0,1},{1,0},{2,3},{3,2},{4,5},{5,4},{6,7},{7,6},{8,9},{9,8},{10,11... | collective-permute-start | bytes 73736 | tf_op jit(solution)/shard_map/ppermute | solution.py:667
  342.6 4.0 %collective-permute-start.30 = (bf16[16,768]{1,0:T(8,128)(2,1)}, bf16[16,768]{1,0:T(8,128)(2,1)S(1)}, u32[]{:S(2)}, u32[]{:S(2)}) collective-permute-start(bf16[16,768]{1,0:T(8,128)(2,1)} %sums.1.refs_0_), channel_id=1, source_target_pairs={{0,2},{1,3},{2,0},{3,1},{4,6},{5,7},{6,4},{7,5},{8,10},{9,11},{10,... | collective-permute-start | bytes 73736 | tf_op jit(solution)/shard_map/ppermute | solution.py:667
  346.6 4.5 %copy-start.21 = (bf16[16,768]{1,0:T(8,128)(2,1)}, bf16[16,768]{1,0:T(8,128)(2,1)S(1)}, u32[]{:S(2)}) copy-start(bf16[16,768]{1,0:T(8,128)(2,1)S(1)} %collective-permute-done.29.refs_1_) | copy-start | bytes 73732
  346.7 4.4 %copy-start.22 = (bf16[16,768]{1,0:T(8,128)(2,1)}, bf16[16,768]{1,0:T(8,128)(2,1)S(1)}, u32[]{:S(2)}) copy-start(bf16[16,768]{1,0:T(8,128)(2,1)S(1)} %collective-permute-done.30.refs_2_) | copy-start | bytes 73732
  346.7 7.1 %collective-permute-start.33 = (bf16[144,384]{1,0:T(8,128)(2,1)S(1)}, bf16[144,384]{1,0:T(8,128)(2,1)S(1)}, u32[]{:S(2)}, u32[]{:S(2)}) collective-permute-start(bf16[144,384]{1,0:T(8,128)(2,1)S(1)} %get-tuple-element.224), channel_id=1, source_target_pairs={{0,8},{1,9},{2,10},{3,11},{4,12},{5,13},{6,14},{7,15},{8,0},{9,1},... | collective-permute-start | bytes 331784 | tf_op jit(solution)/shard_map/ppermute | solution.py:667
  347.3 8.6 %collective-permute-start.34 = (bf16[144,384]{1,0:T(8,128)(2,1)S(1)}, bf16[144,384]{1,0:T(8,128)(2,1)S(1)}, u32[]{:S(2)}, u32[]{:S(2)}) collective-permute-start(bf16[144,384]{1,0:T(8,128)(2,1)S(1)} %get-tuple-element.266), channel_id=1, source_target_pairs={{0,16},{1,17},{2,18},{3,19},{4,20},{5,21},{6,22},{7,23},{8,24},{9,... | collective-permute-start | bytes 331784 | tf_op jit(solution)/shard_map/ppermute | solution.py:667
  351.1 6.7 %collective-permute-start.35 = (bf16[144,384]{1,0:T(8,128)(2,1)S(1)}, bf16[144,384]{1,0:T(8,128)(2,1)S(1)}, u32[]{:S(2)}, u32[]{:S(2)}) collective-permute-start(bf16[144,384]{1,0:T(8,128)(2,1)S(1)} %get-tuple-element.265), channel_id=1, source_target_pairs={{0,24},{1,25},{2,26},{3,27},{4,28},{5,29},{6,30},{7,31},{8,16},{9,... | collective-permute-start | bytes 331784 | tf_op jit(solution)/shard_map/ppermute | solution.py:667
  352.1 20.0 %copy-start = (bf16[4,432,384]{2,1,0:T(8,128)(2,1)}, bf16[4,432,384]{2,1,0:T(8,128)(2,1)S(1)}, u32[]{:S(2)}) copy-start(bf16[4,432,384]{2,1,0:T(8,128)(2,1)S(1)} %bitcast_dynamic-update-slice_fusion) | copy-start | bytes 3981316
  357.7 12.6 %collective-permute-start.36 = (bf16[1728,384]{1,0:T(8,128)(2,1)S(1)}, bf16[1728,384]{1,0:T(8,128)(2,1)S(1)}, u32[]{:S(2)}, u32[]{:S(2)}) collective-permute-start(bf16[1728,384]{1,0:T(8,128)(2,1)S(1)} %bitcast.65), channel_id=1, source_target_pairs={{0,4},{1,5},{2,6},{3,7},{4,0},{5,1},{6,2},{7,3},{8,12},{9,13},{10,... | collective-permute-start | bytes 3981320 | tf_op jit(solution)/shard_map/ppermute | solution.py:667
  358.5 3.8 collective-permute-start.40
  359.0 4.4 %collective-permute-start.41 = (bf16[22,768]{1,0:T(8,128)(2,1)}, bf16[22,768]{1,0:T(8,128)(2,1)S(1)}, u32[]{:S(2)}, u32[]{:S(2)}) collective-permute-start(bf16[22,768]{1,0:T(8,128)(2,1)} %group.1.refs_0_), channel_id=1, source_target_pairs={{0,8},{1,9},{2,10},{3,11},{4,12},{5,13},{6,14},{7,15},{8,0},{9,1},... | collective-permute-start | bytes 101384 | tf_op jit(solution)/shard_map/ppermute | solution.py:667
  360.0 4.4 %collective-permute-start.42 = (bf16[22,768]{1,0:T(8,128)(2,1)}, bf16[22,768]{1,0:T(8,128)(2,1)S(1)}, u32[]{:S(2)}, u32[]{:S(2)}) collective-permute-start(bf16[22,768]{1,0:T(8,128)(2,1)} %group.1.refs_0_), channel_id=1, source_target_pairs={{0,12},{1,13},{2,14},{3,15},{4,8},{5,9},{6,10},{7,11},{8,4},{9,5},... | collective-permute-start | bytes 101384 | tf_op jit(solution)/shard_map/ppermute | solution.py:667
  360.3 6.2 %collective-permute-start.43 = (bf16[22,768]{1,0:T(8,128)(2,1)}, bf16[22,768]{1,0:T(8,128)(2,1)}, u32[]{:S(2)}, u32[]{:S(2)}) collective-permute-start(bf16[22,768]{1,0:T(8,128)(2,1)} %group.1.refs_0_), channel_id=1, source_target_pairs={{0,16},{1,17},{2,18},{3,19},{4,20},{5,21},{6,22},{7,23},{8,24},{9,... | collective-permute-start | bytes 101384 | tf_op jit(solution)/shard_map/ppermute | solution.py:667
  362.3 15.7 %copy-start.15 = (bf16[22,768]{1,0:T(8,128)(2,1)}, bf16[22,768]{1,0:T(8,128)(2,1)S(1)}, u32[]{:S(2)}) copy-start(bf16[22,768]{1,0:T(8,128)(2,1)S(1)} %collective-permute-done.40.refs_1_) | copy-start | bytes 101380
  362.3 5.7 %collective-permute-start.44 = (bf16[22,768]{1,0:T(8,128)(2,1)}, bf16[22,768]{1,0:T(8,128)(2,1)S(1)}, u32[]{:S(2)}, u32[]{:S(2)}) collective-permute-start(bf16[22,768]{1,0:T(8,128)(2,1)} %group.1.refs_0_), channel_id=1, source_target_pairs={{0,20},{1,21},{2,22},{3,23},{4,16},{5,17},{6,18},{7,19},{8,28},{9,... | collective-permute-start | bytes 101384 | tf_op jit(solution)/shard_map/ppermute | solution.py:667
  363.4 14.6 %copy-start.16 = (bf16[22,768]{1,0:T(8,128)(2,1)}, bf16[22,768]{1,0:T(8,128)(2,1)S(1)}, u32[]{:S(2)}) copy-start(bf16[22,768]{1,0:T(8,128)(2,1)S(1)} %collective-permute-done.41.refs_2_) | copy-start | bytes 101380
  363.4 13.3 %collective-permute-start.37 = (bf16[144,384]{1,0:T(8,128)(2,1)}, bf16[144,384]{1,0:T(8,128)(2,1)S(1)}, u32[]{:S(2)}, u32[]{:S(2)}) collective-permute-start(bf16[144,384]{1,0:T(8,128)(2,1)} %fusion.7), channel_id=1, source_target_pairs={{0,8},{1,9},{2,10},{3,11},{4,12},{5,13},{6,14},{7,15},{8,0},{9,1},... | collective-permute-start | bytes 331784 | tf_op jit(solution)/shard_map/ppermute | solution.py:667
  364.4 13.6 %copy-start.17 = (bf16[22,768]{1,0:T(8,128)(2,1)}, bf16[22,768]{1,0:T(8,128)(2,1)S(1)}, u32[]{:S(2)}) copy-start(bf16[22,768]{1,0:T(8,128)(2,1)S(1)} %collective-permute-done.42.refs_3_) | copy-start | bytes 101380
  364.4 13.4 %collective-permute-start.38 = (bf16[144,384]{1,0:T(8,128)(2,1)}, bf16[144,384]{1,0:T(8,128)(2,1)S(1)}, u32[]{:S(2)}, u32[]{:S(2)}) collective-permute-start(bf16[144,384]{1,0:T(8,128)(2,1)} %fusion.7), channel_id=1, source_target_pairs={{0,16},{1,17},{2,18},{3,19},{4,20},{5,21},{6,22},{7,23},{8,24},{9,... | collective-permute-start | bytes 331784 | tf_op jit(solution)/shard_map/ppermute | solution.py:667
  366.5 11.3 %collective-permute-start.39 = (bf16[144,384]{1,0:T(8,128)(2,1)}, bf16[144,384]{1,0:T(8,128)(2,1)S(1)}, u32[]{:S(2)}, u32[]{:S(2)}) collective-permute-start(bf16[144,384]{1,0:T(8,128)(2,1)} %fusion.7), channel_id=1, source_target_pairs={{0,24},{1,25},{2,26},{3,27},{4,28},{5,29},{6,30},{7,31},{8,16},{9,... | collective-permute-start | bytes 331784 | tf_op jit(solution)/shard_map/ppermute | solution.py:667
  368.0 8.7 %collective-permute-start.45 = (bf16[22,768]{1,0:T(8,128)(2,1)}, bf16[22,768]{1,0:T(8,128)(2,1)}, u32[]{:S(2)}, u32[]{:S(2)}) collective-permute-start(bf16[22,768]{1,0:T(8,128)(2,1)} %group.1.refs_0_), channel_id=1, source_target_pairs={{0,24},{1,25},{2,26},{3,27},{4,28},{5,29},{6,30},{7,31},{8,16},{9,... | collective-permute-start | bytes 101384 | tf_op jit(solution)/shard_map/ppermute | solution.py:667
  370.3 6.3 %collective-permute-start.46 = (bf16[22,768]{1,0:T(8,128)(2,1)}, bf16[22,768]{1,0:T(8,128)(2,1)}, u32[]{:S(2)}, u32[]{:S(2)}) collective-permute-start(bf16[22,768]{1,0:T(8,128)(2,1)} %group.1.refs_0_), channel_id=1, source_target_pairs={{0,28},{1,29},{2,30},{3,31},{4,24},{5,25},{6,26},{7,27},{8,20},{9,... | collective-permute-start | bytes 101384 | tf_op jit(solution)/shard_map/ppermute | solution.py:667
  377.9 2.6 collective-permute-start.47
  (8 other events, 10.6 us)

commit v2 on v1

--- a/solution.py
+++ b/solution.py
@@ -358,6 +358,8 @@
                     put(src.at[pl.ds(wr+b*wr,wr)],up.at[r16(sh,wr),pl.ds(pl.multiple_of(cc*4*HC+b*HC,128),HC)])
                 put(src.at[pl.ds(5*wr,fr)],dn.at[r16(sh,fr),cd])
         return cps
+    def early():
+        return [0]+[3+6*k for k in range(2*(ns-1))]
     @pl.when(i==0)
     def _():
         cps=copies()
@@ -368,8 +370,8 @@
         aow[...]=jnp.zeros_like(aow)
         sv_ref[...]=jnp.zeros_like(sv_ref)
         sub_ref[...]=jnp.zeros_like(sub_ref)
-        for cp in cps:
-            cp.wait()
+        for k in early():
+            cps[k].wait()
     ob=vec_ref[4:5,:]
     g2=vec_ref[5:6,:]
     b2=vec_ref[6:7,:]
@@ -382,6 +384,12 @@
     cot=cot_ref[...]
     g=cot.astype(BF)
     res=mixed+db
+    @pl.when(i==0)
+    def _():
+        cps=copies()
+        for k in range(len(cps)):
+            if k not in early():
+                cps[k].wait()
     gn2=jnp.zeros((tb,D),F32)
     for j in range(FF//fc):
         cs=slice(j*fc,(j+1)*fc)
@@ -451,17 +459,14 @@
         name="mid")(idx,tok,row,att,cot,vec,*own,*mine,*other)
 
 
-def dw_kernel(idx_ref,nt_ref,d_ref,keep_ref,send_ref,sv_ref,acc,*,ns,wr):
+def dw_kernel(idx_ref,nt_ref,d_ref,keep_ref,send_ref,acc,*,ns,wr):
     i=pl.program_id(0)
     c=idx_ref[0]
     @pl.when(i==0)
     def _():
         acc[...]=jnp.zeros_like(acc)
-        sv_ref[...]=jnp.zeros_like(sv_ref)
     for w in range(3):
         acc[w]+=nn(nt_ref[...],d_ref[w])
-    sv_ref[0:8,:]+=sum8(d_ref[0].astype(F32))
-    sv_ref[8:16,:]+=sum8(d_ref[2].astype(F32))
     @pl.when(i==pl.num_programs(0)-1)
     def _():
         for ref,base,odd in ((keep_ref,1+ns,0),(send_ref,1+2*ns,1)):
@@ -484,9 +489,9 @@
         grid_spec=pltpu.PrefetchScalarGridSpec(
             num_scalar_prefetch=1,grid=(T//tb,),
             in_specs=[pl.BlockSpec((D,tb),lambda i,*_:(0,i)),pl.BlockSpec((3,tb,D),lambda i,*_:(0,i,0))],
-            out_specs=[full(ns,3*wr,HC),full(ns,3*wr,HC),full(16,D)],
+            out_specs=[full(ns,3*wr,HC),full(ns,3*wr,HC)],
             scratch_shapes=[pltpu.VMEM((3,D,D),F32)]),
-        out_shape=[S_((ns,3*wr,HC),BF)]*2+[S_((16,D),F32)],
+        out_shape=[S_((ns,3*wr,HC),BF)]*2,
         compiler_params=pltpu.CompilerParams(dimension_semantics=("arbitrary",)),
         cost_estimate=cost(6*T*D*D,T*D*8+12*D*D),
         name="dw")(idx,n1t,d)
@@ -509,6 +514,8 @@
     gt_ref[...]=gt
     sv_ref[0:8,:]+=sum8(gn*xhat)
     sv_ref[8:16,:]+=sum8(gn)
+    sv_ref[16:24,:]+=sum8(d_ref[0].astype(F32))
+    sv_ref[24:32,:]+=sum8(d_ref[2].astype(F32))
     ts_ref[0]+=sum8(gt)
 
 
@@ -519,8 +526,8 @@
     return pl.pallas_call(
         functools.partial(dx_kernel,per=per),grid=(T//tb,),
         in_specs=[blk,pl.BlockSpec((1,1,D),lambda i:(i//per,0,0)),pl.BlockSpec((3,tb,D),lambda i:(0,i,0)),blk,full(3,D,D),full(VR,D)],
-        out_specs=[blk,full(16,D),pl.BlockSpec((1,8,D),lambda i:(i//per,0,0))],
-        out_shape=[S_((T,D),F32),S_((16,D),F32),S_((T//L,8,D),F32)],
+        out_specs=[blk,full(32,D),pl.BlockSpec((1,8,D),lambda i:(i//per,0,0))],
+        out_shape=[S_((T,D),F32),S_((32,D),F32),S_((T//L,8,D),F32)],
         compiler_params=pltpu.CompilerParams(dimension_semantics=("arbitrary",)),
         cost_estimate=cost(6*T*D*D,T*D*16+6*D*D),
         name="dx")(tok,row,d,gm,w,vec)
@@ -530,17 +537,17 @@
     return jnp.sum(x,axis=0,keepdims=True)
 
 
-def sums_kernel(id_ref,sv1_ref,svq_ref,sv2_ref,sub_ref,ts_ref,out_ref):
-    src=[sv1_ref[0:8],sv1_ref[8:16],svq_ref[0:8],svq_ref[8:16]]+[sv2_ref[8*i:8*i+8] for i in range(4)]
+def sums_kernel(id_ref,sv1_ref,sv2_ref,sub_ref,ts_ref,out_ref):
+    src=[sv1_ref[8*i:8*i+8] for i in range(4)]+[sv2_ref[8*i:8*i+8] for i in range(4)]
     src+=[sub_ref[:,i*D:(i+1)*D] for i in range(FF//D)]
     rows=[rows8(x) for x in src]+[id_ref[0:1],id_ref[1:2]]+[rows8(ts_ref[i]) for i in range(ts_ref.shape[0])]
     out_ref[...]=jnp.concatenate(rows,axis=0).astype(BF)
 
 
-def sums(ids,sv1,svq,sv2,sub,ts):
+def sums(ids,sv1,sv2,sub,ts):
     vm=pl.BlockSpec(memory_space=pltpu.VMEM)
-    return pl.pallas_call(sums_kernel,in_specs=[vm]*6,out_specs=vm,
-        out_shape=S_((VR+ts.shape[0],D),BF),cost_estimate=cost(0,10**6),name="sums")(ids,sv1,svq,sv2,sub,ts)
+    return pl.pallas_call(sums_kernel,in_specs=[vm]*5,out_specs=vm,
+        out_shape=S_((VR+ts.shape[0],D),BF),cost_estimate=cost(0,10**6),name="sums")(ids,sv1,sv2,sub,ts)
 
 
 def group_kernel(idx_ref,*refs,ns,nseq):
@@ -646,6 +653,22 @@
     return pl.pallas_call(functools.partial(small_kernel,w=vecs[0].shape[0],fr=vecs[8].shape[0],nseq=time_steps.shape[0],me=idx.shape[0]-3),
         in_specs=[sm,sm]+[vm]*9,out_specs=[vm,vm],
         out_shape=[S_((VR,D),BF),S_((2,D),F32)],cost_estimate=cost(0,10**6),name="small")(idx,time_steps,*vecs)
+
+
+def fold_kernel(*refs):
+    y=refs[0][...].astype(F32)
+    for ref in refs[1:-1]:
+        y=y+ref[...].astype(F32)
+    refs[-1][...]=y.astype(BF)
+
+
+def fold(terms,n):
+    rows=terms[0].shape[1]
+    cut=2 if n==1 and rows%32==0 else 1
+    return pl.pallas_call(fold_kernel,grid=(n,cut),
+        in_specs=[pl.BlockSpec((1,rows//cut,HC),lambda i,j:(n+i,j,0))]*len(terms),
+        out_specs=pl.BlockSpec((1,rows//cut,HC),lambda i,j:(i,j,0)),
+        out_shape=S_((n,rows,HC),BF),cost_estimate=cost(0,4*n*rows*HC),name="fold")(*terms)
 
 
 class Ring:
@@ -802,7 +825,8 @@
     x=[keep_b]
     for t in reversed(range(g.nb)):
         n//=2
-        up,x=upper(x+[got],n)
+        x=x+[got]
+        up=fold(x,n)
         d,up=tie(d,up)
         got=g.step(up,t)
         i=g.nb-t
@@ -813,7 +837,7 @@
     d,xb,*rows_b=tie(d,xb,*plane_rows(g,xb))
     parts=plane_send(g,rows_b)
     d=call((d,),3)
-    keep_a,send_a,svq=dw(idx,n1t,d,S)
+    keep_a,send_a=dw(idx,n1t,d,S)
     keep_a,send_a,*parts=tie(keep_a,send_a,*parts)
     got=g.core(send_a)
     mine=plane_sum(g,xb,parts)
@@ -830,7 +854,7 @@
         up,x=upper(x+[got],n)
         ts,up=tie(ts,up)
         got=g.step(up,t)
-    pay=sums(ids,sv1,svq,sv2,sub,ts)
+    pay=sums(ids,sv1,sv2,sub,ts)
     pays=[pay]+[g.direct(pay,j) for j in range(1,S)]
     pays[-1],got=tie(pays[-1],got)
     xa=add(*[y[0] for y in x],got[0])

time: 389 us -> 388 us (level)
  other arithmetic: 25.9 us -> 15.8 us
  Pallas kernels: 276 us -> 284 us
    convert_element_type x4 -> x2, other arithmetic: 13.2 us -> 4.25 us  [add(): return y.astype(BF)]
    pallas_call x1 -> x3, Pallas kernels: 1.7 us -> 8.81 us  [the longest x2 7.11 us: fold(): pl.pallas_call(fold_kernel, grid=(n, cut), in_specs=[pl.BlockSpec((1, row...]
  transfers between devices with their start and end apart: 48 -> 48, of which waited for: 14 -> 12; matrix products, arithmetic and copies ran while one was open for 4% -> 4% of each run, Pallas kernels for 47% -> 47%
where the time goes in v2:
time: 388 us; the launch traced here: 384 us
  Pallas kernels  284 us (73%)
  starting transfers between devices  50.3 us (13%)
  waiting for transfers between devices  20.3 us (5%)
  other arithmetic  15.8 us (4%)
  local copies, waits for them, and re-layouts  11.5 us (3%)
    pallas_call x1, Pallas kernels, mid(): pl.pallas_call(functools.partial(mid_kernel, tb=tb, fc=fc, ns=ns, wr=wr,...  89.2 us
    pallas_call x4, Pallas kernels, attn_bwd(): pl.pallas_call(functools.partial(bwd_kernel, f0=f0, ns=ns), grid_spec=plt...  77.4 us
    ppermute x48, starting transfers between devices, move(): return lax.ppermute(x, ('rep', 'shard'), pairs)  50.3 us
    pallas_call x3, Pallas kernels, attn_fwd(): pl.pallas_call(functools.partial(fwd_kernel, f0=f0, ns=ns), grid_spec=plt...  42.7 us
    ppermute x48, waiting for transfers between devices, move(): return lax.ppermute(x, ('rep', 'shard'), pairs)  20.3 us
    pallas_call x1, Pallas kernels, qkv(): pl.pallas_call(functools.partial(qkv_kernel, ns=ns, wr=wr), grid_spec=plt...  18.7 us
    pallas_call x1, Pallas kernels, dx(): pl.pallas_call(functools.partial(dx_kernel, per=per), grid=(T // tb,), in...  16.4 us
    pallas_call x1, Pallas kernels, dw(): pl.pallas_call(functools.partial(dw_kernel, ns=ns, wr=wr), grid_spec=pltp...  13.6 us
  transfers between devices with their start and end apart: 48, of which 12 were waited for; matrix products, arithmetic and copies ran while one was open for 4% of the time, Pallas kernels for 47%

profile of v2, /device:TPU:0, one launch (start us, length us, event | category | flops | bytes accessed | tf_op | source)
XLA Modules:
  0.0 384.0 jit_solution(6272371478750010990)
XLA Ops:
  0.7 1.3 compare_select_fusion.6.idx_ref
  2.0 1.5 small.1
  3.5 2.0 pack_a.1
  5.5 2.9 collective-permute-start.3
  8.5 1.5 collective-permute-start.4
  10.0 2.0 collective-permute-start.1
  12.0 1.5 collective-permute-start.2
  14.2 1.1 fusion.1.fk_ref
  15.3 5.6 %collective-permute-done = bf16[14,768]{1,0:T(8,128)(2,1)S(1)} collective-permute-done((bf16[14,768]{1,0:T(8,128)(2,1)}, bf16[14,768]{1,0:T(8,128)(2,1)S(1)}, u32[]{:S(2)}, u32[]{:S(2)}) %collective-permute-start) | collective-permute-done | bytes 21536 | tf_op jit(solution)/shard_map/ppermute | solution.py:690
  20.9 1.4 collective-permute-start.5
  23.1 1.8 collective-permute-start.7
  24.9 1.4 collective-permute-start.8
  26.3 1.1 select_convert_fusion.fq_ref
  27.4 2.9 pack_b.1
  30.4 2.1 collective-permute-done.5.refs_8_
  33.9 1.5 collective-permute-start.12
  38.2 1.3 collective-permute-done.11.refs_11_
  39.5 18.7 %qkv.1 = (bf16[2048,768]{1,0:T(8,128)(2,1)}, bf16[2048,768]{1,0:T(8,128)(2,1)}, bf16[2048,768]{1,0:T(8,128)(2,1)}, bf16[768,2048]{1,0:T(8,128)(2,1)}, bf16[3,768,768]{2,1,0:T(8,128)(2,1)}) custom-call(s32[16]{0:T(128)} %compare_select_fusion.6.idx_ref, f32[2048,768]{1,0:T(8,128)} %bitcast.59, f32[2,1,768]{2,1,0:T(1,128)} %reshape.143.refs_1_.row_ref, ...), custom_call_target="tpu_custom_call" | custom-call | flops 724775744 | bytes 2103705 | tf_op jit(solution)/shard_map/qkv/pallas_call | solution.py:117
  58.2 11.3 %attn_fwd.3 = (bf16[2048,768]{1,0:T(8,128)(2,1)}, bf16[2048,768]{1,0:T(8,128)(2,1)}) custom-call(s32[26]{0:T(128)} %pad_add_fusion.s_ref, bf16[2048,768]{1,0:T(8,128)(2,1)} %get-tuple-element.153.q_ref, bf16[2048,768]{1,0:T(8,128)(2,1)} %get-tuple-element.154.k_ref, bf16[2048,768]{1,0:T(8,128)(2,1)} %get-tuple-element.155.v_ref, ...), custom_call_target="tpu_custom_call" | custom-call | flops 644245120 | bytes 550502 | tf_op jit(solution)/shard_map/attn_fwd/pallas_call | solution.py:238
  69.6 1.5 collective-permute-start.14
  71.6 20.0 %attn_fwd.4 = (bf16[2048,768]{1,0:T(8,128)(2,1)}, bf16[2048,768]{1,0:T(8,128)(2,1)}) custom-call(s32[26]{0:T(128)} %pad_add_fusion.s_ref, bf16[2048,768]{1,0:T(8,128)(2,1)} %get-tuple-element.153.q_ref, bf16[2048,768]{1,0:T(8,128)(2,1)} %get-tuple-element.154.k_ref, ...), custom_call_target="tpu_custom_call", output_to_operand_aliasing={{0}: (6, {}), {1}: (7, {})} | custom-call | flops 1288490240 | bytes 1101004 | tf_op jit(solution)/shard_map/attn_fwd/pallas_call | solution.py:238
  91.7 11.4 %attn_fwd.5 = (bf16[2048,768]{1,0:T(8,128)(2,1)}, bf16[2048,768]{1,0:T(8,128)(2,1)}) custom-call(s32[26]{0:T(128)} %pad_add_fusion.s_ref, bf16[2048,768]{1,0:T(8,128)(2,1)} %get-tuple-element.153.q_ref, bf16[2048,768]{1,0:T(8,128)(2,1)} %get-tuple-element.154.k_ref, ...), custom_call_target="tpu_custom_call", output_to_operand_aliasing={{0}: (6, {}), {1}: (7, {})} | custom-call | flops 644245120 | bytes 550502 | tf_op jit(solution)/shard_map/attn_fwd/pallas_call | solution.py:238
  103.1 89.2 %mid.1 = (f32[2048,768]{1,0:T(8,128)}, bf16[2048,768]{1,0:T(8,128)(2,1)}, bf16[2048,768]{1,0:T(8,128)(2,1)}, bf16[4,1728,384]{2,1,0:T(8,128)(2,1)}, bf16[4,1728,...) custom-call(s32[16]{0:T(128)} %compare_select_fusion.6.idx_ref, f32[2048,768]{1,0:T(8,128)} %bitcast.60, ...), custom_call_target="tpu_custom_call" | custom-call | flops 6522981376 | bytes 10223616 | tf_op jit(solution)/shard_map/mid/pallas_call | solution.py:447
  192.7 14.0 %attn_bwd.4.refs_0_ = bf16[3,2048,768]{2,1,0:T(8,128)(2,1)} custom-call(s32[26]{0:T(128)} %pad_add_fusion.s_ref, bf16[2048,768]{1,0:T(8,128)(2,1)} %get-tuple-element.153.q_ref, bf16[2048,768]{1,0:T(8,128)(2,1)} %get-tuple-element.154.k_ref, bf16[2048,768]{1,0:T(8,128)(2,1)} %get-tuple-element.155.v_ref, bf16[2048,768]{1,0:T(8,128)(2,1)} %get-tuple-element.172.fx_ref, ...), custom_call_target="tpu_custom_call" | custom-call | flops 1073741824 | bytes 524288 | tf_op jit(solution)/shard_map/attn_bwd/pallas_call | solution.py:321
  206.7 3.9 %fold.2 = bf16[2,1728,384]{2,1,0:T(8,128)(2,1)} custom-call(bf16[4,1728,384]{2,1,0:T(8,128)(2,1)} %get-tuple-element.176.refs_0_, bf16[4,1728,384]{2,1,0:T(8,128)(2,1)} %collective-permute-done.18.refs_1_), custom_call_target="tpu_custom_call" | custom-call | bytes 530841 | tf_op jit(solution)/shard_map/fold/pallas_call | solution.py:668
  211.0 30.0 %attn_bwd.5.refs_0_ = bf16[3,2048,768]{2,1,0:T(8,128)(2,1)} custom-call(s32[26]{0:T(128)} %pad_add_fusion.s_ref, bf16[2048,768]{1,0:T(8,128)(2,1)} %get-tuple-element.153.q_ref, bf16[2048,768]{1,0:T(8,128)(2,1)} %get-tuple-element.154.k_ref, bf16[2048,768]{1,0:T(8,128)(2,1)} %get-tuple-element.155.v_ref, ...), custom_call_target="tpu_custom_call", output_to_operand_aliasing={{}: (8, {})} | custom-call | flops 2684354560 | bytes 1310720 | tf_op jit(solution)/shard_map/attn_bwd/pallas_call | solution.py:321
  241.0 1.8 collective-permute-done.19.refs_2_
  242.9 1.5 copy-done
  244.4 3.2 fold.3
  247.8 19.6 %attn_bwd.6.refs_0_ = bf16[3,2048,768]{2,1,0:T(8,128)(2,1)} custom-call(s32[26]{0:T(128)} %pad_add_fusion.s_ref, bf16[2048,768]{1,0:T(8,128)(2,1)} %get-tuple-element.153.q_ref, bf16[2048,768]{1,0:T(8,128)(2,1)} %get-tuple-element.154.k_ref, bf16[2048,768]{1,0:T(8,128)(2,1)} %get-tuple-element.155.v_ref, ...), custom_call_target="tpu_custom_call", output_to_operand_aliasing={{}: (8, {})} | custom-call | flops 1610612736 | bytes 786432 | tf_op jit(solution)/shard_map/attn_bwd/pallas_call | solution.py:321
  267.4 2.8 add_convert_fusion
  270.2 1.1 copy-done.2
  271.3 1.9 collective-permute-start.21
  273.2 2.3 collective-permute-start.22
  275.8 13.8 %attn_bwd.7.d_ref = bf16[3,2048,768]{2,1,0:T(8,128)(2,1)} custom-call(s32[26]{0:T(128)} %pad_add_fusion.s_ref, bf16[2048,768]{1,0:T(8,128)(2,1)} %get-tuple-element.153.q_ref, bf16[2048,768]{1,0:T(8,128)(2,1)} %get-tuple-element.154.k_ref, bf16[2048,768]{1,0:T(8,128)(2,1)} %get-tuple-element.155.v_ref, ...), custom_call_target="tpu_custom_call", output_to_operand_aliasing={{}: (8, {})} | custom-call | flops 1073741824 | bytes 524288 | tf_op jit(solution)/shard_map/attn_bwd/pallas_call | solution.py:321
  289.6 13.6 %dw.1 = (bf16[4,576,384]{2,1,0:T(8,128)(2,1)}, bf16[4,576,384]{2,1,0:T(8,128)(2,1)}) custom-call(s32[16]{0:T(128)} %compare_select_fusion.6.idx_ref, bf16[768,2048]{1,0:T(8,128)(2,1)} %get-tuple-element.189.nt_ref, bf16[3,2048,768]{2,1,0:T(8,128)(2,1)} %attn_bwd.7.d_ref), custom_call_target="tpu_custom_call" | custom-call | flops 724775744 | bytes 1966080 | tf_op jit(solution)/shard_map/dw/pallas_call | solution.py:487
  303.4 1.9 fusion.4
  305.2 2.0 collective-permute-done.24
  307.2 2.9 add_convert_fusion.1
  310.9 1.6 collective-permute-start.25
  312.4 2.6 collective-permute-start.26
  316.4 16.4 %dx.1 = (f32[2048,768]{1,0:T(8,128)}, f32[32,768]{1,0:T(8,128)}, f32[2,8,768]{2,1,0:T(8,128)}) custom-call(f32[2048,768]{1,0:T(8,128)} %bitcast.61, f32[2,1,768]{2,1,0:T(1,128)} %reshape.143.refs_1_.row_ref, bf16[3,2048,768]{2,1,0:T(8,128)(2,1)} %attn_bwd.7.d_ref, bf16[2048,768]{1,0:T(8,128)(2,1)} %get-tuple-element.202.gm_ref, ...), custom_call_target="tpu_custom_call" | custom-call | flops 724775744 | bytes 2870476 | tf_op jit(solution)/shard_map/dx/pallas_call | solution.py:526
  332.9 1.3 add_convert_fusion.3
  334.2 1.3 collective-permute-start.32
  336.5 1.7 sums.1.refs_0_
  338.2 1.6 collective-permute-start.31
  340.8 1.6 collective-permute-start.29
  342.8 1.3 collective-permute-done.31.refs_3_
  344.7 1.5 add_convert_fusion.2
  346.8 3.8 collective-permute-start.34
  351.8 1.6 group.1.refs_0_
  353.4 2.2 collective-permute-done.34
  355.6 1.7 collective-permute-done.35
  358.5 1.3 collective-permute-start.41
  359.9 2.2 collective-permute-start.43
  362.9 1.3 collective-permute-start.37
  364.2 1.3 collective-permute-start.38
  365.5 1.9 collective-permute-start.39
  367.8 2.1 collective-permute-start.45
  369.9 1.1 collective-permute-start.46
  372.0 4.5 %unpack.2 = (f32[192,768]{1,0:T(8,128)}, f32[192,3072]{1,0:T(8,128)}, f32[768,768]{1,0:T(8,128)}) custom-call(s32[16]{0:T(128)} %compare_select_fusion.6.idx_ref, bf16[1728,384]{1,0:T(8,128)(2,1)} %bitcast.66, bf16[1728,384]{1,0:T(8,128)(2,1)} %copy-done.7), custom_call_target="tpu_custom_call" | custom-call | bytes 796262 | tf_op jit(solution)/shard_map/unpack/pallas_call | solution.py:621
  376.5 1.1 collective-permute-done.38
  377.8 2.5 table.1
  381.0 2.5 unpack.3
  (143 shorter events, 19.2 us)
Async XLA Ops:
  0.7 21.8 %copy-start.11 = (bf16[500,768]{1,0:T(8,128)(2,1)S(1)}, bf16[500,768]{1,0:T(8,128)(2,1)}, u32[]{:S(2)}) copy-start(bf16[500,768]{1,0:T(8,128)(2,1)} %param.26) | copy-start | bytes 2304004
  3.5 18.8 %copy-start.21 = (bf16[14,768]{1,0:T(8,128)(2,1)S(1)}, bf16[14,768]{1,0:T(8,128)(2,1)}, u32[]{:S(2)}) copy-start(bf16[14,768]{1,0:T(8,128)(2,1)} %get-tuple-element.144) | copy-start | bytes 64516
  5.5 19.3 %collective-permute-start.3 = (bf16[576,384]{1,0:T(8,128)(2,1)}, bf16[576,384]{1,0:T(8,128)(2,1)S(1)}, u32[]{:S(2)}, u32[]{:S(2)}) collective-permute-start(bf16[576,384]{1,0:T(8,128)(2,1)} %pack_a.1), channel_id=1, source_target_pairs={{0,1},{1,0},{2,3},{3,2},{4,5},{5,4},{6,7},{7,6},{8,9},{9,8},{10,11... | collective-permute-start | bytes 1327112 | tf_op jit(solution)/shard_map/ppermute | solution.py:690
  8.5 21.9 %collective-permute-start.4 = (bf16[576,384]{1,0:T(8,128)(2,1)}, bf16[576,384]{1,0:T(8,128)(2,1)S(1)}, u32[]{:S(2)}, u32[]{:S(2)}) collective-permute-start(bf16[576,384]{1,0:T(8,128)(2,1)} %pack_a.1), channel_id=1, source_target_pairs={{0,2},{1,3},{2,0},{3,1},{4,6},{5,7},{6,4},{7,5},{8,10},{9,11},{10,... | collective-permute-start | bytes 1327112 | tf_op jit(solution)/shard_map/ppermute | solution.py:690
  10.0 11.0 %collective-permute-start = (bf16[14,768]{1,0:T(8,128)(2,1)}, bf16[14,768]{1,0:T(8,128)(2,1)S(1)}, u32[]{:S(2)}, u32[]{:S(2)}) collective-permute-start(bf16[14,768]{1,0:T(8,128)(2,1)} %get-tuple-element.144), channel_id=1, source_target_pairs={{0,3},{1,2},{2,1},{3,0},{4,7},{5,6},{6,5},{7,4},{8,11},{9,10},{10,... | collective-permute-start | bytes 64520 | tf_op jit(solution)/shard_map/ppermute | solution.py:690
  10.0 12.4 %collective-permute-start.1 = (bf16[14,768]{1,0:T(8,128)(2,1)}, bf16[14,768]{1,0:T(8,128)(2,1)S(1)}, u32[]{:S(2)}, u32[]{:S(2)}) collective-permute-start(bf16[14,768]{1,0:T(8,128)(2,1)} %get-tuple-element.144), channel_id=1, source_target_pairs={{0,2},{1,3},{2,0},{3,1},{4,6},{5,7},{6,4},{7,5},{8,10},{9,11},{10,... | collective-permute-start | bytes 64520 | tf_op jit(solution)/shard_map/ppermute | solution.py:690
  12.0 10.4 %collective-permute-start.2 = (bf16[14,768]{1,0:T(8,128)(2,1)}, bf16[14,768]{1,0:T(8,128)(2,1)S(1)}, u32[]{:S(2)}, u32[]{:S(2)}) collective-permute-start(bf16[14,768]{1,0:T(8,128)(2,1)} %get-tuple-element.144), channel_id=1, source_target_pairs={{0,1},{1,0},{2,3},{3,2},{4,5},{5,4},{6,7},{7,6},{8,9},{9,8},{10,11... | collective-permute-start | bytes 64520 | tf_op jit(solution)/shard_map/ppermute | solution.py:690
  20.9 11.6 %collective-permute-start.5 = (bf16[576,384]{1,0:T(8,128)(2,1)}, bf16[576,384]{1,0:T(8,128)(2,1)S(1)}, u32[]{:S(2)}, u32[]{:S(2)}) collective-permute-start(bf16[576,384]{1,0:T(8,128)(2,1)} %pack_a.1), channel_id=1, source_target_pairs={{0,3},{1,2},{2,1},{3,0},{4,7},{5,6},{6,5},{7,4},{8,11},{9,10},{10,... | collective-permute-start | bytes 1327112 | tf_op jit(solution)/shard_map/ppermute | solution.py:690
  22.4 8.0 %copy-start.10 = (f32[14,768]{1,0:T(8,128)}, f32[14,768]{1,0:T(8,128)S(1)}, u32[]{:S(2)}) copy-start(f32[14,768]{1,0:T(8,128)S(1)} %convert_add_fusion.2.refs_2_.refs_4_.vec_ref) | copy-start | bytes 129028
  22.7 9.8 %collective-permute-start.6 = (bf16[2,768]{1,0:T(2,128)(2,1)S(1)}, bf16[2,768]{1,0:T(2,128)(2,1)S(1)}, u32[]{:S(2)}, u32[]{:S(2)}) collective-permute-start(bf16[2,768]{1,0:T(2,128)(2,1)S(1)} %get-tuple-element.269), channel_id=1, source_target_pairs={{0,1},{1,0},{2,3},{3,2},{4,5},{5,4},{6,7},{7,6},{8,9},{9,8},{10,11... | collective-permute-start | bytes 9224 | tf_op jit(solution)/shard_map/ppermute | solution.py:690
  23.1 9.4 %collective-permute-start.7 = (bf16[2,768]{1,0:T(2,128)(2,1)S(1)}, bf16[2,768]{1,0:T(2,128)(2,1)S(1)}, u32[]{:S(2)}, u32[]{:S(2)}) collective-permute-start(bf16[2,768]{1,0:T(2,128)(2,1)S(1)} %get-tuple-element.268), channel_id=1, source_target_pairs={{0,2},{1,3},{2,0},{3,1},{4,6},{5,7},{6,4},{7,5},{8,10},{9,11},{10,... | collective-permute-start | bytes 9224 | tf_op jit(solution)/shard_map/ppermute | solution.py:690
  24.9 11.7 %copy-start.13 = (bf16[576,384]{1,0:T(8,128)(2,1)}, bf16[576,384]{1,0:T(8,128)(2,1)S(1)}, u32[]{:S(2)}) copy-start(bf16[576,384]{1,0:T(8,128)(2,1)S(1)} %collective-permute-done.3.refs_6_) | copy-start | bytes 1327108
  24.9 7.7 %collective-permute-start.8 = (bf16[2,768]{1,0:T(2,128)(2,1)S(1)}, bf16[2,768]{1,0:T(2,128)(2,1)S(1)}, u32[]{:S(2)}, u32[]{:S(2)}) collective-permute-start(bf16[2,768]{1,0:T(2,128)(2,1)S(1)} %get-tuple-element.267), channel_id=1, source_target_pairs={{0,3},{1,2},{2,1},{3,0},{4,7},{5,6},{6,5},{7,4},{8,11},{9,10},{10,... | collective-permute-start | bytes 9224 | tf_op jit(solution)/shard_map/ppermute | solution.py:690
  27.4 8.4 %copy-start.20 = (s32[2,1024]{1,0:T(2,128)S(1)}, s32[2,1024]{1,0:T(2,128)}, u32[]{:S(2)}) copy-start(s32[2,1024]{1,0:T(2,128)} %param.24) | copy-start | bytes 24580
  27.4 9.6 %copy-start.25 = (s32[24]{0:T(128)S(1)}, s32[24]{0:T(128)}, u32[]{:S(2)}) copy-start(s32[24]{0:T(128)} %constant.141.clone) | copy-start | bytes 292
  33.9 35.7 %collective-permute-start.12 = (bf16[1728,384]{1,0:T(8,128)(2,1)}, bf16[1728,384]{1,0:T(8,128)(2,1)S(1)}, u32[]{:S(2)}, u32[]{:S(2)}) collective-permute-start(bf16[1728,384]{1,0:T(8,128)(2,1)} %pack_b.1), channel_id=1, source_target_pairs={{0,1},{1,0},{2,3},{3,2},{4,6},{5,7},{6,4},{7,5},{8,9},{9,8},{10,11... | collective-permute-start | bytes 3981320 | tf_op jit(solution)/shard_map/ppermute | solution.py:690
  35.4 34.2 %collective-permute-start.13 = (bf16[1728,384]{1,0:T(8,128)(2,1)}, bf16[1728,384]{1,0:T(8,128)(2,1)S(1)}, u32[]{:S(2)}, u32[]{:S(2)}) collective-permute-start(bf16[1728,384]{1,0:T(8,128)(2,1)} %pack_b.1), channel_id=1, source_target_pairs={{0,2},{1,3},{2,0},{3,1},{4,5},{5,4},{6,7},{7,6},{8,10},{9,11},{10,... | collective-permute-start | bytes 3981320 | tf_op jit(solution)/shard_map/ppermute | solution.py:690
  36.0 2.2 collective-permute-start.10
  36.1 3.4 collective-permute-start.11
  36.6 2.9 collective-permute-start.9
  69.6 22.0 %copy-start.8 = (bf16[1728,384]{1,0:T(8,128)(2,1)}, bf16[1728,384]{1,0:T(8,128)(2,1)S(1)}, u32[]{:S(2)}) copy-start(bf16[1728,384]{1,0:T(8,128)(2,1)S(1)} %collective-permute-done.12.refs_8_) | copy-start | bytes 3981316
  69.6 22.0 %copy-start.9 = (bf16[1728,384]{1,0:T(8,128)(2,1)}, bf16[1728,384]{1,0:T(8,128)(2,1)S(1)}, u32[]{:S(2)}) copy-start(bf16[1728,384]{1,0:T(8,128)(2,1)S(1)} %collective-permute-done.13.refs_9_) | copy-start | bytes 3981316
  69.6 22.0 %collective-permute-start.14 = (bf16[1728,384]{1,0:T(8,128)(2,1)S(1)}, bf16[1728,384]{1,0:T(8,128)(2,1)}, u32[]{:S(2)}, u32[]{:S(2)}) collective-permute-start(bf16[1728,384]{1,0:T(8,128)(2,1)S(1)} %collective-permute-done.12.refs_8_), channel_id=1, source_target_pairs={{0,2},{1,3},{2,0},{3,1},{4,5},{5,4},{6,7},{7,6},{8,10},{9,11},{10,... | collective-permute-start | bytes 3981320 | tf_op jit(solution)/shard_map/ppermute | solution.py:690
  71.1 32.0 %collective-permute-start.15 = (bf16[1728,384]{1,0:T(8,128)(2,1)S(1)}, bf16[1728,384]{1,0:T(8,128)(2,1)}, u32[]{:S(2)}, u32[]{:S(2)}) collective-permute-start(bf16[1728,384]{1,0:T(8,128)(2,1)S(1)} %collective-permute-done.12.refs_8_), channel_id=1, source_target_pairs={{0,4},{1,5},{2,6},{3,7},{4,0},{5,1},{6,2},{7,3},{8,12},{9,13},{10,... | collective-permute-start | bytes 3981320 | tf_op jit(solution)/shard_map/ppermute | solution.py:690
  71.1 32.0 %collective-permute-start.16 = (bf16[1728,384]{1,0:T(8,128)(2,1)S(1)}, bf16[1728,384]{1,0:T(8,128)(2,1)}, u32[]{:S(2)}, u32[]{:S(2)}) collective-permute-start(bf16[1728,384]{1,0:T(8,128)(2,1)S(1)} %collective-permute-done.13.refs_9_), channel_id=1, source_target_pairs={{0,4},{1,5},{2,6},{3,7},{4,0},{5,1},{6,2},{7,3},{8,12},{9,13},{10,... | collective-permute-start | bytes 3981320 | tf_op jit(solution)/shard_map/ppermute | solution.py:690
  91.7 11.5 %collective-permute-start.17 = (bf16[1728,384]{1,0:T(8,128)(2,1)}, bf16[1728,384]{1,0:T(8,128)(2,1)}, u32[]{:S(2)}, u32[]{:S(2)}) collective-permute-start(bf16[1728,384]{1,0:T(8,128)(2,1)} %collective-permute-done.14.refs_10_), channel_id=1, source_target_pairs={{0,4},{1,5},{2,6},{3,7},{4,0},{5,1},{6,2},{7,3},{8,12},{9,13},{10,... | collective-permute-start | bytes 3981320 | tf_op jit(solution)/shard_map/ppermute | solution.py:690
  192.3 14.4 %collective-permute-start.18 = (bf16[4,1728,384]{2,1,0:T(8,128)(2,1)}, bf16[4,1728,384]{2,1,0:T(8,128)(2,1)}, u32[]{:S(2)}, u32[]{:S(2)}) collective-permute-start(bf16[4,1728,384]{2,1,0:T(8,128)(2,1)} %get-tuple-element.174), channel_id=1, source_target_pairs={{0,4},{1,5},{2,6},{3,7},{4,0},{5,1},{6,2},{7,3},{8,12},{9,13},{10,... | collective-permute-start | bytes 15925256 | tf_op jit(solution)/shard_map/ppermute | solution.py:690
  210.6 32.2 %collective-permute-start.19 = (bf16[2,1728,384]{2,1,0:T(8,128)(2,1)}, bf16[2,1728,384]{2,1,0:T(8,128)(2,1)S(1)}, u32[]{:S(2)}, u32[]{:S(2)}) collective-permute-start(bf16[2,1728,384]{2,1,0:T(8,128)(2,1)} %fold.2), channel_id=1, source_target_pairs={{0,2},{1,3},{2,0},{3,1},{4,5},{5,4},{6,7},{7,6},{8,10},{9,11},{10,... | collective-permute-start | bytes 7962632 | tf_op jit(solution)/shard_map/ppermute | solution.py:690
  247.5 19.8 %collective-permute-start.20 = (bf16[1,1728,384]{2,1,0:T(8,128)(2,1)}, bf16[1,1728,384]{2,1,0:T(8,128)(2,1)}, u32[]{:S(2)}, u32[]{:S(2)}) collective-permute-start(bf16[1,1728,384]{2,1,0:T(8,128)(2,1)} %fold.3), channel_id=1, source_target_pairs={{0,1},{1,0},{2,3},{3,2},{4,6},{5,7},{6,4},{7,5},{8,9},{9,8},{10,11... | collective-permute-start | bytes 3981320 | tf_op jit(solution)/shard_map/ppermute | solution.py:690
  247.8 19.6 %copy-start.1 = (bf16[2,1728,384]{2,1,0:T(8,128)(2,1)S(1)}, bf16[2,1728,384]{2,1,0:T(8,128)(2,1)}, u32[]{:S(2)}) copy-start(bf16[2,1728,384]{2,1,0:T(8,128)(2,1)} %copy-done) | copy-start | bytes 7962628
  271.3 31.9 %collective-permute-start.21 = (bf16[432,384]{1,0:T(8,128)(2,1)S(1)}, bf16[432,384]{1,0:T(8,128)(2,1)S(1)}, u32[]{:S(2)}, u32[]{:S(2)}) collective-permute-start(bf16[432,384]{1,0:T(8,128)(2,1)S(1)} %get-tuple-element.192), channel_id=1, source_target_pairs={{0,8},{1,9},{2,10},{3,11},{4,12},{5,13},{6,14},{7,15},{8,0},{9,1},... | collective-permute-start | bytes 995336 | tf_op jit(solution)/shard_map/ppermute | solution.py:690
  273.2 30.0 %collective-permute-start.22 = (bf16[432,384]{1,0:T(8,128)(2,1)S(1)}, bf16[432,384]{1,0:T(8,128)(2,1)S(1)}, u32[]{:S(2)}, u32[]{:S(2)}) collective-permute-start(bf16[432,384]{1,0:T(8,128)(2,1)S(1)} %get-tuple-element.193), channel_id=1, source_target_pairs={{0,16},{1,17},{2,18},{3,19},{4,20},{5,21},{6,22},{7,23},{8,24},{9,... | collective-permute-start | bytes 995336 | tf_op jit(solution)/shard_map/ppermute | solution.py:690
  275.5 27.8 %collective-permute-start.23 = (bf16[432,384]{1,0:T(8,128)(2,1)S(1)}, bf16[432,384]{1,0:T(8,128)(2,1)S(1)}, u32[]{:S(2)}, u32[]{:S(2)}) collective-permute-start(bf16[432,384]{1,0:T(8,128)(2,1)S(1)} %get-tuple-element.194), channel_id=1, source_target_pairs={{0,24},{1,25},{2,26},{3,27},{4,28},{5,29},{6,30},{7,31},{8,16},{9,... | collective-permute-start | bytes 995336 | tf_op jit(solution)/shard_map/ppermute | solution.py:690
  303.3 4.0 %collective-permute-start.24 = (bf16[4,576,384]{2,1,0:T(8,128)(2,1)}, bf16[4,576,384]{2,1,0:T(8,128)(2,1)S(1)}, u32[]{:S(2)}, u32[]{:S(2)}) collective-permute-start(bf16[4,576,384]{2,1,0:T(8,128)(2,1)} %get-tuple-element.198), channel_id=1, source_target_pairs={{0,4},{1,5},{2,6},{3,7},{4,0},{5,1},{6,2},{7,3},{8,12},{9,13},{10,... | collective-permute-start | bytes 5308424 | tf_op jit(solution)/shard_map/ppermute | solution.py:690
  307.2 7.8 %copy-start.6 = (bf16[4,576,384]{2,1,0:T(8,128)(2,1)}, bf16[4,576,384]{2,1,0:T(8,128)(2,1)S(1)}, u32[]{:S(2)}) copy-start(bf16[4,576,384]{2,1,0:T(8,128)(2,1)S(1)} %collective-permute-done.24) | copy-start | bytes 5308420
  310.2 22.7 %collective-permute-start.28 = (bf16[2,576,384]{2,1,0:T(8,128)(2,1)}, bf16[2,576,384]{2,1,0:T(8,128)(2,1)}, u32[]{:S(2)}, u32[]{:S(2)}) collective-permute-start(bf16[2,576,384]{2,1,0:T(8,128)(2,1)} %add_convert_fusion.1), channel_id=1, source_target_pairs={{0,2},{1,3},{2,0},{3,1},{4,5},{5,4},{6,7},{7,6},{8,10},{9,11},{10,... | collective-permute-start | bytes 2654216 | tf_op jit(solution)/shard_map/ppermute | solution.py:690
  310.9 24.6 %collective-permute-start.25 = (bf16[432,384]{1,0:T(8,128)(2,1)}, bf16[432,384]{1,0:T(8,128)(2,1)}, u32[]{:S(2)}, u32[]{:S(2)}) collective-permute-start(bf16[432,384]{1,0:T(8,128)(2,1)} %fusion.4), channel_id=1, source_target_pairs={{0,8},{1,9},{2,10},{3,11},{4,12},{5,13},{6,14},{7,15},{8,0},{9,1},... | collective-permute-start | bytes 995336 | tf_op jit(solution)/shard_map/ppermute | solution.py:690
  312.4 27.3 %collective-permute-start.26 = (bf16[432,384]{1,0:T(8,128)(2,1)}, bf16[432,384]{1,0:T(8,128)(2,1)}, u32[]{:S(2)}, u32[]{:S(2)}) collective-permute-start(bf16[432,384]{1,0:T(8,128)(2,1)} %fusion.4), channel_id=1, source_target_pairs={{0,16},{1,17},{2,18},{3,19},{4,20},{5,21},{6,22},{7,23},{8,24},{9,... | collective-permute-start | bytes 995336 | tf_op jit(solution)/shard_map/ppermute | solution.py:690
  315.0 35.8 %collective-permute-start.27 = (bf16[432,384]{1,0:T(8,128)(2,1)}, bf16[432,384]{1,0:T(8,128)(2,1)}, u32[]{:S(2)}, u32[]{:S(2)}) collective-permute-start(bf16[432,384]{1,0:T(8,128)(2,1)} %fusion.4), channel_id=1, source_target_pairs={{0,24},{1,25},{2,26},{3,27},{4,28},{5,29},{6,30},{7,31},{8,16},{9,... | collective-permute-start | bytes 995336 | tf_op jit(solution)/shard_map/ppermute | solution.py:690
  316.4 16.4 %copy-start.5 = (bf16[4,576,384]{2,1,0:T(8,128)(2,1)S(1)}, bf16[4,576,384]{2,1,0:T(8,128)(2,1)}, u32[]{:S(2)}) copy-start(bf16[4,576,384]{2,1,0:T(8,128)(2,1)} %get-tuple-element.200) | copy-start | bytes 5308420
  334.2 10.5 %collective-permute-start.32 = (bf16[1,576,384]{2,1,0:T(8,128)(2,1)S(1)}, bf16[1,576,384]{2,1,0:T(8,128)(2,1)}, u32[]{:S(2)}, u32[]{:S(2)}) collective-permute-start(bf16[1,576,384]{2,1,0:T(8,128)(2,1)S(1)} %add_convert_fusion.3), channel_id=1, source_target_pairs={{0,1},{1,0},{2,3},{3,2},{4,6},{5,7},{6,4},{7,5},{8,9},{9,8},{10,11... | collective-permute-start | bytes 1327112 | tf_op jit(solution)/shard_map/ppermute | solution.py:690
  338.2 5.9 %collective-permute-start.31 = (bf16[16,768]{1,0:T(8,128)(2,1)}, bf16[16,768]{1,0:T(8,128)(2,1)S(1)}, u32[]{:S(2)}, u32[]{:S(2)}) collective-permute-start(bf16[16,768]{1,0:T(8,128)(2,1)} %sums.1.refs_0_), channel_id=1, source_target_pairs={{0,3},{1,2},{2,1},{3,0},{4,7},{5,6},{6,5},{7,4},{8,11},{9,10},{10,... | collective-permute-start | bytes 73736 | tf_op jit(solution)/shard_map/ppermute | solution.py:690
  340.8 5.5 %collective-permute-start.29 = (bf16[16,768]{1,0:T(8,128)(2,1)}, bf16[16,768]{1,0:T(8,128)(2,1)S(1)}, u32[]{:S(2)}, u32[]{:S(2)}) collective-permute-start(bf16[16,768]{1,0:T(8,128)(2,1)} %sums.1.refs_0_), channel_id=1, source_target_pairs={{0,1},{1,0},{2,3},{3,2},{4,5},{5,4},{6,7},{7,6},{8,9},{9,8},{10,11... | collective-permute-start | bytes 73736 | tf_op jit(solution)/shard_map/ppermute | solution.py:690
  342.4 4.0 %collective-permute-start.30 = (bf16[16,768]{1,0:T(8,128)(2,1)}, bf16[16,768]{1,0:T(8,128)(2,1)S(1)}, u32[]{:S(2)}, u32[]{:S(2)}) collective-permute-start(bf16[16,768]{1,0:T(8,128)(2,1)} %sums.1.refs_0_), channel_id=1, source_target_pairs={{0,2},{1,3},{2,0},{3,1},{4,6},{5,7},{6,4},{7,5},{8,10},{9,11},{10,... | collective-permute-start | bytes 73736 | tf_op jit(solution)/shard_map/ppermute | solution.py:690
  346.3 4.5 %copy-start.23 = (bf16[16,768]{1,0:T(8,128)(2,1)}, bf16[16,768]{1,0:T(8,128)(2,1)S(1)}, u32[]{:S(2)}) copy-start(bf16[16,768]{1,0:T(8,128)(2,1)S(1)} %collective-permute-done.29.refs_1_) | copy-start | bytes 73732
  346.4 7.0 %collective-permute-start.33 = (bf16[144,384]{1,0:T(8,128)(2,1)S(1)}, bf16[144,384]{1,0:T(8,128)(2,1)S(1)}, u32[]{:S(2)}, u32[]{:S(2)}) collective-permute-start(bf16[144,384]{1,0:T(8,128)(2,1)S(1)} %get-tuple-element.222), channel_id=1, source_target_pairs={{0,8},{1,9},{2,10},{3,11},{4,12},{5,13},{6,14},{7,15},{8,0},{9,1},... | collective-permute-start | bytes 331784 | tf_op jit(solution)/shard_map/ppermute | solution.py:690
  346.8 8.8 %collective-permute-start.34 = (bf16[144,384]{1,0:T(8,128)(2,1)S(1)}, bf16[144,384]{1,0:T(8,128)(2,1)S(1)}, u32[]{:S(2)}, u32[]{:S(2)}) collective-permute-start(bf16[144,384]{1,0:T(8,128)(2,1)S(1)} %get-tuple-element.264), channel_id=1, source_target_pairs={{0,16},{1,17},{2,18},{3,19},{4,20},{5,21},{6,22},{7,23},{8,24},{9,... | collective-permute-start | bytes 331784 | tf_op jit(solution)/shard_map/ppermute | solution.py:690
  350.6 6.7 %collective-permute-start.35 = (bf16[144,384]{1,0:T(8,128)(2,1)S(1)}, bf16[144,384]{1,0:T(8,128)(2,1)S(1)}, u32[]{:S(2)}, u32[]{:S(2)}) collective-permute-start(bf16[144,384]{1,0:T(8,128)(2,1)S(1)} %get-tuple-element.263), channel_id=1, source_target_pairs={{0,24},{1,25},{2,26},{3,27},{4,28},{5,29},{6,30},{7,31},{8,16},{9,... | collective-permute-start | bytes 331784 | tf_op jit(solution)/shard_map/ppermute | solution.py:690
  351.8 20.2 %copy-start.3 = (bf16[4,432,384]{2,1,0:T(8,128)(2,1)}, bf16[4,432,384]{2,1,0:T(8,128)(2,1)S(1)}, u32[]{:S(2)}) copy-start(bf16[4,432,384]{2,1,0:T(8,128)(2,1)S(1)} %bitcast_dynamic-update-slice_fusion) | copy-start | bytes 3981316
  357.3 12.6 %collective-permute-start.36 = (bf16[1728,384]{1,0:T(8,128)(2,1)S(1)}, bf16[1728,384]{1,0:T(8,128)(2,1)S(1)}, u32[]{:S(2)}, u32[]{:S(2)}) collective-permute-start(bf16[1728,384]{1,0:T(8,128)(2,1)S(1)} %bitcast.65), channel_id=1, source_target_pairs={{0,4},{1,5},{2,6},{3,7},{4,0},{5,1},{6,2},{7,3},{8,12},{9,13},{10,... | collective-permute-start | bytes 3981320 | tf_op jit(solution)/shard_map/ppermute | solution.py:690
  358.0 4.1 %collective-permute-start.40 = (bf16[22,768]{1,0:T(8,128)(2,1)}, bf16[22,768]{1,0:T(8,128)(2,1)S(1)}, u32[]{:S(2)}, u32[]{:S(2)}) collective-permute-start(bf16[22,768]{1,0:T(8,128)(2,1)} %group.1.refs_0_), channel_id=1, source_target_pairs={{0,4},{1,5},{2,6},{3,7},{4,0},{5,1},{6,2},{7,3},{8,12},{9,13},{10,... | collective-permute-start | bytes 101384 | tf_op jit(solution)/shard_map/ppermute | solution.py:690
  358.5 4.4 %collective-permute-start.41 = (bf16[22,768]{1,0:T(8,128)(2,1)}, bf16[22,768]{1,0:T(8,128)(2,1)S(1)}, u32[]{:S(2)}, u32[]{:S(2)}) collective-permute-start(bf16[22,768]{1,0:T(8,128)(2,1)} %group.1.refs_0_), channel_id=1, source_target_pairs={{0,8},{1,9},{2,10},{3,11},{4,12},{5,13},{6,14},{7,15},{8,0},{9,1},... | collective-permute-start | bytes 101384 | tf_op jit(solution)/shard_map/ppermute | solution.py:690
  359.8 4.4 %collective-permute-start.42 = (bf16[22,768]{1,0:T(8,128)(2,1)}, bf16[22,768]{1,0:T(8,128)(2,1)S(1)}, u32[]{:S(2)}, u32[]{:S(2)}) collective-permute-start(bf16[22,768]{1,0:T(8,128)(2,1)} %group.1.refs_0_), channel_id=1, source_target_pairs={{0,12},{1,13},{2,14},{3,15},{4,8},{5,9},{6,10},{7,11},{8,4},{9,5},... | collective-permute-start | bytes 101384 | tf_op jit(solution)/shard_map/ppermute | solution.py:690
  359.9 5.6 %collective-permute-start.43 = (bf16[22,768]{1,0:T(8,128)(2,1)}, bf16[22,768]{1,0:T(8,128)(2,1)}, u32[]{:S(2)}, u32[]{:S(2)}) collective-permute-start(bf16[22,768]{1,0:T(8,128)(2,1)} %group.1.refs_0_), channel_id=1, source_target_pairs={{0,16},{1,17},{2,18},{3,19},{4,20},{5,21},{6,22},{7,23},{8,24},{9,... | collective-permute-start | bytes 101384 | tf_op jit(solution)/shard_map/ppermute | solution.py:690
  362.1 15.7 %copy-start.16 = (bf16[22,768]{1,0:T(8,128)(2,1)}, bf16[22,768]{1,0:T(8,128)(2,1)S(1)}, u32[]{:S(2)}) copy-start(bf16[22,768]{1,0:T(8,128)(2,1)S(1)} %collective-permute-done.40.refs_1_) | copy-start | bytes 101380
  362.1 5.7 %collective-permute-start.44 = (bf16[22,768]{1,0:T(8,128)(2,1)}, bf16[22,768]{1,0:T(8,128)(2,1)S(1)}, u32[]{:S(2)}, u32[]{:S(2)}) collective-permute-start(bf16[22,768]{1,0:T(8,128)(2,1)} %group.1.refs_0_), channel_id=1, source_target_pairs={{0,20},{1,21},{2,22},{3,23},{4,16},{5,17},{6,18},{7,19},{8,28},{9,... | collective-permute-start | bytes 101384 | tf_op jit(solution)/shard_map/ppermute | solution.py:690
  362.9 14.9 %copy-start.17 = (bf16[22,768]{1,0:T(8,128)(2,1)}, bf16[22,768]{1,0:T(8,128)(2,1)S(1)}, u32[]{:S(2)}) copy-start(bf16[22,768]{1,0:T(8,128)(2,1)S(1)} %collective-permute-done.41.refs_2_) | copy-start | bytes 101380
  362.9 13.6 %collective-permute-start.37 = (bf16[144,384]{1,0:T(8,128)(2,1)}, bf16[144,384]{1,0:T(8,128)(2,1)S(1)}, u32[]{:S(2)}, u32[]{:S(2)}) collective-permute-start(bf16[144,384]{1,0:T(8,128)(2,1)} %fusion.7), channel_id=1, source_target_pairs={{0,8},{1,9},{2,10},{3,11},{4,12},{5,13},{6,14},{7,15},{8,0},{9,1},... | collective-permute-start | bytes 331784 | tf_op jit(solution)/shard_map/ppermute | solution.py:690
  364.2 13.6 %copy-start.18 = (bf16[22,768]{1,0:T(8,128)(2,1)}, bf16[22,768]{1,0:T(8,128)(2,1)S(1)}, u32[]{:S(2)}) copy-start(bf16[22,768]{1,0:T(8,128)(2,1)S(1)} %collective-permute-done.42.refs_3_) | copy-start | bytes 101380
  364.2 13.4 %collective-permute-start.38 = (bf16[144,384]{1,0:T(8,128)(2,1)}, bf16[144,384]{1,0:T(8,128)(2,1)S(1)}, u32[]{:S(2)}, u32[]{:S(2)}) collective-permute-start(bf16[144,384]{1,0:T(8,128)(2,1)} %fusion.7), channel_id=1, source_target_pairs={{0,16},{1,17},{2,18},{3,19},{4,20},{5,21},{6,22},{7,23},{8,24},{9,... | collective-permute-start | bytes 331784 | tf_op jit(solution)/shard_map/ppermute | solution.py:690
  365.5 12.1 %collective-permute-start.39 = (bf16[144,384]{1,0:T(8,128)(2,1)}, bf16[144,384]{1,0:T(8,128)(2,1)S(1)}, u32[]{:S(2)}, u32[]{:S(2)}) collective-permute-start(bf16[144,384]{1,0:T(8,128)(2,1)} %fusion.7), channel_id=1, source_target_pairs={{0,24},{1,25},{2,26},{3,27},{4,28},{5,29},{6,30},{7,31},{8,16},{9,... | collective-permute-start | bytes 331784 | tf_op jit(solution)/shard_map/ppermute | solution.py:690
  367.8 8.7 %collective-permute-start.45 = (bf16[22,768]{1,0:T(8,128)(2,1)}, bf16[22,768]{1,0:T(8,128)(2,1)}, u32[]{:S(2)}, u32[]{:S(2)}) collective-permute-start(bf16[22,768]{1,0:T(8,128)(2,1)} %group.1.refs_0_), channel_id=1, source_target_pairs={{0,24},{1,25},{2,26},{3,27},{4,28},{5,29},{6,30},{7,31},{8,16},{9,... | collective-permute-start | bytes 101384 | tf_op jit(solution)/shard_map/ppermute | solution.py:690
  369.9 6.6 %collective-permute-start.46 = (bf16[22,768]{1,0:T(8,128)(2,1)}, bf16[22,768]{1,0:T(8,128)(2,1)}, u32[]{:S(2)}, u32[]{:S(2)}) collective-permute-start(bf16[22,768]{1,0:T(8,128)(2,1)} %group.1.refs_0_), channel_id=1, source_target_pairs={{0,28},{1,29},{2,30},{3,31},{4,24},{5,25},{6,26},{7,27},{8,20},{9,... | collective-permute-start | bytes 101384 | tf_op jit(solution)/shard_map/ppermute | solution.py:690
  377.7 2.6 collective-permute-start.47
  (10 other events, 18.2 us)
